TPU v7x, 32 devices: a whole 2x2x4 slice. The times are simulated.
32 devices in a mesh: grp: 2 (over y), mom: 16 (over z, x, core).
Axes of the slice: x: 2, y: 2, z: 4, core: 2. Of those that a mesh axis runs over, the one named last changes fastest.
Arguments:
- green_function: bfloat16 [2, 4096, 512], P(None, ('grp', 'mom')), parts along dimension 1, may hold values from -0.8984375 to 0.8984375
- couplings: bfloat16 [8, 2, 512, 512], replicated, may hold values from -0.1875 to 0.1875
- phonon_modes: int32 [3, 4], replicated, may hold values from 0 to 7
- weights: float32 [3, 4], replicated, may hold values from 0.5 to 2
Outputs:
- self_energy: float32 [2, 4096, 512], P(None, ('grp', 'mom')), parts along dimension 1
There are 2 independent parts, one for each index of `grp`. A program takes and returns all parts, laid end to end along the dimension named above; an argument that names none is the same for every part. Nothing has to cross between parts.
Inputs may be any that keep to these rules, and one draw needn't show every extreme that they name: `phonon_modes`: each entry names one matrix of couplings.
All inputs are finite; a program needn't handle non-finite values.
Results may differ from a plain program's by a relative error of at most 0.0042.
Values may be sent and summed in bfloat16 or wider, within the bound.
No kernel may reach another device: no remote copies, remote signals or barrier semaphores. Data moves between devices by JAX's collectives and lax.ppermute only.
A program may use at most 64 MiB of HBM per device.

v0:
```python
import jax
import jax.numpy as jnp
import numpy as np
from jax import lax
from jax.sharding import PartitionSpec as P


def partner(block, axis, bit):
    count = lax.axis_size(axis)
    route = []
    for low in range(count):
        high = low | 1 << bit
        if high != low and high < count:
            route += [(low, high), (high, low)]
    return lax.ppermute(block, axis, route)


def passed_along(block, axis, distance):
    devices = range(lax.axis_size(axis))
    route = [((i - distance) % len(devices), i) for i in devices]
    return lax.ppermute(block, axis, route)


def stack_spectral(spectral):
    upper_half = jnp.concatenate([spectral[0], spectral[1]], axis=1)
    lower_half = jnp.concatenate([-spectral[1], spectral[0]], axis=1)
    return jnp.concatenate([upper_half, lower_half], axis=0)


def stack_coupling(coupling):
    upper_half = jnp.concatenate([coupling[0], coupling[1]], axis=1)
    lower_half = jnp.concatenate([-coupling[1], coupling[0]], axis=1)
    return jnp.concatenate([upper_half, lower_half], axis=0)


def place_pair(gathered, received, member, level):
    upper_half = member >> level & 1
    return jnp.where(
        upper_half == 1,
        jnp.concatenate([received, gathered]),
        jnp.concatenate([gathered, received]),
    )


def collect_own_rows(local_piece, levels, member):
    gathered = local_piece[None]
    for level in range(levels):
        received = partner(gathered, "mom", level)
        gathered = place_pair(gathered, received, member, level)
    return gathered


def as_slab(row_blocks):
    group_size, parts, tile_rows, slab_order = row_blocks.shape
    return row_blocks.transpose(1, 0, 2, 3).reshape(parts, group_size * tile_rows, slab_order)


def stop_term(spectral, stop_index, couplings, phonon_modes, weights, member, tile_rows):
    stacked = stack_spectral(spectral)
    mode_count = phonon_modes.shape[1]
    left_list = []
    right_list = []
    for mode_index in range(mode_count):
        coupling = lax.dynamic_index_in_dim(
            couplings, phonon_modes[stop_index, mode_index], 0, keepdims=False
        )
        coupled_rows = lax.dynamic_slice_in_dim(coupling, member * tile_rows, tile_rows, 1)
        left_list.append(jnp.concatenate([coupled_rows[0], coupled_rows[1]], axis=1))
        right_list.append(stack_coupling(coupling))
    products = jnp.dot(
        jnp.concatenate(left_list, axis=0), stacked, preferred_element_type=jnp.float32
    ).astype(jnp.bfloat16)
    total = None
    for mode_index in range(mode_count):
        product = products[mode_index * tile_rows : (mode_index + 1) * tile_rows]
        contribution = lax.dot_general(
            product,
            right_list[mode_index],
            (((1,), (1,)), ((), ())),
            preferred_element_type=jnp.float32,
        )
        weighted = weights[stop_index, mode_index] * contribution
        total = weighted if total is None else total + weighted
    return total


def body(green_function, couplings, phonon_modes, weights):
    tile_rows = green_function.shape[1]
    slab_order = green_function.shape[2]
    group_size = slab_order // tile_rows
    levels = group_size.bit_length() - 1
    member = lax.axis_index("mom") % group_size
    stop_count = phonon_modes.shape[0]
    reach = (stop_count - 1) // 2
    whole_spectral = None
    blocks = green_function.reshape(2, tile_rows, group_size, tile_rows).transpose(2, 0, 1, 3)
    partner_order = jnp.arange(group_size, dtype=jnp.int32) ^ member
    mirror_slots = jnp.take(blocks, partner_order, axis=0)
    for level in range(levels):
        chosen = [slot_index for slot_index in range(group_size) if slot_index >> level & 1]
        picked = jnp.stack([mirror_slots[slot_index] for slot_index in chosen])
        arrived = partner(picked, "mom", level)
        mirror_slots = mirror_slots.at[np.array(chosen)].set(arrived)
    mirrored = jnp.take(mirror_slots, partner_order, axis=0)
    mirror_rows = jnp.transpose(mirrored, (1, 3, 0, 2)).reshape(2, tile_rows, slab_order)
    spec_real = -(green_function[1].astype(jnp.float32) + mirror_rows[1].astype(jnp.float32))
    spec_imag = green_function[0].astype(jnp.float32) - mirror_rows[0].astype(jnp.float32)
    own_rows = jnp.stack([spec_real, spec_imag]).astype(jnp.bfloat16)
    whole_spectral = as_slab(collect_own_rows(own_rows, levels, member))
    terms = [
        stop_term(whole_spectral, stop_index, couplings, phonon_modes, weights, member, tile_rows)
        for stop_index in range(stop_count)
    ]
    accumulated = terms[reach]
    carried = terms[stop_count - 1]
    carried = passed_along(carried, "mom", group_size)
    accumulated = accumulated + carried
    carried = terms[0]
    carried = passed_along(carried, "mom", -group_size)
    accumulated = accumulated + carried
    return accumulated.reshape(tile_rows, 2, slab_order).transpose(1, 0, 2)


def solution(mesh):
    in_specs = (P(None, ("grp", "mom"), None), P(), P(), P())
    out_specs = P(None, ("grp", "mom"), None)
    return jax.shard_map(body, mesh=mesh, in_specs=in_specs, out_specs=out_specs, check_vma=False)
```

profile of v0, /device:TPU:0, one launch (start us, length us, event | category | flops | bytes accessed | tf_op | source)
XLA Modules:
  0.0 94.4 jit_solution(5716834924307445345)
XLA Ops:
  0.0 1.1 %copy.13 = bf16[2,128,512]{1,2,0:T(8,128)(2,1)S(1)} copy(bf16[2,128,512]{2,1,0:T(8,128)(2,1)} %param.10) | data formatting | bytes 524288 | tf_op args[0]
  1.2 0.2 copy.14
  1.4 0.6 gather_fusion
  2.0 0.1 broadcast_select_fusion
  2.1 0.5 collective-permute-start
  2.6 0.7 fusion.256
  25.9 0.6 scatter_fusion
  26.6 2.6 %collective-permute-start.1 = (bf16[2,2,128,128]{3,2,1,0:T(8,128)(2,1)S(1)}, bf16[2,2,128,128]{3,2,1,0:T(8,128)(2,1)S(1)}, u32[]{:S(2)}, u32[]{:S(2)}) collective-permute-start(bf16[2,2,128,128]{3,2,1,0:T(8,128)(2,1)S(1)} %stack.20), channel_id=1, source_target_pairs={{0,2},{2,0},{1,3},{3,1},{4,6},{6,4},{5,7},{7,5},{8,10},{10,8},{9,1... | collective-permute-start | bytes 393224 | tf_op jit(solution)/shard_map/ppermute | solution.py:15
  29.1 4.0 %dynamic-slice_bitcast_fusion.47 = (bf16[128,512]{1,0:T(8,128)(2,1)}, bf16[128,512]{1,0:T(8,128)(2,1)}, bf16[128,512]{1,0:T(8,128)(2,1)}, bf16[128,512]{1,0:T(8,...) fusion(bf16[8,2,512,512]{3,2,1,0:T(8,128)(2,1)} %param.11, ...), kind=kLoop, calls=%fused_computation.242 | loop fusion | bytes 6291512 | tf_op jit(solution)/shard_map/squeeze | solution.py:68
  33.2 0.1 collective-permute-done.1
  33.3 0.6 scatter_fusion.1
  33.9 0.6 gather_fusion.1
  34.5 0.1 select_bitcast_fusion
  34.7 0.1 copy.16
  34.8 0.1 copy.15
  34.9 0.1 fusion.223
  35.1 0.2 collective-permute-start.2
  35.3 4.4 %dynamic-slice_bitcast_fusion.17 = (bf16[512,512]{1,0:T(8,128)(2,1)S(1)}, bf16[512,512]{1,0:T(8,128)(2,1)S(1)}, bf16[512,512]{1,0:T(8,128)(2,1)}, bf16[512,512]{...) fusion(bf16[8,2,512,512]{3,2,1,0:T(8,128)(2,1)} %param.11, ...), kind=kLoop, calls=%fused_computation.192 | loop fusion | bytes 12582960 | tf_op jit(solution)/shard_map/squeeze | solution.py:31
  39.6 0.1 maximum_select_fusion.1
  39.7 1.7 %collective-permute-start.3 = (bf16[2,2,128,512]{3,2,1,0:T(8,128)(2,1)S(1)}, bf16[2,2,128,512]{3,2,1,0:T(8,128)(2,1)}, u32[]{:S(2)}, u32[]{:S(2)}) collective-permute-start(bf16[2,2,128,512]{3,2,1,0:T(8,128)(2,1)S(1)} %maximum_select_fusion.1), channel_id=1, source_target_pairs={{0,2},{2,0},{1,3},{3,1},{4,6},{6,4},{5,7},{7,5},{8,10},{10,8},{9,1... | collective-permute-start | bytes 1572872 | tf_op jit(solution)/shard_map/ppermute | solution.py:15
  41.4 0.7 fusion.255
  42.1 3.4 %fusion.240 = (bf16[512,512]{1,0:T(8,128)(2,1)S(1)}, bf16[512,512]{1,0:T(8,128)(2,1)S(1)}, bf16[512,512]{1,0:T(8,128)(2,1)}, bf16[512,512]{1,0:T(8,128)(2,1)}, b...) fusion(bf16[8,2,512,512]{3,2,1,0:T(8,128)(2,1)S(1)} %bitcast.15, ...), kind=kLoop, calls=%fused_computation.263 | loop fusion | flops 3145728 | bytes 18874420 | tf_op jit(solution)/shard_map/neg | solution.py:32
  45.5 8.9 %collective-permute-done.3 = bf16[2,2,128,512]{3,2,1,0:T(8,128)(2,1)} collective-permute-done((bf16[2,2,128,512]{3,2,1,0:T(8,128)(2,1)S(1)}, bf16[2,2,128,512]{3,2,1,0:T(8,128)(2,1)}, u32[]{:S(2)}, u32[]{:S(2)}) %collective-permute-start.3) | collective-permute-done | bytes 524320 | tf_op jit(solution)/shard_map/ppermute | solution.py:15
  54.4 1.4 %fusion.180 = bf16[2,4,128,512]{3,2,0,1:T(8,128)(2,1)S(1)} fusion(bf16[2,2,128,512]{3,2,1,0:T(8,128)(2,1)S(1)} %maximum_select_fusion.1, bf16[2,2,128,512]{3,2,1,0:T(8,128)(2,1)} %collective-permute-done.3, pred[]{:T(512)S(6)} %eq.8), kind=kLoop, calls=%fused_computation.143 | loop fusion | flops 1572864 | bytes 2097153 | tf_op jit(solution)/shard_map/transpose | solution.py:55
  55.9 0.1 fusion.252
  55.9 0.1 bitcast_negate_fusion
  56.0 0.7 copy-done.36
  56.8 0.1 copy-done.38
  56.9 0.1 copy-done.40
  57.1 1.2 %convolution_convert_fusion = bf16[512,1024]{1,0:T(8,128)(2,1)S(1)} fusion(bf16[128,512]{1,0:T(8,128)(2,1)S(1)} %copy-done.40, bf16[128,512]{1,0:T(8,128)(2,1)S(1)} %copy-done.36, bf16[128,512]{1,0:T(8,128)(2,1)S(1)} %copy-done.41, bf16[128,512]{1,0:T(8,128)(2,1)S(1)} %copy-done.37, bf16[128,512]{1,0:T(8,128)(2,1)S(1)} %copy-done.42, ...), kind=kOutput, calls=%fused_computation.101 | convolution fusion | flops 1091043328 | bytes 3670016 | tf_op jit(solution)/shard_map/dot_general | solution.py:70
  58.4 0.1 copy-done.19
  58.4 1.6 %fusion.114 = f32[128,1024]{1,0:T(8,128)S(1)} fusion(bf16[512,512]{1,0:T(8,128)(2,1)S(1)} %copy-done.5, bf16[512,512]{1,0:T(8,128)(2,1)S(1)} %copy-done.18, bf16[512,512]{1,0:T(8,128)(2,1)S(1)} %copy-done.19, bf16[512,1024]{1,0:T(8,128)(2,1)S(1)} %convolution_convert_fusion, f32[]{:T(128)} %bitcast.58), kind=kOutput, calls=%fused_computation.110 | convolution fusion | flops 276955136 | bytes 2359300 | tf_op jit(solution)/shard_map/dot_general | solution.py:76
  60.1 1.6 %fusion.111 = f32[128,1024]{1,0:T(8,128)S(1)} fusion(f32[128,1024]{1,0:T(8,128)S(1)} %fusion.114, bf16[512,512]{1,0:T(8,128)(2,1)S(1)} %copy-done.2, bf16[512,512]{1,0:T(8,128)(2,1)S(1)} %copy-done.16, bf16[512,512]{1,0:T(8,128)(2,1)S(1)} %copy-done.17, bf16[512,1024]{1,0:T(8,128)(2,1)S(1)} %convolution_convert_fusion, f32[]{:T(128)} %bitcast.73), kind=kOutput, calls=%fused_computation.109 | convolution fusion | flops 277086208 | bytes 2883588 | tf_op jit(solution)/shard_map/dot_general | solution.py:76
  61.7 1.5 %fusion.105 = f32[128,1024]{1,0:T(8,128)S(1)} fusion(f32[128,1024]{1,0:T(8,128)S(1)} %fusion.111, bf16[512,512]{1,0:T(8,128)(2,1)S(1)} %copy-done.1, bf16[512,512]{1,0:T(8,128)(2,1)S(1)} %copy-done.14, bf16[512,512]{1,0:T(8,128)(2,1)S(1)} %copy-done.15, bf16[512,1024]{1,0:T(8,128)(2,1)S(1)} %convolution_convert_fusion, f32[]{:T(128)} %bitcast.76), kind=kOutput, calls=%fused_computation.107 | convolution fusion | flops 277086208 | bytes 2883588 | tf_op jit(solution)/shard_map/dot_general | solution.py:76
  63.4 1.6 %fusion.99 = f32[128,1024]{1,0:T(8,128)S(1)} fusion(f32[128,1024]{1,0:T(8,128)S(1)} %fusion.105, bf16[512,512]{1,0:T(8,128)(2,1)S(1)} %get-tuple-element.53, bf16[512,512]{1,0:T(8,128)(2,1)S(1)} %copy-done.12, bf16[512,512]{1,0:T(8,128)(2,1)S(1)} %copy-done.13, bf16[512,1024]{1,0:T(8,128)(2,1)S(1)} %convolution_convert_fusion, f32[]{:T(128)} %bitcast.79), kind=kOutput, calls=%fused_computation.105 | convolution fusion | flops 277086208 | bytes 2883588 | tf_op jit(solution)/shard_map/dot_general | solution.py:76
  64.9 3.8 %collective-permute-start.5 = (f32[128,1024]{1,0:T(8,128)S(1)}, f32[128,1024]{1,0:T(8,128)S(1)}, u32[]{:S(2)}, u32[]{:S(2)}) collective-permute-start(f32[128,1024]{1,0:T(8,128)S(1)} %fusion.99), channel_id=1, source_target_pairs={{4,0},{5,1},{6,2},{7,3},{8,4},{9,5},{10,6},{11,7},{12,8},{13,9},{1... | collective-permute-start | bytes 1572872 | tf_op jit(solution)/shard_map/ppermute | solution.py:21
  68.8 1.2 %convolution_convert_fusion.1 = bf16[512,1024]{1,0:T(8,128)(2,1)S(1)} fusion(bf16[128,512]{1,0:T(8,128)(2,1)S(1)} %copy-done.32, bf16[128,512]{1,0:T(8,128)(2,1)S(1)} %copy-done.28, bf16[128,512]{1,0:T(8,128)(2,1)S(1)} %copy-done.33, bf16[128,512]{1,0:T(8,128)(2,1)S(1)} %copy-done.29, bf16[128,512]{1,0:T(8,128)(2,1)S(1)} %copy-done.34, ...), kind=kOutput, calls=%fused_computation.102 | convolution fusion | flops 1091043328 | bytes 3670016 | tf_op jit(solution)/shard_map/dot_general | solution.py:70
  70.1 1.6 %fusion.135 = f32[128,1024]{1,0:T(8,128)S(1)} fusion(bf16[512,512]{1,0:T(8,128)(2,1)S(1)} %get-tuple-element.60, bf16[512,512]{1,0:T(8,128)(2,1)S(1)} %copy-done.10, bf16[512,512]{1,0:T(8,128)(2,1)S(1)} %copy-done.11, bf16[512,1024]{1,0:T(8,128)(2,1)S(1)} %convolution_convert_fusion.1, f32[]{:T(128)} %bitcast.34), kind=kOutput, calls=%fused_computation.117 | convolution fusion | flops 276955136 | bytes 2359300 | tf_op jit(solution)/shard_map/dot_general | solution.py:76
  71.8 1.5 %fusion.132 = f32[128,1024]{1,0:T(8,128)S(1)} fusion(f32[128,1024]{1,0:T(8,128)S(1)} %fusion.135, bf16[512,512]{1,0:T(8,128)(2,1)S(1)} %get-tuple-element.59, bf16[512,512]{1,0:T(8,128)(2,1)S(1)} %copy-done.8, bf16[512,512]{1,0:T(8,128)(2,1)S(1)} %copy-done.9, bf16[512,1024]{1,0:T(8,128)(2,1)S(1)} %convolution_convert_fusion.1, f32[]{:T(128)} %bitcast.49), kind=kOutput, calls=%fused_computation.116 | convolution fusion | flops 277086208 | bytes 2883588 | tf_op jit(solution)/shard_map/dot_general | solution.py:76
  73.3 1.5 %fusion.126 = f32[128,1024]{1,0:T(8,128)S(1)} fusion(f32[128,1024]{1,0:T(8,128)S(1)} %fusion.132, bf16[512,512]{1,0:T(8,128)(2,1)S(1)} %get-tuple-element.58, bf16[512,512]{1,0:T(8,128)(2,1)S(1)} %copy-done.6, bf16[512,512]{1,0:T(8,128)(2,1)S(1)} %copy-done.7, bf16[512,1024]{1,0:T(8,128)(2,1)S(1)} %convolution_convert_fusion.1, f32[]{:T(128)} %bitcast.52), kind=kOutput, calls=%fused_computation.114 | convolution fusion | flops 277086208 | bytes 2883588 | tf_op jit(solution)/shard_map/dot_general | solution.py:76
  74.9 1.6 %fusion.120 = f32[128,1024]{1,0:T(8,128)S(1)} fusion(f32[128,1024]{1,0:T(8,128)S(1)} %fusion.126, bf16[512,512]{1,0:T(8,128)(2,1)S(1)} %get-tuple-element.57, bf16[512,512]{1,0:T(8,128)(2,1)S(1)} %copy-done.3, bf16[512,512]{1,0:T(8,128)(2,1)S(1)} %copy-done.4, bf16[512,1024]{1,0:T(8,128)(2,1)S(1)} %convolution_convert_fusion.1, f32[]{:T(128)} %bitcast.55), kind=kOutput, calls=%fused_computation.112 | convolution fusion | flops 277086208 | bytes 2883588 | tf_op jit(solution)/shard_map/dot_general | solution.py:76
  76.6 1.2 %convolution_convert_fusion.2 = bf16[512,1024]{1,0:T(8,128)(2,1)S(1)} fusion(bf16[128,512]{1,0:T(8,128)(2,1)S(1)} %copy-done.24, bf16[128,512]{1,0:T(8,128)(2,1)S(1)} %copy-done.21, bf16[128,512]{1,0:T(8,128)(2,1)S(1)} %copy-done.25, bf16[128,512]{1,0:T(8,128)(2,1)S(1)} %copy-done.22, bf16[128,512]{1,0:T(8,128)(2,1)S(1)} %copy-done.26, ...), kind=kOutput, calls=%fused_computation.103 | convolution fusion | flops 1091043328 | bytes 3670016 | tf_op jit(solution)/shard_map/dot_general | solution.py:70
  77.9 1.4 %fusion.156 = f32[128,1024]{1,0:T(8,128)S(1)} fusion(bf16[512,512]{1,0:T(8,128)(2,1)S(1)} %get-tuple-element.63, bf16[512,512]{1,0:T(8,128)(2,1)S(1)} %get-tuple-element.46, bf16[512,512]{1,0:T(8,128)(2,1)S(1)} %get-tuple-element.47, bf16[512,1024]{1,0:T(8,128)(2,1)S(1)} %convolution_convert_fusion.2, f32[]{:T(128)} %bitcast), kind=kOutput, calls=%fused_computation.124 | convolution fusion | flops 276955136 | bytes 2359300 | tf_op jit(solution)/shard_map/dot_general | solution.py:76
  79.3 1.4 %fusion.153 = f32[128,1024]{1,0:T(8,128)S(1)} fusion(f32[128,1024]{1,0:T(8,128)S(1)} %fusion.156, bf16[512,512]{1,0:T(8,128)(2,1)S(1)} %get-tuple-element.62, bf16[512,512]{1,0:T(8,128)(2,1)S(1)} %get-tuple-element.44, bf16[512,512]{1,0:T(8,128)(2,1)S(1)} %get-tuple-element.45, bf16[512,1024]{1,0:T(8,128)(2,1)S(1)} %convolution_convert_fusion.2, f32[]{:T(128)} %bitcast.25), kind=kOutput, calls=%fused_computation.123 | convolution fusion | flops 277086208 | bytes 2883588 | tf_op jit(solution)/shard_map/dot_general | solution.py:76
  80.7 1.4 %fusion.147 = f32[128,1024]{1,0:T(8,128)S(1)} fusion(f32[128,1024]{1,0:T(8,128)S(1)} %fusion.153, bf16[512,512]{1,0:T(8,128)(2,1)S(1)} %get-tuple-element.61, bf16[512,512]{1,0:T(8,128)(2,1)S(1)} %get-tuple-element.42, bf16[512,512]{1,0:T(8,128)(2,1)S(1)} %get-tuple-element.43, bf16[512,1024]{1,0:T(8,128)(2,1)S(1)} %convolution_convert_fusion.2, f32[]{:T(128)} %bitcast.28), kind=kOutput, calls=%fused_computation.121 | convolution fusion | flops 277086208 | bytes 2883588 | tf_op jit(solution)/shard_map/dot_general | solution.py:76
  82.1 10.0 %collective-permute-done.4 = f32[128,1024]{1,0:T(8,128)S(1)} collective-permute-done((f32[128,1024]{1,0:T(8,128)S(1)}, f32[128,1024]{1,0:T(8,128)S(1)}, u32[]{:S(2)}, u32[]{:S(2)}) %collective-permute-start.4) | collective-permute-done | bytes 524320 | tf_op jit(solution)/shard_map/ppermute | solution.py:21
  92.2 1.5 %fusion.162 = f32[128,1024]{1,0:T(8,128)S(1)} fusion(f32[128,1024]{1,0:T(8,128)S(1)} %collective-permute-done.5, f32[128,1024]{1,0:T(8,128)S(1)} %collective-permute-done.4, f32[128,1024]{1,0:T(8,128)S(1)} %fusion.147, bf16[512,512]{1,0:T(8,128)(2,1)S(1)} %get-tuple-element.52, bf16[512,512]{1,0:T(8,128)(2,1)S(1)} %get-tuple-element.6, ...), kind=kOutput, calls=%fused_computation.126 | convolution fusion | flops 277348352 | bytes 3932164 | tf_op jit(solution)/shard_map/dot_general | solution.py:76
  93.6 0.8 copy.20
  (109 shorter events, 0.6 us)
Async XLA Ops:
  0.0 25.9 %copy-start.47 = (s32[2]{0:T(128)S(1)}, s32[2]{0:T(128)}, u32[]{:S(2)}) copy-start(s32[2]{0:T(128)} %constant.315) | copy-start | bytes 28
  0.0 2.6 %copy-start.44 = (s32[3,4]{1,0:T(4,128)S(1)}, s32[3,4]{1,0:T(4,128)}, u32[]{:S(2)}) copy-start(s32[3,4]{1,0:T(4,128)} %param.12) | copy-start | bytes 148
  2.1 23.8 %collective-permute-start = (bf16[2,2,128,128]{3,2,1,0:T(8,128)(2,1)S(1)}, bf16[2,2,128,128]{3,2,1,0:T(8,128)(2,1)S(1)}, u32[]{:S(2)}, u32[]{:S(2)}) collective-permute-start(bf16[2,2,128,128]{3,2,1,0:T(8,128)(2,1)S(1)} %pad_maximum_fusion.1), channel_id=1, source_target_pairs={{0,1},{1,0},{2,3},{3,2},{4,5},{5,4},{6,7},{7,6},{8,9},{9,8},{10,11... | collective-permute-start | bytes 393224 | tf_op jit(solution)/shard_map/ppermute | solution.py:15
  26.6 6.7 %copy-start.46 = (s32[2]{0:T(128)S(1)}, s32[2]{0:T(128)}, u32[]{:S(2)}) copy-start(s32[2]{0:T(128)} %constant.316) | copy-start | bytes 28
  26.6 6.7 %collective-permute-start.1 = (bf16[2,2,128,128]{3,2,1,0:T(8,128)(2,1)S(1)}, bf16[2,2,128,128]{3,2,1,0:T(8,128)(2,1)S(1)}, u32[]{:S(2)}, u32[]{:S(2)}) collective-permute-start(bf16[2,2,128,128]{3,2,1,0:T(8,128)(2,1)S(1)} %stack.20), channel_id=1, source_target_pairs={{0,2},{2,0},{1,3},{3,1},{4,6},{6,4},{5,7},{7,5},{8,10},{10,8},{9,1... | collective-permute-start | bytes 393224 | tf_op jit(solution)/shard_map/ppermute | solution.py:15
  33.2 1.7 %copy-start = (bf16[2,128,512]{2,1,0:T(8,128)(2,1)S(1)}, bf16[2,128,512]{2,1,0:T(8,128)(2,1)}, u32[]{:S(2)}) copy-start(bf16[2,128,512]{2,1,0:T(8,128)(2,1)} %param.10) | copy-start | bytes 786436
  34.9 7.2 %slice-start = ((s8[8388608]{0:T(1024)(128)(4,1)}), s8[4194304]{0:T(1024)(128)(4,1)S(1)}, s32[]{:S(2)}) async-start(s8[8388608]{0:T(1024)(128)(4,1)} %bitcast.158), calls=%async_computation | async-start | bytes 8388608
  35.0 6.4 %copy-start.45 = (f32[3,4]{1,0:T(4,128)S(1)}, f32[3,4]{1,0:T(4,128)}, u32[]{:S(2)}) copy-start(f32[3,4]{1,0:T(4,128)} %param.13) | copy-start | bytes 148
  35.1 7.0 %slice-start.1 = ((s8[8388608]{0:T(1024)(128)(4,1)}), s8[4194304]{0:T(1024)(128)(4,1)S(1)}, s32[]{:S(2)}) async-start(s8[8388608]{0:T(1024)(128)(4,1)} %bitcast.158), calls=%async_computation.1 | async-start | bytes 8388608
  35.1 4.6 %collective-permute-start.2 = (bf16[1,2,128,512]{3,2,1,0:T(8,128)(2,1)S(1)}, bf16[1,2,128,512]{3,2,1,0:T(8,128)(2,1)S(1)}, u32[]{:S(2)}, u32[]{:S(2)}) collective-permute-start(bf16[1,2,128,512]{3,2,1,0:T(8,128)(2,1)S(1)} %pad_maximum_fusion), channel_id=1, source_target_pairs={{0,1},{1,0},{2,3},{3,2},{4,5},{5,4},{6,7},{7,6},{8,9},{9,8},{10,11... | collective-permute-start | bytes 786440 | tf_op jit(solution)/shard_map/ppermute | solution.py:15
  39.7 14.7 %collective-permute-start.3 = (bf16[2,2,128,512]{3,2,1,0:T(8,128)(2,1)S(1)}, bf16[2,2,128,512]{3,2,1,0:T(8,128)(2,1)}, u32[]{:S(2)}, u32[]{:S(2)}) collective-permute-start(bf16[2,2,128,512]{3,2,1,0:T(8,128)(2,1)S(1)} %maximum_select_fusion.1), channel_id=1, source_target_pairs={{0,2},{2,0},{1,3},{3,1},{4,6},{6,4},{5,7},{7,5},{8,10},{10,8},{9,1... | collective-permute-start | bytes 1572872 | tf_op jit(solution)/shard_map/ppermute | solution.py:15
  57.1 1.3 %copy-start.5 = (bf16[512,512]{1,0:T(8,128)(2,1)S(1)}, bf16[512,512]{1,0:T(8,128)(2,1)}, u32[]{:S(2)}) copy-start(bf16[512,512]{1,0:T(8,128)(2,1)} %get-tuple-element.56) | copy-start | bytes 1572868
  57.1 1.3 %copy-start.18 = (bf16[512,512]{1,0:T(8,128)(2,1)S(1)}, bf16[512,512]{1,0:T(8,128)(2,1)}, u32[]{:S(2)}) copy-start(bf16[512,512]{1,0:T(8,128)(2,1)} %get-tuple-element.32) | copy-start | bytes 1572868
  57.1 1.4 %copy-start.19 = (bf16[512,512]{1,0:T(8,128)(2,1)S(1)}, bf16[512,512]{1,0:T(8,128)(2,1)}, u32[]{:S(2)}) copy-start(bf16[512,512]{1,0:T(8,128)(2,1)} %get-tuple-element.33) | copy-start | bytes 1572868
  58.4 1.6 %copy-start.2 = (bf16[512,512]{1,0:T(8,128)(2,1)S(1)}, bf16[512,512]{1,0:T(8,128)(2,1)}, u32[]{:S(2)}) copy-start(bf16[512,512]{1,0:T(8,128)(2,1)} %get-tuple-element.55) | copy-start | bytes 1572868
  58.4 1.6 %copy-start.16 = (bf16[512,512]{1,0:T(8,128)(2,1)S(1)}, bf16[512,512]{1,0:T(8,128)(2,1)}, u32[]{:S(2)}) copy-start(bf16[512,512]{1,0:T(8,128)(2,1)} %get-tuple-element.30) | copy-start | bytes 1572868
  58.4 1.6 %copy-start.17 = (bf16[512,512]{1,0:T(8,128)(2,1)S(1)}, bf16[512,512]{1,0:T(8,128)(2,1)}, u32[]{:S(2)}) copy-start(bf16[512,512]{1,0:T(8,128)(2,1)} %get-tuple-element.31) | copy-start | bytes 1572868
  60.1 1.6 %copy-start.1 = (bf16[512,512]{1,0:T(8,128)(2,1)S(1)}, bf16[512,512]{1,0:T(8,128)(2,1)}, u32[]{:S(2)}) copy-start(bf16[512,512]{1,0:T(8,128)(2,1)} %get-tuple-element.54) | copy-start | bytes 1572868
  60.1 1.6 %copy-start.14 = (bf16[512,512]{1,0:T(8,128)(2,1)S(1)}, bf16[512,512]{1,0:T(8,128)(2,1)}, u32[]{:S(2)}) copy-start(bf16[512,512]{1,0:T(8,128)(2,1)} %get-tuple-element.50) | copy-start | bytes 1572868
  60.1 1.6 %copy-start.15 = (bf16[512,512]{1,0:T(8,128)(2,1)S(1)}, bf16[512,512]{1,0:T(8,128)(2,1)}, u32[]{:S(2)}) copy-start(bf16[512,512]{1,0:T(8,128)(2,1)} %get-tuple-element.51) | copy-start | bytes 1572868
  61.7 1.6 %copy-start.12 = (bf16[512,512]{1,0:T(8,128)(2,1)S(1)}, bf16[512,512]{1,0:T(8,128)(2,1)}, u32[]{:S(2)}) copy-start(bf16[512,512]{1,0:T(8,128)(2,1)} %get-tuple-element.48) | copy-start | bytes 1572868
  61.7 1.6 %copy-start.13 = (bf16[512,512]{1,0:T(8,128)(2,1)S(1)}, bf16[512,512]{1,0:T(8,128)(2,1)}, u32[]{:S(2)}) copy-start(bf16[512,512]{1,0:T(8,128)(2,1)} %get-tuple-element.49) | copy-start | bytes 1572868
  63.3 5.5 %copy-start.28 = (bf16[128,512]{1,0:T(8,128)(2,1)S(1)}, bf16[128,512]{1,0:T(8,128)(2,1)}, u32[]{:S(2)}) copy-start(bf16[128,512]{1,0:T(8,128)(2,1)} %get-tuple-element.69) | copy-start | bytes 393220
  63.3 5.5 %copy-start.29 = (bf16[128,512]{1,0:T(8,128)(2,1)S(1)}, bf16[128,512]{1,0:T(8,128)(2,1)}, u32[]{:S(2)}) copy-start(bf16[128,512]{1,0:T(8,128)(2,1)} %get-tuple-element.70) | copy-start | bytes 393220
  63.3 5.5 %copy-start.30 = (bf16[128,512]{1,0:T(8,128)(2,1)S(1)}, bf16[128,512]{1,0:T(8,128)(2,1)}, u32[]{:S(2)}) copy-start(bf16[128,512]{1,0:T(8,128)(2,1)} %get-tuple-element.71) | copy-start | bytes 393220
  63.3 5.4 %copy-start.31 = (bf16[128,512]{1,0:T(8,128)(2,1)S(1)}, bf16[128,512]{1,0:T(8,128)(2,1)}, u32[]{:S(2)}) copy-start(bf16[128,512]{1,0:T(8,128)(2,1)} %get-tuple-element.72) | copy-start | bytes 393220
  63.3 5.4 %copy-start.32 = (bf16[128,512]{1,0:T(8,128)(2,1)S(1)}, bf16[128,512]{1,0:T(8,128)(2,1)}, u32[]{:S(2)}) copy-start(bf16[128,512]{1,0:T(8,128)(2,1)} %get-tuple-element.80) | copy-start | bytes 393220
  63.3 5.4 %copy-start.33 = (bf16[128,512]{1,0:T(8,128)(2,1)S(1)}, bf16[128,512]{1,0:T(8,128)(2,1)}, u32[]{:S(2)}) copy-start(bf16[128,512]{1,0:T(8,128)(2,1)} %get-tuple-element.81) | copy-start | bytes 393220
  63.4 5.4 %copy-start.34 = (bf16[128,512]{1,0:T(8,128)(2,1)S(1)}, bf16[128,512]{1,0:T(8,128)(2,1)}, u32[]{:S(2)}) copy-start(bf16[128,512]{1,0:T(8,128)(2,1)} %get-tuple-element.82) | copy-start | bytes 393220
  63.4 5.4 %copy-start.35 = (bf16[128,512]{1,0:T(8,128)(2,1)S(1)}, bf16[128,512]{1,0:T(8,128)(2,1)}, u32[]{:S(2)}) copy-start(bf16[128,512]{1,0:T(8,128)(2,1)} %get-tuple-element.83) | copy-start | bytes 393220
  64.9 17.2 %collective-permute-start.5 = (f32[128,1024]{1,0:T(8,128)S(1)}, f32[128,1024]{1,0:T(8,128)S(1)}, u32[]{:S(2)}, u32[]{:S(2)}) collective-permute-start(f32[128,1024]{1,0:T(8,128)S(1)} %fusion.99), channel_id=1, source_target_pairs={{4,0},{5,1},{6,2},{7,3},{8,4},{9,5},{10,6},{11,7},{12,8},{13,9},{1... | collective-permute-start | bytes 1572872 | tf_op jit(solution)/shard_map/ppermute | solution.py:21
  68.8 1.3 %copy-start.10 = (bf16[512,512]{1,0:T(8,128)(2,1)S(1)}, bf16[512,512]{1,0:T(8,128)(2,1)}, u32[]{:S(2)}) copy-start(bf16[512,512]{1,0:T(8,128)(2,1)} %get-tuple-element.40) | copy-start | bytes 1572868
  68.8 1.3 %copy-start.11 = (bf16[512,512]{1,0:T(8,128)(2,1)S(1)}, bf16[512,512]{1,0:T(8,128)(2,1)}, u32[]{:S(2)}) copy-start(bf16[512,512]{1,0:T(8,128)(2,1)} %get-tuple-element.41) | copy-start | bytes 1572868
  70.1 1.6 %copy-start.8 = (bf16[512,512]{1,0:T(8,128)(2,1)S(1)}, bf16[512,512]{1,0:T(8,128)(2,1)}, u32[]{:S(2)}) copy-start(bf16[512,512]{1,0:T(8,128)(2,1)} %get-tuple-element.38) | copy-start | bytes 1572868
  70.1 1.6 %copy-start.9 = (bf16[512,512]{1,0:T(8,128)(2,1)S(1)}, bf16[512,512]{1,0:T(8,128)(2,1)}, u32[]{:S(2)}) copy-start(bf16[512,512]{1,0:T(8,128)(2,1)} %get-tuple-element.39) | copy-start | bytes 1572868
  71.7 1.5 %copy-start.6 = (bf16[512,512]{1,0:T(8,128)(2,1)S(1)}, bf16[512,512]{1,0:T(8,128)(2,1)}, u32[]{:S(2)}) copy-start(bf16[512,512]{1,0:T(8,128)(2,1)} %get-tuple-element.36) | copy-start | bytes 1572868
  71.7 1.5 %copy-start.7 = (bf16[512,512]{1,0:T(8,128)(2,1)S(1)}, bf16[512,512]{1,0:T(8,128)(2,1)}, u32[]{:S(2)}) copy-start(bf16[512,512]{1,0:T(8,128)(2,1)} %get-tuple-element.37) | copy-start | bytes 1572868
  73.3 1.5 %copy-start.3 = (bf16[512,512]{1,0:T(8,128)(2,1)S(1)}, bf16[512,512]{1,0:T(8,128)(2,1)}, u32[]{:S(2)}) copy-start(bf16[512,512]{1,0:T(8,128)(2,1)} %get-tuple-element.34) | copy-start | bytes 1572868
  73.3 1.5 %copy-start.4 = (bf16[512,512]{1,0:T(8,128)(2,1)S(1)}, bf16[512,512]{1,0:T(8,128)(2,1)}, u32[]{:S(2)}) copy-start(bf16[512,512]{1,0:T(8,128)(2,1)} %get-tuple-element.35) | copy-start | bytes 1572868
  74.8 1.7 %copy-start.20 = (bf16[128,512]{1,0:T(8,128)(2,1)S(1)}, bf16[128,512]{1,0:T(8,128)(2,1)}, u32[]{:S(2)}) copy-start(bf16[128,512]{1,0:T(8,128)(2,1)} %get-tuple-element.64) | copy-start | bytes 393220
  74.8 1.7 %copy-start.21 = (bf16[128,512]{1,0:T(8,128)(2,1)S(1)}, bf16[128,512]{1,0:T(8,128)(2,1)}, u32[]{:S(2)}) copy-start(bf16[128,512]{1,0:T(8,128)(2,1)} %get-tuple-element.73) | copy-start | bytes 393220
  74.8 1.7 %copy-start.22 = (bf16[128,512]{1,0:T(8,128)(2,1)S(1)}, bf16[128,512]{1,0:T(8,128)(2,1)}, u32[]{:S(2)}) copy-start(bf16[128,512]{1,0:T(8,128)(2,1)} %get-tuple-element.74) | copy-start | bytes 393220
  74.8 1.7 %copy-start.23 = (bf16[128,512]{1,0:T(8,128)(2,1)S(1)}, bf16[128,512]{1,0:T(8,128)(2,1)}, u32[]{:S(2)}) copy-start(bf16[128,512]{1,0:T(8,128)(2,1)} %get-tuple-element.75) | copy-start | bytes 393220
  74.9 1.7 %copy-start.24 = (bf16[128,512]{1,0:T(8,128)(2,1)S(1)}, bf16[128,512]{1,0:T(8,128)(2,1)}, u32[]{:S(2)}) copy-start(bf16[128,512]{1,0:T(8,128)(2,1)} %get-tuple-element.84) | copy-start | bytes 393220
  74.9 1.7 %copy-start.25 = (bf16[128,512]{1,0:T(8,128)(2,1)S(1)}, bf16[128,512]{1,0:T(8,128)(2,1)}, u32[]{:S(2)}) copy-start(bf16[128,512]{1,0:T(8,128)(2,1)} %get-tuple-element.85) | copy-start | bytes 393220
  74.9 1.7 %copy-start.26 = (bf16[128,512]{1,0:T(8,128)(2,1)S(1)}, bf16[128,512]{1,0:T(8,128)(2,1)}, u32[]{:S(2)}) copy-start(bf16[128,512]{1,0:T(8,128)(2,1)} %get-tuple-element.86) | copy-start | bytes 393220
  74.9 1.7 %copy-start.27 = (bf16[128,512]{1,0:T(8,128)(2,1)S(1)}, bf16[128,512]{1,0:T(8,128)(2,1)}, u32[]{:S(2)}) copy-start(bf16[128,512]{1,0:T(8,128)(2,1)} %get-tuple-element.87) | copy-start | bytes 393220
  76.5 15.7 %collective-permute-start.4 = (f32[128,1024]{1,0:T(8,128)S(1)}, f32[128,1024]{1,0:T(8,128)S(1)}, u32[]{:S(2)}, u32[]{:S(2)}) collective-permute-start(f32[128,1024]{1,0:T(8,128)S(1)} %fusion.120), channel_id=1, source_target_pairs={{12,0},{13,1},{14,2},{15,3},{0,4},{1,5},{2,6},{3,7},{4,8},{5,9},{6... | collective-permute-start | bytes 1572872 | tf_op jit(solution)/shard_map/ppermute | solution.py:21
  (8 other events, 8.7 us)
where the time goes:
time: 95.1 us; the launch traced here: 94.4 us
  between operations  23.5 us (25%)
  matrix products  21.8 us (23%)
  waiting for transfers between devices  19.1 us (20%)
  local copies, waits for them, and re-layouts  16 us (17%)
  starting transfers between devices  8.86 us (9%)
  other arithmetic  5.21 us (5%)
    dot_general x12, matrix products, stop_term(): lax.dot_general(product, right_list[mode_index], (((1,), (1,)), ((), ()))...  18.1 us
    ppermute x2, waiting for transfers between devices, passed_along(): return lax.ppermute(block, axis, route)  10 us
    ppermute x4, waiting for transfers between devices, partner(): return lax.ppermute(block, axis, route)  9.03 us
    ppermute x4, starting transfers between devices, partner(): return lax.ppermute(block, axis, route)  4.97 us
    squeeze x1, local copies, waits for them, and re-layouts, stack_coupling(): upper_half = jnp.concatenate([coupling[0], coupling[1]], axis=1)  4.36 us
    squeeze x1, local copies, waits for them, and re-layouts, stop_term(): coupled_rows[0]  4.03 us
    ppermute x2, starting transfers between devices, passed_along(): return lax.ppermute(block, axis, route)  3.88 us
    dot_general x3, matrix products, stop_term(): jnp.dot(jnp.concatenate(left_list, axis=0), stacked, preferred_element_ty...  3.74 us
  transfers between devices with their start and end apart: 6, of which 3 were waited for; matrix products, arithmetic and copies ran while one was open for 28% of the time, Pallas kernels for 0%

commit v1 on v0

v1 whole, which is shorter than its diff:
```python
import functools

import jax
import jax.numpy as jnp
from jax import lax
from jax.experimental import pallas as pl
from jax.experimental.pallas import tpu as pltpu
from jax.sharding import PartitionSpec as P

F32 = jnp.float32
BF16 = jnp.bfloat16


def partner(block, axis, bit):
    count = lax.axis_size(axis)
    route = [(i, i ^ 1 << bit) for i in range(count)]
    return lax.ppermute(block, axis, route)


def passed_along(block, axis, distance):
    count = lax.axis_size(axis)
    route = [((i - distance) % count, i) for i in range(count)]
    return lax.ppermute(block, axis, route)


def gathered(block, axis, levels):
    have = {0: block}
    for level in reversed(range(levels)):
        for offset in list(have):
            have[offset | 1 << level] = partner(have[offset], axis, level)
    return [have[offset] for offset in sorted(have)]


def adjoint_rows_kernel(modes, member, *refs):
    *rows, out = refs
    for mode, row in enumerate(rows):
        tile = row.shape[2]
        out[0, mode, :, :tile] = row[0, 0].T
        out[0, mode, :, tile:] = row[0, 1].T


def adjoint_rows(couplings, phonon_modes, member, tile):
    stops, modes = phonon_modes.shape
    slab = couplings.shape[3]

    def spec(mode):
        return pl.BlockSpec((1, 2, tile, slab), lambda s, table, me: (table[s, mode], 0, me[0], 0))

    return pl.pallas_call(
        adjoint_rows_kernel,
        grid_spec=pltpu.PrefetchScalarGridSpec(
            num_scalar_prefetch=2,
            grid=(stops,),
            in_specs=[spec(mode) for mode in range(modes)],
            out_specs=pl.BlockSpec((1, modes, slab, 2 * tile), lambda s, table, me: (s, 0, 0, 0)),
        ),
        out_shape=jax.ShapeDtypeStruct((stops, modes, slab, 2 * tile), BF16),
        compiler_params=pltpu.CompilerParams(vmem_limit_bytes=16 << 20),
        cost_estimate=pl.CostEstimate(flops=0, transcendentals=0, bytes_accessed=6 << 20),
        name="adjoint_rows",
    )(phonon_modes, member, *[couplings] * modes)


def fill_spectral(me, blocks, green, spectral):
    tile, slab = blocks[0].shape[1:]
    for offset, block in enumerate(blocks):
        row = pl.multiple_of((me ^ offset) * tile, tile)
        green[:, pl.ds(row, tile), :] = block[...]
    spots = [slice(i * tile, (i + 1) * tile) for i in range(slab // tile)]
    for i, rows in enumerate(spots):
        for j, cols in enumerate(spots):
            here = slice(slab + j * tile, slab + (j + 1) * tile)
            real = -(green[1, rows, cols].astype(F32) + green[1, cols, rows].T.astype(F32))
            imag = green[0, rows, cols].astype(F32) - green[0, cols, rows].T.astype(F32)
            spectral[rows, cols] = real.astype(BF16)
            spectral[rows, here] = imag.astype(BF16)


def add_modes(stop, modes, weights, spectral, adjoint, couplings, held, sems, total):
    count = adjoint.shape[0]
    half = adjoint.shape[2] // 2
    for mode in range(count):
        turned = adjoint[mode]
        real, imag = turned[:, :half], turned[:, half:]
        right = jnp.concatenate(
            [jnp.concatenate([real, -imag], axis=1), turned_swap(imag, real)], axis=0
        )
        product = jnp.dot(spectral[...], right, preferred_element_type=F32).astype(BF16)
        real, imag = product[:, :half], product[:, half:]
        right = jnp.concatenate([product, turned_swap(-imag, real)], axis=0)
        coupling_copy(stop, mode, modes, couplings, held, sems).wait()
        left = jnp.concatenate([held[mode, 0], held[mode, 1]], axis=1)
        term = weights[stop, mode] * jnp.dot(left, right, preferred_element_type=F32)
        if total is None:
            total = term
        else:
            total = total + term
    return total


def turned_swap(first, second):
    return jnp.concatenate([first, second], axis=1)


def coupling_copy(stop, mode, modes, couplings, held, sems):
    return pltpu.make_async_copy(couplings.at[modes[stop, mode]], held.at[mode], sems.at[mode])


def start_copies(stop, count, modes, couplings, held, sems):
    for mode in range(count):
        coupling_copy(stop, mode, modes, couplings, held, sems).start()


def later_kernel(stop, count, modes, weights, member, *refs):
    blocks = refs[:count]
    adjoint, couplings, term, spectral, green, held, sems = refs[count:]
    start_copies(stop, adjoint.shape[0], modes, couplings, held, sems)
    fill_spectral(member[0], blocks, green, spectral)
    total = add_modes(stop, modes, weights, spectral, adjoint, couplings, held, sems, None)
    term[...] = total.astype(BF16)


def own_kernel(stop, modes, weights, spectral, adjoint, couplings, term, held, sems):
    start_copies(stop, adjoint.shape[0], modes, couplings, held, sems)
    term[...] = add_modes(stop, modes, weights, spectral, adjoint, couplings, held, sems, None)


def last_kernel(stop, count, modes, weights, member, *refs):
    blocks = refs[:count]
    adjoint, couplings, own, arrived, out, spectral, green, held, sems = refs[count:]
    start_copies(stop, adjoint.shape[0], modes, couplings, held, sems)
    fill_spectral(member[0], blocks, green, spectral)
    total = own[...] + arrived[...].astype(F32)
    total = add_modes(stop, modes, weights, spectral, adjoint, couplings, held, sems, total)
    tile = out.shape[1]
    out[0] = total[:, :tile].T
    out[1] = -total[:, tile:].T


def body(green_function, couplings, phonon_modes, weights):
    tile, slab = green_function.shape[1:]
    group = slab // tile
    levels = group.bit_length() - 1
    modes = phonon_modes.shape[1]
    member = (lax.axis_index("mom") % group).astype(jnp.int32).reshape(1)

    smem = pl.BlockSpec(memory_space=pltpu.SMEM)
    vmem = pl.BlockSpec(memory_space=pltpu.VMEM)
    anywhere = pl.BlockSpec(memory_space=pl.ANY)
    columns = (slab, 2 * tile)
    held = [pltpu.VMEM((modes, 2, slab, slab), BF16), pltpu.SemaphoreType.DMA((modes,))]
    green = pltpu.VMEM((2, slab, slab), BF16)
    params = pltpu.CompilerParams(vmem_limit_bytes=24 << 20)
    cost = pl.CostEstimate(
        flops=modes * 2 * 2 * slab * 2 * slab * 2 * tile,
        transcendentals=0,
        bytes_accessed=(modes + 2) * 2 * slab * slab * 2,
    )

    incoming = passed_along(green_function, "mom", group)
    own_blocks = gathered(green_function, "mom", levels)
    adjoint = adjoint_rows(couplings, phonon_modes, member, tile)
    next_blocks = gathered(incoming, "mom", levels)

    leaving, spectral = pl.pallas_call(
        functools.partial(later_kernel, 0, group),
        in_specs=[smem] * 3 + [vmem] * (group + 1) + [anywhere],
        out_specs=[vmem, vmem],
        out_shape=[
            jax.ShapeDtypeStruct(columns, BF16),
            jax.ShapeDtypeStruct((slab, 2 * slab), BF16),
        ],
        scratch_shapes=[green, *held],
        compiler_params=params,
        cost_estimate=cost,
        name="later_stop",
    )(phonon_modes, weights, member, *own_blocks, adjoint[0], couplings)
    arrived = passed_along(leaving, "mom", -group)

    own = pl.pallas_call(
        functools.partial(own_kernel, 1),
        in_specs=[smem] * 2 + [vmem] * 2 + [anywhere],
        out_specs=vmem,
        out_shape=jax.ShapeDtypeStruct(columns, F32),
        scratch_shapes=held,
        compiler_params=params,
        cost_estimate=cost,
        name="own_stop",
    )(phonon_modes, weights, spectral, adjoint[1], couplings)

    return pl.pallas_call(
        functools.partial(last_kernel, 2, group),
        in_specs=[smem] * 3 + [vmem] * (group + 1) + [anywhere] + [vmem] * 2,
        out_specs=vmem,
        out_shape=jax.ShapeDtypeStruct((2, tile, slab), F32),
        scratch_shapes=[pltpu.VMEM((slab, 2 * slab), BF16), green, *held],
        compiler_params=params,
        cost_estimate=cost,
        name="last_stop",
    )(phonon_modes, weights, member, *next_blocks, adjoint[2], couplings, own, arrived)


def solution(mesh):
    in_specs = (P(None, ("grp", "mom"), None), P(), P(), P())
    out_specs = P(None, ("grp", "mom"), None)
    return jax.shard_map(body, mesh=mesh, in_specs=in_specs, out_specs=out_specs, check_vma=False)
```

time: 95.1 us -> 32.8 us (0.34)
  between operations: 23.5 us -> 0.13 us
  matrix products: 21.8 us -> 0 us
  Pallas kernels: 0 us -> 16.6 us
  waiting for transfers between devices: 19.1 us -> 3.97 us
  local copies, waits for them, and re-layouts: 16 us -> 4.29 us
  other arithmetic: 5.21 us -> 0 us
  starting transfers between devices: 8.86 us -> 7.66 us
    dot_general x15 -> x0, matrix products: 21.8 us -> none  [the longest x12 18.1 us: stop_term(): lax.dot_general(product, right_list[mode_index], (((1,), (1,)), ((), ()))...]
    pallas_call x0 -> x4, Pallas kernels: none -> 16.6 us  [the longest x1 5.56 us: body(): pl.pallas_call(functools.partial(last_kernel, 2, group), in_specs=[smem]...]
    ppermute x4 -> x6, waiting for transfers between devices: 9.03 us -> 0.02 us  [partner(): return lax.ppermute(block, axis, route)]
    squeeze x2 -> x1, local copies, waits for them, and re-layouts: 8.39 us -> 0.2 us  [body(): adjoint[1]]
    ppermute x2, waiting for transfers between devices: 10 us -> 3.95 us  [passed_along(): return lax.ppermute(block, axis, route)]
    neg x2 -> x0, other arithmetic: 3.45 us -> none  [the longest x1 3.38 us: stack_coupling(): lower_half = jnp.concatenate([-coupling[1], coupling[0]], axis=1)]
    unnamed x101 -> x12, local copies, waits for them, and re-layouts: 2.46 us -> 4.09 us
    slice x5 -> x0, local copies, waits for them, and re-layouts: 1.47 us -> none  [the longest x1 0.69 us: stop_term(): weighted = weights[stop_index, mode_index] * contribution]
  transfers between devices with their start and end apart: 6 -> 8, of which waited for: 3 -> 2; matrix products, arithmetic and copies ran while one was open for 28% -> 1% of each run, Pallas kernels for 0% -> 34%
where the time goes in v1:
time: 32.8 us; the launch traced here: 32.7 us
  Pallas kernels  16.6 us (51%)
  starting transfers between devices  7.66 us (23%)
  local copies, waits for them, and re-layouts  4.29 us (13%)
  waiting for transfers between devices  3.97 us (12%)
    pallas_call x1, Pallas kernels, body(): pl.pallas_call(functools.partial(last_kernel, 2, group), in_specs=[smem]...  5.56 us
    pallas_call x1, Pallas kernels, body(): pl.pallas_call(functools.partial(later_kernel, 0, group), in_specs=[smem]...  4.66 us
    pallas_call x1, Pallas kernels, body(): pl.pallas_call(functools.partial(own_kernel, 1), in_specs=[smem] * 2 + [v...  4.49 us
    ppermute x6, starting transfers between devices, partner(): return lax.ppermute(block, axis, route)  4.32 us
    unnamed x12, local copies, waits for them, and re-layouts  4.09 us
    ppermute x2, waiting for transfers between devices, passed_along(): return lax.ppermute(block, axis, route)  3.95 us
    ppermute x2, starting transfers between devices, passed_along(): return lax.ppermute(block, axis, route)  3.34 us
    pallas_call x1, Pallas kernels, adjoint_rows(): pl.pallas_call(adjoint_rows_kernel, grid_spec=pltpu.PrefetchScalarGridSpe...  1.91 us
  transfers between devices with their start and end apart: 8, of which 2 were waited for; matrix products, arithmetic and copies ran while one was open for 1% of the time, Pallas kernels for 34%

profile of v1, /device:TPU:0, one launch (start us, length us, event | category | flops | bytes accessed | tf_op | source)
XLA Modules:
  0.0 32.7 jit_solution(7607332103531362505)
XLA Ops:
  0.0 2.9 %collective-permute-start.5 = (bf16[2,128,512]{2,1,0:T(8,128)(2,1)}, bf16[2,128,512]{2,1,0:T(8,128)(2,1)S(1)}, u32[]{:S(2)}, u32[]{:S(2)}) collective-permute-start(bf16[2,128,512]{2,1,0:T(8,128)(2,1)} %refs_0_.3), channel_id=1, source_target_pairs={{0,2},{1,3},{2,0},{3,1},{4,6},{5,7},{6,4},{7,5},{8,10},{9,11},{10,... | collective-permute-start | bytes 786440 | tf_op jit(solution)/shard_map/ppermute | solution.py:17
  2.9 1.6 %collective-permute-start = (bf16[2,128,512]{2,1,0:T(8,128)(2,1)}, bf16[2,128,512]{2,1,0:T(8,128)(2,1)S(1)}, u32[]{:S(2)}, u32[]{:S(2)}) collective-permute-start(bf16[2,128,512]{2,1,0:T(8,128)(2,1)} %refs_0_.3), channel_id=1, source_target_pairs={{12,0},{13,1},{14,2},{15,3},{0,4},{1,5},{2,6},{3,7},{4,8},{5,9},{6... | collective-permute-start | bytes 786440 | tf_op jit(solution)/shard_map/ppermute | solution.py:23
  4.5 0.0 collective-permute-start.4
  4.5 0.0 copy-start
  4.5 3.4 %copy-done = bf16[8,2,512,512]{3,2,1,0:T(8,128)(2,1)S(1)} copy-done((bf16[8,2,512,512]{3,2,1,0:T(8,128)(2,1)S(1)}, bf16[8,2,512,512]{3,2,1,0:T(8,128)(2,1)}, u32[]{:S(2)}) %copy-start) | copy-done | bytes 8388632
  7.9 0.0 copy-start.3
  7.9 0.7 %copy-done.3 = s32[3,4]{1,0:T(4,128)S(1)} copy-done((s32[3,4]{1,0:T(4,128)S(1)}, s32[3,4]{1,0:T(4,128)}, u32[]{:S(2)}) %copy-start.3) | copy-done | bytes 72
  8.6 0.0 copy-start.1
  8.6 1.9 %adjoint_rows.1 = bf16[3,4,512,256]{3,2,1,0:T(8,128)(2,1)S(1)} custom-call(s32[3,4]{1,0:T(4,128)S(1)} %copy-done.3, s32[1]{0:T(128)} %bitcast.member, bf16[8,2,512,512]{3,2,1,0:T(8,128)(2,1)S(1)} %copy-done, bf16[8,2,512,512]{3,2,1,0:T(8,128)(2,1)S(1)} %copy-done, bf16[8,2,512,512]{3,2,1,0:T(8,128)(2,1)S(1)} %copy-done, bf16[8,2,512,512]{3,2,1,0:T(8,128)(2,1)S(1)} %copy-done), custom_call_target="tpu_custom_call" | custom-call | bytes 6291456 | tf_op jit(solution)/shard_map/adjoint_rows/pallas_call | solution.py:49
  10.5 0.0 copy-start.2
  10.5 0.0 copy-start.4
  10.5 0.0 copy-start.5
  10.5 0.0 collective-permute-done.5.refs_2_
  10.6 0.6 %collective-permute-start.6 = (bf16[2,128,512]{2,1,0:T(8,128)(2,1)S(1)}, bf16[2,128,512]{2,1,0:T(8,128)(2,1)S(1)}, u32[]{:S(2)}, u32[]{:S(2)}) collective-permute-start(bf16[2,128,512]{2,1,0:T(8,128)(2,1)S(1)} %collective-permute-done.5.refs_2_), channel_id=1, source_target_pairs={{0,1},{1,0},{2,3},{3,2},{4,5},{5,4},{6,7},{7,6},{8,9},{9,8},{10,11... | collective-permute-start | bytes 786440 | tf_op jit(solution)/shard_map/ppermute | solution.py:17
  11.1 1.7 %collective-permute-done.refs_0_ = bf16[2,128,512]{2,1,0:T(8,128)(2,1)S(1)} collective-permute-done((bf16[2,128,512]{2,1,0:T(8,128)(2,1)}, bf16[2,128,512]{2,1,0:T(8,128)(2,1)S(1)}, u32[]{:S(2)}, u32[]{:S(2)}) %collective-permute-start) | collective-permute-done | bytes 262176 | tf_op jit(solution)/shard_map/ppermute | solution.py:23
  12.8 0.5 %collective-permute-start.2 = (bf16[2,128,512]{2,1,0:T(8,128)(2,1)S(1)}, bf16[2,128,512]{2,1,0:T(8,128)(2,1)S(1)}, u32[]{:S(2)}, u32[]{:S(2)}) collective-permute-start(bf16[2,128,512]{2,1,0:T(8,128)(2,1)S(1)} %collective-permute-done.refs_0_), channel_id=1, source_target_pairs={{0,2},{1,3},{2,0},{3,1},{4,6},{5,7},{6,4},{7,5},{8,10},{9,11},{10,... | collective-permute-start | bytes 786440 | tf_op jit(solution)/shard_map/ppermute | solution.py:17
  13.3 0.2 slice_bitcast_fusion
  13.5 0.1 collective-permute-start.1
  13.6 0.0 collective-permute-done.4.refs_1_
  13.6 0.0 collective-permute-done.6.refs_3_
  13.6 0.0 copy-done.1
  13.7 0.0 copy-done.2
  13.7 0.0 copy-done.4
  13.7 0.0 copy-done.5
  13.7 4.7 %later_stop.1 = (bf16[512,256]{1,0:T(8,128)(2,1)S(1)}, bf16[512,1024]{1,0:T(8,128)(2,1)S(1)}) custom-call(s32[3,4]{1,0:T(4,128)S(1)} %copy-done.4, f32[3,4]{1,0:T(4,128)S(1)} %copy-done.5, s32[1]{0:T(128)} %bitcast.member, bf16[2,128,512]{2,1,0:T(8,128)(2,1)S(1)} %copy-done.2, bf16[2,128,512]{2,1,0:T(8,128)(2,1)S(1)} %collective-permute-done.4.refs_1_, ...), custom_call_target="tpu_custom_call" | custom-call | flops 2147483648 | bytes 6291456 | tf_op jit(solution)/shard_map/later_stop/pallas_call | solution.py:165
  18.4 1.8 %collective-permute-start.7 = (bf16[512,256]{1,0:T(8,128)(2,1)S(1)}, bf16[512,256]{1,0:T(8,128)(2,1)S(1)}, u32[]{:S(2)}, u32[]{:S(2)}) collective-permute-start(bf16[512,256]{1,0:T(8,128)(2,1)S(1)} %get-tuple-element.8), channel_id=1, source_target_pairs={{4,0},{5,1},{6,2},{7,3},{8,4},{9,5},{10,6},{11,7},{12,8},{13,9},{1... | collective-permute-start | bytes 786440 | tf_op jit(solution)/shard_map/ppermute | solution.py:23
  20.1 0.0 collective-permute-done.2.refs_2_
  20.1 0.2 collective-permute-start.3
  20.3 4.5 %own_stop.1.refs_6_ = f32[512,256]{1,0:T(8,128)S(1)} custom-call(s32[3,4]{1,0:T(4,128)S(1)} %copy-done.4, f32[3,4]{1,0:T(4,128)S(1)} %copy-done.5, bf16[512,1024]{1,0:T(8,128)(2,1)S(1)} %get-tuple-element.7.spectral, bf16[4,512,256]{2,1,0:T(8,128)(2,1)S(1)} %get-tuple-element.9.adjoint, bf16[8,2,512,512]{3,2,1,0:T(8,128)(2,1)S(1)} %copy-done.1), custom_call_target="tpu_custom_call" | custom-call | flops 2147483648 | bytes 6291456 | tf_op jit(solution)/shard_map/own_stop/pallas_call | solution.py:180
  24.8 0.0 collective-permute-done.1.refs_1_
  24.8 2.3 %collective-permute-done.7.refs_7_ = bf16[512,256]{1,0:T(8,128)(2,1)S(1)} collective-permute-done((bf16[512,256]{1,0:T(8,128)(2,1)S(1)}, bf16[512,256]{1,0:T(8,128)(2,1)S(1)}, u32[]{:S(2)}, u32[]{:S(2)}) %collective-permute-start.7) | collective-permute-done | bytes 262176 | tf_op jit(solution)/shard_map/ppermute | solution.py:23
  27.1 0.0 collective-permute-done.3.refs_3_
  27.1 5.6 %last_stop.1 = f32[2,128,512]{2,1,0:T(8,128)} custom-call(s32[3,4]{1,0:T(4,128)S(1)} %copy-done.4, f32[3,4]{1,0:T(4,128)S(1)} %copy-done.5, s32[1]{0:T(128)} %bitcast.member, bf16[2,128,512]{2,1,0:T(8,128)(2,1)S(1)} %collective-permute-done.refs_0_, bf16[2,128,512]{2,1,0:T(8,128)(2,1)S(1)} %collective-permute-done.1.refs_1_, ...), custom_call_target="tpu_custom_call" | custom-call | flops 2147483648 | bytes 6291456 | tf_op jit(solution)/shard_map/last_stop/pallas_call | solution.py:191
Async XLA Ops:
  0.0 10.5 %collective-permute-start.5 = (bf16[2,128,512]{2,1,0:T(8,128)(2,1)}, bf16[2,128,512]{2,1,0:T(8,128)(2,1)S(1)}, u32[]{:S(2)}, u32[]{:S(2)}) collective-permute-start(bf16[2,128,512]{2,1,0:T(8,128)(2,1)} %refs_0_.3), channel_id=1, source_target_pairs={{0,2},{1,3},{2,0},{3,1},{4,6},{5,7},{6,4},{7,5},{8,10},{9,11},{10,... | collective-permute-start | bytes 786440 | tf_op jit(solution)/shard_map/ppermute | solution.py:17
  2.9 9.9 %collective-permute-start = (bf16[2,128,512]{2,1,0:T(8,128)(2,1)}, bf16[2,128,512]{2,1,0:T(8,128)(2,1)S(1)}, u32[]{:S(2)}, u32[]{:S(2)}) collective-permute-start(bf16[2,128,512]{2,1,0:T(8,128)(2,1)} %refs_0_.3), channel_id=1, source_target_pairs={{12,0},{13,1},{14,2},{15,3},{0,4},{1,5},{2,6},{3,7},{4,8},{5,9},{6... | collective-permute-start | bytes 786440 | tf_op jit(solution)/shard_map/ppermute | solution.py:23
  4.5 9.1 %collective-permute-start.4 = (bf16[2,128,512]{2,1,0:T(8,128)(2,1)}, bf16[2,128,512]{2,1,0:T(8,128)(2,1)S(1)}, u32[]{:S(2)}, u32[]{:S(2)}) collective-permute-start(bf16[2,128,512]{2,1,0:T(8,128)(2,1)} %refs_0_.3), channel_id=1, source_target_pairs={{0,1},{1,0},{2,3},{3,2},{4,5},{5,4},{6,7},{7,6},{8,9},{9,8},{10,11... | collective-permute-start | bytes 786440 | tf_op jit(solution)/shard_map/ppermute | solution.py:17
  4.5 3.4 %copy-start = (bf16[8,2,512,512]{3,2,1,0:T(8,128)(2,1)S(1)}, bf16[8,2,512,512]{3,2,1,0:T(8,128)(2,1)}, u32[]{:S(2)}) copy-start(bf16[8,2,512,512]{3,2,1,0:T(8,128)(2,1)} %refs_5_.3) | copy-start | bytes 25165828
  7.9 0.7 %copy-start.3 = (s32[3,4]{1,0:T(4,128)S(1)}, s32[3,4]{1,0:T(4,128)}, u32[]{:S(2)}) copy-start(s32[3,4]{1,0:T(4,128)} %modes.7) | copy-start | bytes 148
  8.6 5.1 %copy-start.1 = (bf16[8,2,512,512]{3,2,1,0:T(8,128)(2,1)S(1)}, bf16[8,2,512,512]{3,2,1,0:T(8,128)(2,1)}, u32[]{:S(2)}) copy-start(bf16[8,2,512,512]{3,2,1,0:T(8,128)(2,1)} %refs_5_.3) | copy-start | bytes 25165828
  10.5 3.2 %copy-start.2 = (bf16[2,128,512]{2,1,0:T(8,128)(2,1)S(1)}, bf16[2,128,512]{2,1,0:T(8,128)(2,1)}, u32[]{:S(2)}) copy-start(bf16[2,128,512]{2,1,0:T(8,128)(2,1)} %refs_0_.3) | copy-start | bytes 786436
  10.5 3.2 %copy-start.4 = (s32[3,4]{1,0:T(4,128)S(1)}, s32[3,4]{1,0:T(4,128)}, u32[]{:S(2)}) copy-start(s32[3,4]{1,0:T(4,128)} %modes.7) | copy-start | bytes 148
  10.5 3.2 %copy-start.5 = (f32[3,4]{1,0:T(4,128)S(1)}, f32[3,4]{1,0:T(4,128)}, u32[]{:S(2)}) copy-start(f32[3,4]{1,0:T(4,128)} %weights.5) | copy-start | bytes 148
  10.6 3.1 %collective-permute-start.6 = (bf16[2,128,512]{2,1,0:T(8,128)(2,1)S(1)}, bf16[2,128,512]{2,1,0:T(8,128)(2,1)S(1)}, u32[]{:S(2)}, u32[]{:S(2)}) collective-permute-start(bf16[2,128,512]{2,1,0:T(8,128)(2,1)S(1)} %collective-permute-done.5.refs_2_), channel_id=1, source_target_pairs={{0,1},{1,0},{2,3},{3,2},{4,5},{5,4},{6,7},{7,6},{8,9},{9,8},{10,11... | collective-permute-start | bytes 786440 | tf_op jit(solution)/shard_map/ppermute | solution.py:17
  12.8 7.3 %collective-permute-start.2 = (bf16[2,128,512]{2,1,0:T(8,128)(2,1)S(1)}, bf16[2,128,512]{2,1,0:T(8,128)(2,1)S(1)}, u32[]{:S(2)}, u32[]{:S(2)}) collective-permute-start(bf16[2,128,512]{2,1,0:T(8,128)(2,1)S(1)} %collective-permute-done.refs_0_), channel_id=1, source_target_pairs={{0,2},{1,3},{2,0},{3,1},{4,6},{5,7},{6,4},{7,5},{8,10},{9,11},{10,... | collective-permute-start | bytes 786440 | tf_op jit(solution)/shard_map/ppermute | solution.py:17
  13.5 11.3 %collective-permute-start.1 = (bf16[2,128,512]{2,1,0:T(8,128)(2,1)S(1)}, bf16[2,128,512]{2,1,0:T(8,128)(2,1)S(1)}, u32[]{:S(2)}, u32[]{:S(2)}) collective-permute-start(bf16[2,128,512]{2,1,0:T(8,128)(2,1)S(1)} %collective-permute-done.refs_0_), channel_id=1, source_target_pairs={{0,1},{1,0},{2,3},{3,2},{4,5},{5,4},{6,7},{7,6},{8,9},{9,8},{10,11... | collective-permute-start | bytes 786440 | tf_op jit(solution)/shard_map/ppermute | solution.py:17
  18.4 8.7 %collective-permute-start.7 = (bf16[512,256]{1,0:T(8,128)(2,1)S(1)}, bf16[512,256]{1,0:T(8,128)(2,1)S(1)}, u32[]{:S(2)}, u32[]{:S(2)}) collective-permute-start(bf16[512,256]{1,0:T(8,128)(2,1)S(1)} %get-tuple-element.8), channel_id=1, source_target_pairs={{4,0},{5,1},{6,2},{7,3},{8,4},{9,5},{10,6},{11,7},{12,8},{13,9},{1... | collective-permute-start | bytes 786440 | tf_op jit(solution)/shard_map/ppermute | solution.py:23
  20.1 7.0 %collective-permute-start.3 = (bf16[2,128,512]{2,1,0:T(8,128)(2,1)S(1)}, bf16[2,128,512]{2,1,0:T(8,128)(2,1)S(1)}, u32[]{:S(2)}, u32[]{:S(2)}) collective-permute-start(bf16[2,128,512]{2,1,0:T(8,128)(2,1)S(1)} %collective-permute-done.2.refs_2_), channel_id=1, source_target_pairs={{0,1},{1,0},{2,3},{3,2},{4,5},{5,4},{6,7},{7,6},{8,9},{9,8},{10,11... | collective-permute-start | bytes 786440 | tf_op jit(solution)/shard_map/ppermute | solution.py:17

commit v2 on v0

v2 whole, which is shorter than its diff:
```python
import jax
import jax.numpy as jnp
from jax import lax
from jax.experimental import pallas as pl
from jax.experimental.pallas import tpu as pltpu
from jax.sharding import PartitionSpec as P

F32 = jnp.float32
BF16 = jnp.bfloat16
VMEM = pl.BlockSpec(memory_space=pltpu.VMEM)
HBM = pl.BlockSpec(memory_space=pltpu.HBM)


def partner(block, axis, bit):
    count = lax.axis_size(axis)
    return lax.ppermute(block, axis, [(i, i ^ 1 << bit) for i in range(count)])


def passed_along(block, axis, distance):
    count = lax.axis_size(axis)
    return lax.ppermute(block, axis, [((i - distance) % count, i) for i in range(count)])


def gathered(block, axis, levels, before):
    have = {0: block}
    for level in reversed(range(levels)):
        for offset in list(have):
            moving = have[offset] if offset == 0 else after(have[offset], before)
            have[offset | 1 << level] = partner(moving, axis, level)
    return [have[offset] for offset in sorted(have)]


def after(value, before):
    return lax.optimization_barrier((value, before))[0]


def beside(first, second):
    return jnp.concatenate([first, second], axis=1)


def own_row(offset, group, tile):
    member = lax.axis_index("mom") % group
    return pl.multiple_of((member ^ offset) * tile, tile)


def prepare_kernel(listed, couplings, *refs):
    *outs, modes, listed_sem, sems = refs
    listing = pltpu.make_async_copy(listed, modes, listed_sem)
    listing.start()
    listing.wait()
    picked, turned = outs[::2], outs[1::2]
    stops, count = modes.shape
    slab = couplings.shape[3]
    tile = turned[0].shape[2] // 2
    copies = [
        [
            pltpu.make_async_copy(couplings.at[modes[stop, mode]], picked[stop].at[mode], sems.at[stop, mode])
            for mode in range(count)
        ]
        for stop in range(stops)
    ]
    for row in copies:
        for copy in row:
            copy.start()
    rows = pl.ds(own_row(0, slab // tile, tile), tile)
    for stop in range(stops):
        for mode in range(count):
            copies[stop][mode].wait()
            turned[stop][mode, :, :tile] = picked[stop][mode, 0, rows, :].T
            turned[stop][mode, :, tile:] = picked[stop][mode, 1, rows, :].T


def fill_spectral(blocks, spectral):
    tile, slab = blocks[0].shape[1:]
    starts = [own_row(offset, len(blocks), tile) for offset in range(len(blocks))]
    spots = [pl.ds(start, tile) for start in starts]
    imag_spots = [pl.ds(slab + start, tile) for start in starts]
    for i, block in enumerate(blocks):
        for j, other in enumerate(blocks):
            real = -(block[1, :, spots[j]].astype(F32) + other[1, :, spots[i]].T.astype(F32))
            imag = block[0, :, spots[j]].astype(F32) - other[0, :, spots[i]].T.astype(F32)
            spectral[spots[i], spots[j]] = real.astype(BF16)
            spectral[spots[i], imag_spots[j]] = imag.astype(BF16)


def stop_term(stop, weights, spectral, turned, picked, start):
    count, slab, width = turned.shape
    tile = width // 2
    rights = []
    for mode in range(count):
        real, imag = turned[mode, :, :tile], turned[mode, :, tile:]
        rights.append(jnp.concatenate([beside(real, -imag), beside(imag, real)], axis=0))
    products = jnp.dot(
        spectral[...], jnp.concatenate(rights, axis=1), preferred_element_type=F32
    ).astype(BF16)
    total = start
    for mode in range(count):
        product = products[:, mode * width : (mode + 1) * width]
        real, imag = product[:, :tile], product[:, tile:]
        right = jnp.concatenate([product, beside(-imag, real)], axis=0)
        left = beside(picked[mode, 0], picked[mode, 1])
        term = weights[stop : stop + 1, mode : mode + 1] * jnp.dot(
            left, right, preferred_element_type=F32
        )
        total = term if total is None else total + term
    return total


def body(green_function, couplings, phonon_modes, weights):
    tile, slab = green_function.shape[1:]
    group = slab // tile
    levels = group.bit_length() - 1
    stops, modes = phonon_modes.shape
    width = 2 * tile

    def kernel(name, function, args, outs, specs=None, scratch=(), limit=12, flops=0):
        return pl.pallas_call(
            function,
            in_specs=specs or [VMEM] * len(args),
            out_specs=[VMEM] * len(outs),
            out_shape=[jax.ShapeDtypeStruct(*out) for out in outs],
            scratch_shapes=list(scratch),
            compiler_params=pltpu.CompilerParams(vmem_limit_bytes=limit << 20),
            cost_estimate=pl.CostEstimate(flops=flops, transcendentals=0, bytes_accessed=4096),
            name=name,
        )(*args)

    incoming = passed_along(green_function, "mom", group)
    prepared = kernel(
        "prepare",
        prepare_kernel,
        [phonon_modes, couplings],
        [((modes, 2, slab, slab), BF16), ((modes, slab, width), BF16)] * stops,
        specs=[HBM, HBM],
        scratch=[
            pltpu.SMEM((stops, modes), jnp.int32),
            pltpu.SemaphoreType.DMA,
            pltpu.SemaphoreType.DMA((stops, modes)),
        ],
        limit=38,
    )
    picked, turned = prepared[::2], prepared[1::2]
    own_blocks = gathered(green_function, "mom", levels, turned[0])

    def later(*refs):
        *blocks, weights, turned, picked, leaving, spectral = refs
        fill_spectral(blocks, spectral)
        leaving[...] = stop_term(0, weights, spectral, turned, picked, None).astype(BF16)

    leaving, spectral = kernel(
        "later_stop",
        later,
        [*own_blocks, weights, turned[0], picked[0]],
        [((slab, width), BF16), ((slab, 2 * slab), BF16)],
        flops=2147483648,
    )
    arrived = passed_along(leaving, "mom", -group)

    def own(spectral, weights, turned, picked, out):
        out[...] = stop_term(1, weights, spectral, turned, picked, None)

    (total,) = kernel(
        "own_stop", own, [spectral, weights, turned[1], picked[1]], [((slab, width), F32)], flops=2147483648
    )

    def earlier(*refs):
        *blocks, weights, turned, picked, before, out, spectral = refs
        fill_spectral(blocks, spectral)
        out[...] = stop_term(2, weights, spectral, turned, picked, before[...])

    next_blocks = gathered(incoming, "mom", levels, leaving)
    (total,) = kernel(
        "earlier_stop",
        earlier,
        [*next_blocks, weights, turned[2], picked[2], total],
        [((slab, width), F32)],
        scratch=[pltpu.VMEM((slab, 2 * slab), BF16)],
        flops=2147483648,
    )

    def finish(total, arrived, out):
        whole = total[...] + arrived[...].astype(F32)
        out[0] = whole[:, :tile].T
        out[1] = -whole[:, tile:].T

    (rows,) = kernel("finish", finish, [total, arrived], [((2, tile, slab), F32)])
    return rows


def solution(mesh):
    in_specs = (P(None, ("grp", "mom"), None), P(), P(), P())
    out_specs = P(None, ("grp", "mom"), None)
    return jax.shard_map(body, mesh=mesh, in_specs=in_specs, out_specs=out_specs, check_vma=False)
```

time: 95.1 us -> 29.9 us (0.31)
  between operations: 23.5 us -> 0.08 us
  matrix products: 21.8 us -> 0 us
  local copies, waits for them, and re-layouts: 16 us -> 0.69 us
  Pallas kernels: 0 us -> 15 us
  waiting for transfers between devices: 19.1 us -> 6.07 us
  other arithmetic: 5.21 us -> 0 us
  starting transfers between devices: 8.86 us -> 7.88 us
    dot_general x15 -> x0, matrix products: 21.8 us -> none  [the longest x12 18.1 us: stop_term(): lax.dot_general(product, right_list[mode_index], (((1,), (1,)), ((), ()))...]
    pallas_call x0 -> x5, Pallas kernels: none -> 15 us  [kernel(): pl.pallas_call(function, in_specs=specs or [VMEM] * len(args), out_specs=...]
    ppermute x6 -> x8, waiting for transfers between devices: 19.1 us -> 6.07 us  [the longest x6 3.76 us: partner(): return lax.ppermute(block, axis, [(i, i ^ 1 << bit) for i in range(count)])]
    squeeze x2 -> x0, local copies, waits for them, and re-layouts: 8.39 us -> none  [the longest x1 4.36 us: stack_coupling(): upper_half = jnp.concatenate([coupling[0], coupling[1]], axis=1)]
    neg x2 -> x0, other arithmetic: 3.45 us -> none  [the longest x1 3.38 us: stack_coupling(): lower_half = jnp.concatenate([-coupling[1], coupling[0]], axis=1)]
    unnamed x101 -> x6, local copies, waits for them, and re-layouts: 2.46 us -> 0.69 us
    slice x5 -> x0, local copies, waits for them, and re-layouts: 1.47 us -> none  [the longest x1 0.69 us: stop_term(): weighted = weights[stop_index, mode_index] * contribution]
    transpose x2 -> x0, other arithmetic: 1.46 us -> none  [the longest x1 1.37 us: as_slab(): row_blocks.transpose(1, 0, 2, 3)]
  transfers between devices with their start and end apart: 6 -> 8, of which waited for: 3 -> 3; matrix products, arithmetic and copies ran while one was open for 28% -> 0% of each run, Pallas kernels for 0% -> 47%
where the time goes in v2:
time: 29.9 us; the launch traced here: 29.7 us
  Pallas kernels  15 us (50%)
  starting transfers between devices  7.88 us (26%)
  waiting for transfers between devices  6.07 us (20%)
  local copies, waits for them, and re-layouts  0.69 us (2%)
    pallas_call x5, Pallas kernels, kernel(): pl.pallas_call(function, in_specs=specs or [VMEM] * len(args), out_specs=...  15 us
    ppermute x6, starting transfers between devices, partner(): return lax.ppermute(block, axis, [(i, i ^ 1 << bit) for i in range(count)])  4.05 us
    ppermute x2, starting transfers between devices, passed_along(): lax.ppermute(block, axis, [((i - distance) % count, i) for i in range(cou...  3.82 us
    ppermute x6, waiting for transfers between devices, partner(): return lax.ppermute(block, axis, [(i, i ^ 1 << bit) for i in range(count)])  3.76 us
    ppermute x2, waiting for transfers between devices, passed_along(): lax.ppermute(block, axis, [((i - distance) % count, i) for i in range(cou...  2.31 us
    unnamed x6, local copies, waits for them, and re-layouts  0.69 us
  transfers between devices with their start and end apart: 8, of which 3 were waited for; matrix products, arithmetic and copies ran while one was open for 0% of the time, Pallas kernels for 47%

profile of v2, /device:TPU:0, one launch (start us, length us, event | category | flops | bytes accessed | tf_op | source)
XLA Modules:
  0.0 29.7 jit_solution(8072359289983457561)
XLA Ops:
  0.0 2.9 %collective-permute-start.4 = (bf16[2,128,512]{2,1,0:T(8,128)(2,1)}, bf16[2,128,512]{2,1,0:T(8,128)(2,1)S(1)}, u32[]{:S(2)}, u32[]{:S(2)}) collective-permute-start(bf16[2,128,512]{2,1,0:T(8,128)(2,1)} %refs_0_.1), channel_id=1, source_target_pairs={{0,2},{1,3},{2,0},{3,1},{4,6},{5,7},{6,4},{7,5},{8,10},{9,11},{10,... | collective-permute-start | bytes 786440 | tf_op jit(solution)/shard_map/ppermute | solution.py:16
  2.9 1.6 %collective-permute-start = (bf16[2,128,512]{2,1,0:T(8,128)(2,1)}, bf16[2,128,512]{2,1,0:T(8,128)(2,1)S(1)}, u32[]{:S(2)}, u32[]{:S(2)}) collective-permute-start(bf16[2,128,512]{2,1,0:T(8,128)(2,1)} %refs_0_.1), channel_id=1, source_target_pairs={{12,0},{13,1},{14,2},{15,3},{0,4},{1,5},{2,6},{3,7},{4,8},{5,9},{6... | collective-permute-start | bytes 786440 | tf_op jit(solution)/shard_map/ppermute | solution.py:21
  4.5 0.0 collective-permute-start.3
  4.5 0.0 copy-start
  4.5 0.7 %copy-done = s32[3,4]{1,0:T(4,128)S(1)} copy-done((s32[3,4]{1,0:T(4,128)S(1)}, s32[3,4]{1,0:T(4,128)}, u32[]{:S(2)}) %copy-start) | copy-done | bytes 72
  5.2 0.0 copy-start.1
  5.2 0.0 copy-start.2
  5.2 5.9 %prepare.1 = (bf16[4,2,512,512]{3,2,1,0:T(8,128)(2,1)S(1)}, bf16[4,512,256]{2,1,0:T(8,128)(2,1)S(1)}, bf16[4,2,512,512]{3,2,1,0:T(8,128)(2,1)S(1)}, bf16[4,512,2...) custom-call(s32[3,4]{1,0:T(4,128)S(1)} %copy-done, ...), custom_call_target="tpu_custom_call" | custom-call | bytes 4096 | tf_op jit(solution)/shard_map/prepare/pallas_call | solution.py:117
  11.1 0.0 collective-permute-done.4.refs_2_
  11.1 0.6 %collective-permute-start.5 = (bf16[2,128,512]{2,1,0:T(8,128)(2,1)S(1)}, bf16[2,128,512]{2,1,0:T(8,128)(2,1)S(1)}, u32[]{:S(2)}, u32[]{:S(2)}) collective-permute-start(bf16[2,128,512]{2,1,0:T(8,128)(2,1)S(1)} %collective-permute-done.4.refs_2_), channel_id=1, source_target_pairs={{0,1},{1,0},{2,3},{3,2},{4,5},{5,4},{6,7},{7,6},{8,9},{9,8},{10,11... | collective-permute-start | bytes 786440 | tf_op jit(solution)/shard_map/ppermute | solution.py:16
  11.7 1.1 %collective-permute-done.refs_0_ = bf16[2,128,512]{2,1,0:T(8,128)(2,1)S(1)} collective-permute-done((bf16[2,128,512]{2,1,0:T(8,128)(2,1)}, bf16[2,128,512]{2,1,0:T(8,128)(2,1)S(1)}, u32[]{:S(2)}, u32[]{:S(2)}) %collective-permute-start) | collective-permute-done | bytes 262176 | tf_op jit(solution)/shard_map/ppermute | solution.py:21
  12.8 0.5 %collective-permute-start.2 = (bf16[2,128,512]{2,1,0:T(8,128)(2,1)S(1)}, bf16[2,128,512]{2,1,0:T(8,128)(2,1)S(1)}, u32[]{:S(2)}, u32[]{:S(2)}) collective-permute-start(bf16[2,128,512]{2,1,0:T(8,128)(2,1)S(1)} %collective-permute-done.refs_0_), channel_id=1, source_target_pairs={{0,2},{1,3},{2,0},{3,1},{4,6},{5,7},{6,4},{7,5},{8,10},{9,11},{10,... | collective-permute-start | bytes 786440 | tf_op jit(solution)/shard_map/ppermute | solution.py:16
  13.3 0.0 collective-permute-start.1
  13.3 0.0 collective-permute-done.3.refs_1_
  13.3 0.0 collective-permute-done.5.refs_3_
  13.4 0.0 copy-done.1
  13.4 0.0 copy-done.2
  13.4 2.9 %later_stop.1 = (bf16[512,256]{1,0:T(8,128)(2,1)S(1)}, bf16[512,1024]{1,0:T(8,128)(2,1)S(1)}) custom-call(bf16[2,128,512]{2,1,0:T(8,128)(2,1)S(1)} %copy-done.1, bf16[2,128,512]{2,1,0:T(8,128)(2,1)S(1)} %collective-permute-done.3.refs_1_, bf16[2,128,512]{2,1,0:T(8,128)(2,1)S(1)} %collective-permute-done.4.refs_2_, ...), custom_call_target="tpu_custom_call" | custom-call | flops 2147483648 | bytes 4096 | tf_op jit(solution)/shard_map/later_stop/pallas_call | solution.py:117
  16.2 3.8 %collective-permute-done.2.refs_2_ = bf16[2,128,512]{2,1,0:T(8,128)(2,1)S(1)} collective-permute-done((bf16[2,128,512]{2,1,0:T(8,128)(2,1)S(1)}, bf16[2,128,512]{2,1,0:T(8,128)(2,1)S(1)}, u32[]{:S(2)}, u32[]{:S(2)}) %collective-permute-start.2) | collective-permute-done | bytes 262176 | tf_op jit(solution)/shard_map/ppermute | solution.py:16
  20.0 0.0 collective-permute-start.6
  20.0 2.2 %collective-permute-start.7 = (bf16[512,256]{1,0:T(8,128)(2,1)S(1)}, bf16[512,256]{1,0:T(8,128)(2,1)S(1)}, u32[]{:S(2)}, u32[]{:S(2)}) collective-permute-start(bf16[512,256]{1,0:T(8,128)(2,1)S(1)} %get-tuple-element.18), channel_id=1, source_target_pairs={{4,0},{5,1},{6,2},{7,3},{8,4},{9,5},{10,6},{11,7},{12,8},{13,9},{1... | collective-permute-start | bytes 786440 | tf_op jit(solution)/shard_map/ppermute | solution.py:21
  22.2 2.4 %own_stop.1.refs_7_ = f32[512,256]{1,0:T(8,128)S(1)} custom-call(bf16[512,1024]{1,0:T(8,128)(2,1)S(1)} %get-tuple-element.22.spectral, f32[3,4]{1,0:T(4,128)S(1)} %copy-done.2, bf16[4,512,256]{2,1,0:T(8,128)(2,1)S(1)} %get-tuple-element.23.turned, bf16[4,2,512,512]{3,2,1,0:T(8,128)(2,1)S(1)} %get-tuple-element.24.picked), custom_call_target="tpu_custom_call" | custom-call | flops 2147483648 | bytes 4096 | tf_op jit(solution)/shard_map/own_stop/pallas_call | solution.py:117
  24.7 0.0 collective-permute-done.1.refs_1_
  24.7 0.0 collective-permute-done.6.refs_3_
  24.7 2.8 %earlier_stop.1.total = f32[512,256]{1,0:T(8,128)S(1)} custom-call(bf16[2,128,512]{2,1,0:T(8,128)(2,1)S(1)} %collective-permute-done.refs_0_, bf16[2,128,512]{2,1,0:T(8,128)(2,1)S(1)} %collective-permute-done.1.refs_1_, bf16[2,128,512]{2,1,0:T(8,128)(2,1)S(1)} %collective-permute-done.2.refs_2_, bf16[2,128,512]{2,1,0:T(8,128)(2,1)S(1)} %collective-permute-done.6.refs_3_, ...), custom_call_target="tpu_custom_call" | custom-call | flops 2147483648 | bytes 4096 | tf_op jit(solution)/shard_map/earlier_stop/pallas_call | solution.py:117
  27.5 1.2 %collective-permute-done.7.arrived = bf16[512,256]{1,0:T(8,128)(2,1)S(1)} collective-permute-done((bf16[512,256]{1,0:T(8,128)(2,1)S(1)}, bf16[512,256]{1,0:T(8,128)(2,1)S(1)}, u32[]{:S(2)}, u32[]{:S(2)}) %collective-permute-start.7) | collective-permute-done | bytes 262176 | tf_op jit(solution)/shard_map/ppermute | solution.py:21
  28.7 1.0 %finish.1 = f32[2,128,512]{2,1,0:T(8,128)} custom-call(f32[512,256]{1,0:T(8,128)S(1)} %earlier_stop.1.total, bf16[512,256]{1,0:T(8,128)(2,1)S(1)} %collective-permute-done.7.arrived), custom_call_target="tpu_custom_call" | custom-call | bytes 4096 | tf_op jit(solution)/shard_map/finish/pallas_call | solution.py:117
Async XLA Ops:
  0.0 11.1 %collective-permute-start.4 = (bf16[2,128,512]{2,1,0:T(8,128)(2,1)}, bf16[2,128,512]{2,1,0:T(8,128)(2,1)S(1)}, u32[]{:S(2)}, u32[]{:S(2)}) collective-permute-start(bf16[2,128,512]{2,1,0:T(8,128)(2,1)} %refs_0_.1), channel_id=1, source_target_pairs={{0,2},{1,3},{2,0},{3,1},{4,6},{5,7},{6,4},{7,5},{8,10},{9,11},{10,... | collective-permute-start | bytes 786440 | tf_op jit(solution)/shard_map/ppermute | solution.py:16
  2.9 9.9 %collective-permute-start = (bf16[2,128,512]{2,1,0:T(8,128)(2,1)}, bf16[2,128,512]{2,1,0:T(8,128)(2,1)S(1)}, u32[]{:S(2)}, u32[]{:S(2)}) collective-permute-start(bf16[2,128,512]{2,1,0:T(8,128)(2,1)} %refs_0_.1), channel_id=1, source_target_pairs={{12,0},{13,1},{14,2},{15,3},{0,4},{1,5},{2,6},{3,7},{4,8},{5,9},{6... | collective-permute-start | bytes 786440 | tf_op jit(solution)/shard_map/ppermute | solution.py:21
  4.5 8.8 %collective-permute-start.3 = (bf16[2,128,512]{2,1,0:T(8,128)(2,1)}, bf16[2,128,512]{2,1,0:T(8,128)(2,1)S(1)}, u32[]{:S(2)}, u32[]{:S(2)}) collective-permute-start(bf16[2,128,512]{2,1,0:T(8,128)(2,1)} %refs_0_.1), channel_id=1, source_target_pairs={{0,1},{1,0},{2,3},{3,2},{4,5},{5,4},{6,7},{7,6},{8,9},{9,8},{10,11... | collective-permute-start | bytes 786440 | tf_op jit(solution)/shard_map/ppermute | solution.py:16
  4.5 0.7 %copy-start = (s32[3,4]{1,0:T(4,128)S(1)}, s32[3,4]{1,0:T(4,128)}, u32[]{:S(2)}) copy-start(s32[3,4]{1,0:T(4,128)} %listed.1) | copy-start | bytes 148
  5.2 8.2 %copy-start.1 = (bf16[2,128,512]{2,1,0:T(8,128)(2,1)S(1)}, bf16[2,128,512]{2,1,0:T(8,128)(2,1)}, u32[]{:S(2)}) copy-start(bf16[2,128,512]{2,1,0:T(8,128)(2,1)} %refs_0_.1) | copy-start | bytes 786436
  5.2 8.2 %copy-start.2 = (f32[3,4]{1,0:T(4,128)S(1)}, f32[3,4]{1,0:T(4,128)}, u32[]{:S(2)}) copy-start(f32[3,4]{1,0:T(4,128)} %refs_4_.3) | copy-start | bytes 148
  11.1 2.2 %collective-permute-start.5 = (bf16[2,128,512]{2,1,0:T(8,128)(2,1)S(1)}, bf16[2,128,512]{2,1,0:T(8,128)(2,1)S(1)}, u32[]{:S(2)}, u32[]{:S(2)}) collective-permute-start(bf16[2,128,512]{2,1,0:T(8,128)(2,1)S(1)} %collective-permute-done.4.refs_2_), channel_id=1, source_target_pairs={{0,1},{1,0},{2,3},{3,2},{4,5},{5,4},{6,7},{7,6},{8,9},{9,8},{10,11... | collective-permute-start | bytes 786440 | tf_op jit(solution)/shard_map/ppermute | solution.py:16
  12.8 7.2 %collective-permute-start.2 = (bf16[2,128,512]{2,1,0:T(8,128)(2,1)S(1)}, bf16[2,128,512]{2,1,0:T(8,128)(2,1)S(1)}, u32[]{:S(2)}, u32[]{:S(2)}) collective-permute-start(bf16[2,128,512]{2,1,0:T(8,128)(2,1)S(1)} %collective-permute-done.refs_0_), channel_id=1, source_target_pairs={{0,2},{1,3},{2,0},{3,1},{4,6},{5,7},{6,4},{7,5},{8,10},{9,11},{10,... | collective-permute-start | bytes 786440 | tf_op jit(solution)/shard_map/ppermute | solution.py:16
  13.3 11.3 %collective-permute-start.1 = (bf16[2,128,512]{2,1,0:T(8,128)(2,1)S(1)}, bf16[2,128,512]{2,1,0:T(8,128)(2,1)S(1)}, u32[]{:S(2)}, u32[]{:S(2)}) collective-permute-start(bf16[2,128,512]{2,1,0:T(8,128)(2,1)S(1)} %collective-permute-done.refs_0_), channel_id=1, source_target_pairs={{0,1},{1,0},{2,3},{3,2},{4,5},{5,4},{6,7},{7,6},{8,9},{9,8},{10,11... | collective-permute-start | bytes 786440 | tf_op jit(solution)/shard_map/ppermute | solution.py:16
  20.0 4.7 %collective-permute-start.6 = (bf16[2,128,512]{2,1,0:T(8,128)(2,1)S(1)}, bf16[2,128,512]{2,1,0:T(8,128)(2,1)S(1)}, u32[]{:S(2)}, u32[]{:S(2)}) collective-permute-start(bf16[2,128,512]{2,1,0:T(8,128)(2,1)S(1)} %collective-permute-done.2.refs_2_), channel_id=1, source_target_pairs={{0,1},{1,0},{2,3},{3,2},{4,5},{5,4},{6,7},{7,6},{8,9},{9,8},{10,11... | collective-permute-start | bytes 786440 | tf_op jit(solution)/shard_map/ppermute | solution.py:16
  20.0 8.7 %collective-permute-start.7 = (bf16[512,256]{1,0:T(8,128)(2,1)S(1)}, bf16[512,256]{1,0:T(8,128)(2,1)S(1)}, u32[]{:S(2)}, u32[]{:S(2)}) collective-permute-start(bf16[512,256]{1,0:T(8,128)(2,1)S(1)} %get-tuple-element.18), channel_id=1, source_target_pairs={{4,0},{5,1},{6,2},{7,3},{8,4},{9,5},{10,6},{11,7},{12,8},{13,9},{1... | collective-permute-start | bytes 786440 | tf_op jit(solution)/shard_map/ppermute | solution.py:21

commit v3 on v2

v3 whole, which is shorter than its diff:
```python
import jax
import jax.numpy as jnp
from jax import lax
from jax.experimental import pallas as pl
from jax.experimental.pallas import tpu as pltpu
from jax.sharding import PartitionSpec as P

F32 = jnp.float32
BF16 = jnp.bfloat16
VMEM = pl.BlockSpec(memory_space=pltpu.VMEM)
ANY = pl.BlockSpec(memory_space=pl.ANY)


def partner(block, axis, bit):
    count = lax.axis_size(axis)
    return lax.ppermute(block, axis, [(i, i ^ 1 << bit) for i in range(count)])


def passed_along(block, axis, distance):
    count = lax.axis_size(axis)
    return lax.ppermute(block, axis, [((i - distance) % count, i) for i in range(count)])


def after(value, *before):
    return lax.optimization_barrier((value, *before))[0]


def gathered(block, axis, levels, before, halves=None):
    have = {0: block}
    for level in reversed(range(levels)):
        for offset in list(have):
            moving = have[offset] if offset == 0 else after(have[offset], before)
            if halves and offset:
                have[offset | 1 << level] = tuple(partner(part, axis, level) for part in halves(moving))
            else:
                have[offset | 1 << level] = partner(moving, axis, level)
    return [have[offset] for offset in sorted(have)]


def beside(first, second):
    return jnp.concatenate([first, second], axis=1)


def own_row(offset, group, tile):
    member = lax.axis_index("mom") % group
    return pl.multiple_of((member ^ offset) * tile, tile)


def fill_spectral(blocks, spectral):
    tile, slab = blocks[0].shape[1:]
    reals = [block[0] if isinstance(block, tuple) else block.at[0] for block in blocks]
    imags = [block[1] if isinstance(block, tuple) else block.at[1] for block in blocks]
    starts = [own_row(offset, len(blocks), tile) for offset in range(len(blocks))]
    spots = [pl.ds(start, tile) for start in starts]
    imag_spots = [pl.ds(slab + start, tile) for start in starts]
    for i in range(len(blocks)):
        for j in range(len(blocks)):
            real = -(imags[i][:, spots[j]].astype(F32) + imags[j][:, spots[i]].T.astype(F32))
            imag = reals[i][:, spots[j]].astype(F32) - reals[j][:, spots[i]].T.astype(F32)
            spectral[spots[i], spots[j]] = real.astype(BF16)
            spectral[spots[i], imag_spots[j]] = imag.astype(BF16)


def stop_term(stop, weights, spectral, turned, couplings, chosen, listing, start):
    count, slab, width = turned.shape
    tile = width // 2
    rights = []
    for mode in range(count):
        real, imag = turned[mode, :, :tile], turned[mode, :, tile:]
        rights.append(jnp.concatenate([beside(real, -imag), beside(imag, real)], axis=0))
    products = jnp.dot(
        spectral[...], jnp.concatenate(rights, axis=1), preferred_element_type=F32
    ).astype(BF16)
    listing.wait()
    total = start
    for mode in range(count):
        product = products[:, mode * width : (mode + 1) * width]
        real, imag = product[:, :tile], product[:, tile:]
        right = jnp.concatenate([product, beside(-imag, real)], axis=0)
        index = chosen[stop, mode]
        left = beside(couplings[index, 0], couplings[index, 1])
        term = weights[stop : stop + 1, mode : mode + 1] * jnp.dot(
            left, right, preferred_element_type=F32
        )
        total = term if total is None else total + term
    return total


def body(green_function, couplings, phonon_modes, weights):
    tile, slab = green_function.shape[1:]
    group = slab // tile
    levels = group.bit_length() - 1
    stops, modes = phonon_modes.shape
    width = 2 * tile
    term_shape = (slab, width)
    spectral_shape = (slab, 2 * slab)

    def kernel(name, function, args, outs, scratch=()):
        def started(listed, *refs):
            *refs, chosen, sem = refs
            listing = pltpu.make_async_copy(listed, chosen, sem)
            listing.start()
            function(listing, chosen, *refs)

        return pl.pallas_call(
            started,
            in_specs=[ANY] + [VMEM] * (len(args) - 1),
            out_specs=[VMEM] * len(outs),
            out_shape=[jax.ShapeDtypeStruct(*out) for out in outs],
            scratch_shapes=[*scratch, pltpu.SMEM((stops, modes), jnp.int32), pltpu.SemaphoreType.DMA],
            compiler_params=pltpu.CompilerParams(vmem_limit_bytes=12 << 20),
            cost_estimate=pl.CostEstimate(flops=0, transcendentals=0, bytes_accessed=4096),
            name=name,
        )(*args)

    def prepare(listing, chosen, couplings, *turned):
        listing.wait()
        rows = pl.ds(own_row(0, group, tile), tile)
        for stop in range(stops):
            for mode in range(modes):
                index = chosen[stop, mode]
                turned[stop][mode, :, :tile] = couplings[index, 0, rows, :].T
                turned[stop][mode, :, tile:] = couplings[index, 1, rows, :].T

    incoming = passed_along(green_function, "mom", group)
    turned = kernel("prepare", prepare, [phonon_modes, couplings], [((modes, slab, width), BF16)] * stops)
    own_blocks = gathered(green_function, "mom", levels, turned[0])

    def later(listing, chosen, *refs):
        *blocks, weights, turned, couplings, leaving, spectral = refs
        fill_spectral(blocks, spectral)
        leaving[...] = stop_term(
            0, weights, spectral, turned, couplings, chosen, listing, None
        ).astype(BF16)

    leaving, spectral = kernel(
        "later_stop",
        later,
        [phonon_modes, *own_blocks, weights, turned[0], couplings],
        [(term_shape, BF16), (spectral_shape, BF16)],
    )
    arrived = passed_along(leaving, "mom", -group)

    def own(listing, chosen, spectral, weights, turned, couplings, out):
        out[...] = stop_term(1, weights, spectral, turned, couplings, chosen, listing, None)

    (total,) = kernel(
        "own_stop", own, [phonon_modes, spectral, weights, turned[1], couplings], [(term_shape, F32)]
    )

    def halves(block):
        def split(block, real, imag):
            real[...] = block[0]
            imag[...] = block[1]

        half = jax.ShapeDtypeStruct(block.shape[1:], block.dtype)
        return pl.pallas_call(
            split,
            in_specs=[VMEM],
            out_specs=[VMEM] * 2,
            out_shape=[half] * 2,
            compiler_params=pltpu.CompilerParams(vmem_limit_bytes=4 << 20),
            cost_estimate=pl.CostEstimate(flops=0, transcendentals=0, bytes_accessed=4096),
            name="split",
        )(block)

    next_blocks = gathered(incoming, "mom", levels, total, halves)

    def earlier(listing, chosen, *refs):
        *parts, weights, turned, couplings, before, out, spectral = refs
        parts = iter(parts)
        blocks = [(next(parts), next(parts)) if isinstance(b, tuple) else next(parts) for b in next_blocks]
        fill_spectral(blocks, spectral)
        out[...] = stop_term(2, weights, spectral, turned, couplings, chosen, listing, before[...])

    (total,) = kernel(
        "earlier_stop",
        earlier,
        [phonon_modes, *jax.tree.leaves(next_blocks), weights, turned[2], couplings, total],
        [(term_shape, F32)],
        [pltpu.VMEM(spectral_shape, BF16)],
    )

    def finish(total, arrived, out):
        whole = total[...] + arrived[...].astype(F32)
        out[0] = whole[:, :tile].T
        out[1] = -whole[:, tile:].T

    return pl.pallas_call(
        finish,
        in_specs=[VMEM, VMEM],
        out_specs=VMEM,
        out_shape=jax.ShapeDtypeStruct((2, tile, slab), F32),
        compiler_params=pltpu.CompilerParams(vmem_limit_bytes=4 << 20),
        cost_estimate=pl.CostEstimate(flops=0, transcendentals=0, bytes_accessed=4096),
        name="finish",
    )(total, arrived)


def solution(mesh):
    in_specs = (P(None, ("grp", "mom"), None), P(), P(), P())
    out_specs = P(None, ("grp", "mom"), None)
    return jax.shard_map(body, mesh=mesh, in_specs=in_specs, out_specs=out_specs, check_vma=False)
```

time: 29.9 us -> 26.6 us (0.89)
  Pallas kernels: 15 us -> 11.1 us
  local copies, waits for them, and re-layouts: 0.69 us -> 4.09 us
  waiting for transfers between devices: 6.07 us -> 3.23 us
    pallas_call x5 -> x6, Pallas kernels: 15 us -> 11.1 us  [the longest x4 10.1 us: kernel(): pl.pallas_call(started, in_specs=[ANY] + [VMEM] * (len(args) - 1), out_sp...]
    unnamed x6 -> x14, local copies, waits for them, and re-layouts: 0.69 us -> 4.09 us
    ppermute x6 -> x7, waiting for transfers between devices: 3.76 us -> 1.07 us  [partner(): return lax.ppermute(block, axis, [(i, i ^ 1 << bit) for i in range(count)])]
    ppermute x6 -> x7, starting transfers between devices: 4.05 us -> 4.63 us  [partner(): return lax.ppermute(block, axis, [(i, i ^ 1 << bit) for i in range(count)])]
    ppermute x2, starting transfers between devices: 3.82 us -> 3.34 us  [passed_along(): lax.ppermute(block, axis, [((i - distance) % count, i) for i in range(cou...]
  transfers between devices with their start and end apart: 8 -> 9, of which waited for: 3 -> 3; matrix products, arithmetic and copies ran while one was open for 0% -> 0% of each run, Pallas kernels for 47% -> 38%
where the time goes in v3:
time: 26.6 us; the launch traced here: 26.5 us
  Pallas kernels  11.1 us (42%)
  starting transfers between devices  7.96 us (30%)
  local copies, waits for them, and re-layouts  4.09 us (15%)
  waiting for transfers between devices  3.23 us (12%)
    pallas_call x4, Pallas kernels, kernel(): pl.pallas_call(started, in_specs=[ANY] + [VMEM] * (len(args) - 1), out_sp...  10.1 us
    ppermute x7, starting transfers between devices, partner(): return lax.ppermute(block, axis, [(i, i ^ 1 << bit) for i in range(count)])  4.63 us
    unnamed x14, local copies, waits for them, and re-layouts  4.09 us
    ppermute x2, starting transfers between devices, passed_along(): lax.ppermute(block, axis, [((i - distance) % count, i) for i in range(cou...  3.34 us
    ppermute x2, waiting for transfers between devices, passed_along(): lax.ppermute(block, axis, [((i - distance) % count, i) for i in range(cou...  2.16 us
    ppermute x7, waiting for transfers between devices, partner(): return lax.ppermute(block, axis, [(i, i ^ 1 << bit) for i in range(count)])  1.07 us
    pallas_call x1, Pallas kernels, body(): pl.pallas_call(finish, in_specs=[VMEM, VMEM], out_specs=VMEM, out_shape=j...  1 us
  transfers between devices with their start and end apart: 9, of which 3 were waited for; matrix products, arithmetic and copies ran while one was open for 0% of the time, Pallas kernels for 38%

profile of v3, /device:TPU:0, one launch (start us, length us, event | category | flops | bytes accessed | tf_op | source)
XLA Modules:
  0.0 26.5 jit_solution(7223589253855023889)
XLA Ops:
  0.0 2.9 %collective-permute-start.4 = (bf16[2,128,512]{2,1,0:T(8,128)(2,1)}, bf16[2,128,512]{2,1,0:T(8,128)(2,1)S(1)}, u32[]{:S(2)}, u32[]{:S(2)}) collective-permute-start(bf16[2,128,512]{2,1,0:T(8,128)(2,1)} %refs_0_.3), channel_id=1, source_target_pairs={{0,2},{1,3},{2,0},{3,1},{4,6},{5,7},{6,4},{7,5},{8,10},{9,11},{10,... | collective-permute-start | bytes 786440 | tf_op jit(solution)/shard_map/ppermute | solution.py:16
  2.9 1.6 %collective-permute-start = (bf16[2,128,512]{2,1,0:T(8,128)(2,1)}, bf16[2,128,512]{2,1,0:T(8,128)(2,1)S(1)}, u32[]{:S(2)}, u32[]{:S(2)}) collective-permute-start(bf16[2,128,512]{2,1,0:T(8,128)(2,1)} %refs_0_.3), channel_id=1, source_target_pairs={{12,0},{13,1},{14,2},{15,3},{0,4},{1,5},{2,6},{3,7},{4,8},{5,9},{6... | collective-permute-start | bytes 786440 | tf_op jit(solution)/shard_map/ppermute | solution.py:21
  4.5 0.0 collective-permute-start.3
  4.5 0.0 copy-start
  4.5 3.4 %copy-done = bf16[8,2,512,512]{3,2,1,0:T(8,128)(2,1)S(1)} copy-done((bf16[8,2,512,512]{3,2,1,0:T(8,128)(2,1)S(1)}, bf16[8,2,512,512]{3,2,1,0:T(8,128)(2,1)}, u32[]{:S(2)}) %copy-start) | copy-done | bytes 8388632
  7.9 0.0 copy-start.2
  7.9 0.7 %copy-done.2 = s32[3,4]{1,0:T(4,128)S(1)} copy-done((s32[3,4]{1,0:T(4,128)S(1)}, s32[3,4]{1,0:T(4,128)}, u32[]{:S(2)}) %copy-start.2) | copy-done | bytes 72
  8.6 0.0 copy-start.1
  8.6 0.0 copy-start.4
  8.6 1.4 %prepare.1 = (bf16[4,512,256]{2,1,0:T(8,128)(2,1)S(1)}, bf16[4,512,256]{2,1,0:T(8,128)(2,1)S(1)}, bf16[4,512,256]{2,1,0:T(8,128)(2,1)S(1)}) custom-call(s32[3,4]{1,0:T(4,128)S(1)} %copy-done.2, bf16[8,2,512,512]{3,2,1,0:T(8,128)(2,1)S(1)} %copy-done), custom_call_target="tpu_custom_call" | custom-call | bytes 4096 | tf_op jit(solution)/shard_map/prepare/pallas_call | solution.py:105
  10.0 0.0 collective-permute-done.4.refs_2_
  10.0 0.0 slice-start
  10.1 0.0 copy-start.3
  10.1 0.6 %collective-permute-start.5 = (bf16[2,128,512]{2,1,0:T(8,128)(2,1)S(1)}, bf16[2,128,512]{2,1,0:T(8,128)(2,1)S(1)}, u32[]{:S(2)}, u32[]{:S(2)}) collective-permute-start(bf16[2,128,512]{2,1,0:T(8,128)(2,1)S(1)} %collective-permute-done.4.refs_2_), channel_id=1, source_target_pairs={{0,1},{1,0},{2,3},{3,2},{4,5},{5,4},{6,7},{7,6},{8,9},{9,8},{10,11... | collective-permute-start | bytes 786440 | tf_op jit(solution)/shard_map/ppermute | solution.py:16
  10.6 2.2 %collective-permute-done.refs_0_ = bf16[2,128,512]{2,1,0:T(8,128)(2,1)S(1)} collective-permute-done((bf16[2,128,512]{2,1,0:T(8,128)(2,1)}, bf16[2,128,512]{2,1,0:T(8,128)(2,1)S(1)}, u32[]{:S(2)}, u32[]{:S(2)}) %collective-permute-start) | collective-permute-done | bytes 262176 | tf_op jit(solution)/shard_map/ppermute | solution.py:21
  12.8 0.5 %collective-permute-start.2 = (bf16[2,128,512]{2,1,0:T(8,128)(2,1)S(1)}, bf16[2,128,512]{2,1,0:T(8,128)(2,1)S(1)}, u32[]{:S(2)}, u32[]{:S(2)}) collective-permute-start(bf16[2,128,512]{2,1,0:T(8,128)(2,1)S(1)} %collective-permute-done.refs_0_), channel_id=1, source_target_pairs={{0,2},{1,3},{2,0},{3,1},{4,6},{5,7},{6,4},{7,5},{8,10},{9,11},{10,... | collective-permute-start | bytes 786440 | tf_op jit(solution)/shard_map/ppermute | solution.py:16
  13.3 0.0 collective-permute-start.1
  13.3 0.0 collective-permute-done.3.refs_1_
  13.3 0.0 collective-permute-done.5.refs_3_
  13.4 0.0 copy-done.1
  13.4 0.0 copy-done.4
  13.4 3.0 %later_stop.1 = (bf16[512,256]{1,0:T(8,128)(2,1)S(1)}, bf16[512,1024]{1,0:T(8,128)(2,1)S(1)}) custom-call(s32[3,4]{1,0:T(4,128)S(1)} %copy-done.2, bf16[2,128,512]{2,1,0:T(8,128)(2,1)S(1)} %copy-done.1, bf16[2,128,512]{2,1,0:T(8,128)(2,1)S(1)} %collective-permute-done.3.refs_1_, bf16[2,128,512]{2,1,0:T(8,128)(2,1)S(1)} %collective-permute-done.4.refs_2_, ...), custom_call_target="tpu_custom_call" | custom-call | bytes 4096 | tf_op jit(solution)/shard_map/later_stop/pallas_call | solution.py:105
  16.4 1.8 %collective-permute-start.8 = (bf16[512,256]{1,0:T(8,128)(2,1)S(1)}, bf16[512,256]{1,0:T(8,128)(2,1)S(1)}, u32[]{:S(2)}, u32[]{:S(2)}) collective-permute-start(bf16[512,256]{1,0:T(8,128)(2,1)S(1)} %get-tuple-element.22), channel_id=1, source_target_pairs={{4,0},{5,1},{6,2},{7,3},{8,4},{9,5},{10,6},{11,7},{12,8},{13,9},{1... | collective-permute-start | bytes 786440 | tf_op jit(solution)/shard_map/ppermute | solution.py:21
  18.2 0.0 slice-start.1
  18.2 2.6 %own_stop.1.refs_8_ = f32[512,256]{1,0:T(8,128)S(1)} custom-call(s32[3,4]{1,0:T(4,128)S(1)} %copy-done.2, bf16[512,1024]{1,0:T(8,128)(2,1)S(1)} %get-tuple-element.16.refs_0_, f32[3,4]{1,0:T(4,128)S(1)} %copy-done.4, bf16[4,512,256]{2,1,0:T(8,128)(2,1)S(1)} %get-tuple-element.17.refs_2_, bf16[8,2,512,512]{3,2,1,0:T(8,128)(2,1)S(1)} %copy-done), custom_call_target="tpu_custom_call" | custom-call | bytes 4096 | tf_op jit(solution)/shard_map/own_stop/pallas_call | solution.py:105
  20.8 0.0 collective-permute-done.2.block.refs_2_
  20.8 0.3 %collective-permute-start.6 = (bf16[128,512]{1,0:T(8,128)(2,1)S(1)}, bf16[128,512]{1,0:T(8,128)(2,1)S(1)}, u32[]{:S(2)}, u32[]{:S(2)}) collective-permute-start(bf16[128,512]{1,0:T(8,128)(2,1)S(1)} %get-tuple-element.19), channel_id=1, source_target_pairs={{0,1},{1,0},{2,3},{3,2},{4,5},{5,4},{6,7},{7,6},{8,9},{9,8},{10,11... | collective-permute-start | bytes 393224 | tf_op jit(solution)/shard_map/ppermute | solution.py:16
  21.1 0.3 %collective-permute-start.7 = (bf16[128,512]{1,0:T(8,128)(2,1)S(1)}, bf16[128,512]{1,0:T(8,128)(2,1)S(1)}, u32[]{:S(2)}, u32[]{:S(2)}) collective-permute-start(bf16[128,512]{1,0:T(8,128)(2,1)S(1)} %get-tuple-element.20), channel_id=1, source_target_pairs={{0,1},{1,0},{2,3},{3,2},{4,5},{5,4},{6,7},{7,6},{8,9},{9,8},{10,11... | collective-permute-start | bytes 393224 | tf_op jit(solution)/shard_map/ppermute | solution.py:16
  21.4 0.0 collective-permute-done.1.refs_1_
  21.4 0.8 %collective-permute-done.6.refs_3_ = bf16[128,512]{1,0:T(8,128)(2,1)S(1)} collective-permute-done((bf16[128,512]{1,0:T(8,128)(2,1)S(1)}, bf16[128,512]{1,0:T(8,128)(2,1)S(1)}, u32[]{:S(2)}, u32[]{:S(2)}) %collective-permute-start.6) | collective-permute-done | bytes 131104 | tf_op jit(solution)/shard_map/ppermute | solution.py:16
  22.2 0.2 collective-permute-done.7.refs_4_
  22.4 0.0 slice-done
  22.4 0.0 copy-done.3
  22.4 0.0 slice-done.1
  22.5 3.0 %earlier_stop.1.total = f32[512,256]{1,0:T(8,128)S(1)} custom-call(s32[3,4]{1,0:T(4,128)S(1)} %copy-done.3, bf16[2,128,512]{2,1,0:T(8,128)(2,1)S(1)} %collective-permute-done.refs_0_, bf16[2,128,512]{2,1,0:T(8,128)(2,1)S(1)} %collective-permute-done.1.refs_1_, bf16[2,128,512]{2,1,0:T(8,128)(2,1)S(1)} %collective-permute-done.2.block.refs_2_, ...), custom_call_target="tpu_custom_call" | custom-call | bytes 4096 | tf_op jit(solution)/shard_map/earlier_stop/pallas_call | solution.py:105
  25.5 0.0 collective-permute-done.8.arrived
  25.5 1.0 %finish.1 = f32[2,128,512]{2,1,0:T(8,128)} custom-call(f32[512,256]{1,0:T(8,128)S(1)} %earlier_stop.1.total, bf16[512,256]{1,0:T(8,128)(2,1)S(1)} %collective-permute-done.8.arrived), custom_call_target="tpu_custom_call" | custom-call | bytes 4096 | tf_op jit(solution)/shard_map/finish/pallas_call | solution.py:189
  (2 shorter events, 0.0 us)
Async XLA Ops:
  0.0 10.0 %collective-permute-start.4 = (bf16[2,128,512]{2,1,0:T(8,128)(2,1)}, bf16[2,128,512]{2,1,0:T(8,128)(2,1)S(1)}, u32[]{:S(2)}, u32[]{:S(2)}) collective-permute-start(bf16[2,128,512]{2,1,0:T(8,128)(2,1)} %refs_0_.3), channel_id=1, source_target_pairs={{0,2},{1,3},{2,0},{3,1},{4,6},{5,7},{6,4},{7,5},{8,10},{9,11},{10,... | collective-permute-start | bytes 786440 | tf_op jit(solution)/shard_map/ppermute | solution.py:16
  2.9 9.9 %collective-permute-start = (bf16[2,128,512]{2,1,0:T(8,128)(2,1)}, bf16[2,128,512]{2,1,0:T(8,128)(2,1)S(1)}, u32[]{:S(2)}, u32[]{:S(2)}) collective-permute-start(bf16[2,128,512]{2,1,0:T(8,128)(2,1)} %refs_0_.3), channel_id=1, source_target_pairs={{12,0},{13,1},{14,2},{15,3},{0,4},{1,5},{2,6},{3,7},{4,8},{5,9},{6... | collective-permute-start | bytes 786440 | tf_op jit(solution)/shard_map/ppermute | solution.py:21
  4.5 8.8 %collective-permute-start.3 = (bf16[2,128,512]{2,1,0:T(8,128)(2,1)}, bf16[2,128,512]{2,1,0:T(8,128)(2,1)S(1)}, u32[]{:S(2)}, u32[]{:S(2)}) collective-permute-start(bf16[2,128,512]{2,1,0:T(8,128)(2,1)} %refs_0_.3), channel_id=1, source_target_pairs={{0,1},{1,0},{2,3},{3,2},{4,5},{5,4},{6,7},{7,6},{8,9},{9,8},{10,11... | collective-permute-start | bytes 786440 | tf_op jit(solution)/shard_map/ppermute | solution.py:16
  4.5 3.4 %copy-start = (bf16[8,2,512,512]{3,2,1,0:T(8,128)(2,1)S(1)}, bf16[8,2,512,512]{3,2,1,0:T(8,128)(2,1)}, u32[]{:S(2)}) copy-start(bf16[8,2,512,512]{3,2,1,0:T(8,128)(2,1)} %refs_7_.1) | copy-start | bytes 25165828
  7.9 0.7 %copy-start.2 = (s32[3,4]{1,0:T(4,128)S(1)}, s32[3,4]{1,0:T(4,128)}, u32[]{:S(2)}) copy-start(s32[3,4]{1,0:T(4,128)} %listed.7) | copy-start | bytes 148
  8.6 4.8 %copy-start.1 = (bf16[2,128,512]{2,1,0:T(8,128)(2,1)S(1)}, bf16[2,128,512]{2,1,0:T(8,128)(2,1)}, u32[]{:S(2)}) copy-start(bf16[2,128,512]{2,1,0:T(8,128)(2,1)} %refs_0_.3) | copy-start | bytes 786436
  8.6 4.8 %copy-start.4 = (f32[3,4]{1,0:T(4,128)S(1)}, f32[3,4]{1,0:T(4,128)}, u32[]{:S(2)}) copy-start(f32[3,4]{1,0:T(4,128)} %refs_5_.1) | copy-start | bytes 148
  10.0 12.4 %slice-start = ((s8[8388608]{0:T(1024)(128)(4,1)}), s8[4194304]{0:T(1024)(128)(4,1)S(1)}, s32[]{:S(2)}) async-start(s8[8388608]{0:T(1024)(128)(4,1)} %bitcast), calls=%async_computation | async-start | bytes 8388608
  10.1 12.4 %copy-start.3 = (s32[3,4]{1,0:T(4,128)S(1)}, s32[3,4]{1,0:T(4,128)}, u32[]{:S(2)}) copy-start(s32[3,4]{1,0:T(4,128)} %listed.7) | copy-start | bytes 148
  10.1 3.3 %collective-permute-start.5 = (bf16[2,128,512]{2,1,0:T(8,128)(2,1)S(1)}, bf16[2,128,512]{2,1,0:T(8,128)(2,1)S(1)}, u32[]{:S(2)}, u32[]{:S(2)}) collective-permute-start(bf16[2,128,512]{2,1,0:T(8,128)(2,1)S(1)} %collective-permute-done.4.refs_2_), channel_id=1, source_target_pairs={{0,1},{1,0},{2,3},{3,2},{4,5},{5,4},{6,7},{7,6},{8,9},{9,8},{10,11... | collective-permute-start | bytes 786440 | tf_op jit(solution)/shard_map/ppermute | solution.py:16
  12.8 8.0 %collective-permute-start.2 = (bf16[2,128,512]{2,1,0:T(8,128)(2,1)S(1)}, bf16[2,128,512]{2,1,0:T(8,128)(2,1)S(1)}, u32[]{:S(2)}, u32[]{:S(2)}) collective-permute-start(bf16[2,128,512]{2,1,0:T(8,128)(2,1)S(1)} %collective-permute-done.refs_0_), channel_id=1, source_target_pairs={{0,2},{1,3},{2,0},{3,1},{4,6},{5,7},{6,4},{7,5},{8,10},{9,11},{10,... | collective-permute-start | bytes 786440 | tf_op jit(solution)/shard_map/ppermute | solution.py:16
  13.3 8.0 %collective-permute-start.1 = (bf16[2,128,512]{2,1,0:T(8,128)(2,1)S(1)}, bf16[2,128,512]{2,1,0:T(8,128)(2,1)S(1)}, u32[]{:S(2)}, u32[]{:S(2)}) collective-permute-start(bf16[2,128,512]{2,1,0:T(8,128)(2,1)S(1)} %collective-permute-done.refs_0_), channel_id=1, source_target_pairs={{0,1},{1,0},{2,3},{3,2},{4,5},{5,4},{6,7},{7,6},{8,9},{9,8},{10,11... | collective-permute-start | bytes 786440 | tf_op jit(solution)/shard_map/ppermute | solution.py:16
  16.4 9.1 %collective-permute-start.8 = (bf16[512,256]{1,0:T(8,128)(2,1)S(1)}, bf16[512,256]{1,0:T(8,128)(2,1)S(1)}, u32[]{:S(2)}, u32[]{:S(2)}) collective-permute-start(bf16[512,256]{1,0:T(8,128)(2,1)S(1)} %get-tuple-element.22), channel_id=1, source_target_pairs={{4,0},{5,1},{6,2},{7,3},{8,4},{9,5},{10,6},{11,7},{12,8},{13,9},{1... | collective-permute-start | bytes 786440 | tf_op jit(solution)/shard_map/ppermute | solution.py:21
  18.2 4.3 %slice-start.1 = ((s8[8388608]{0:T(1024)(128)(4,1)}), s8[4194304]{0:T(1024)(128)(4,1)S(1)}, s32[]{:S(2)}) async-start(s8[8388608]{0:T(1024)(128)(4,1)} %bitcast), calls=%async_computation.1 | async-start | bytes 8388608
  20.8 1.4 %collective-permute-start.6 = (bf16[128,512]{1,0:T(8,128)(2,1)S(1)}, bf16[128,512]{1,0:T(8,128)(2,1)S(1)}, u32[]{:S(2)}, u32[]{:S(2)}) collective-permute-start(bf16[128,512]{1,0:T(8,128)(2,1)S(1)} %get-tuple-element.19), channel_id=1, source_target_pairs={{0,1},{1,0},{2,3},{3,2},{4,5},{5,4},{6,7},{7,6},{8,9},{9,8},{10,11... | collective-permute-start | bytes 393224 | tf_op jit(solution)/shard_map/ppermute | solution.py:16
  21.1 1.3 %collective-permute-start.7 = (bf16[128,512]{1,0:T(8,128)(2,1)S(1)}, bf16[128,512]{1,0:T(8,128)(2,1)S(1)}, u32[]{:S(2)}, u32[]{:S(2)}) collective-permute-start(bf16[128,512]{1,0:T(8,128)(2,1)S(1)} %get-tuple-element.20), channel_id=1, source_target_pairs={{0,1},{1,0},{2,3},{3,2},{4,5},{5,4},{6,7},{7,6},{8,9},{9,8},{10,11... | collective-permute-start | bytes 393224 | tf_op jit(solution)/shard_map/ppermute | solution.py:16

commit v4 on v3

--- a/solution.py
+++ b/solution.py
@@ -11,30 +11,34 @@
 ANY = pl.BlockSpec(memory_space=pl.ANY)
 
 
-def partner(block, axis, bit):
-    count = lax.axis_size(axis)
-    return lax.ppermute(block, axis, [(i, i ^ 1 << bit) for i in range(count)])
+def moved(block, axis, route):
+    return lax.ppermute(block, axis, [(i, route(i)) for i in range(lax.axis_size(axis))])
 
 
 def passed_along(block, axis, distance):
     count = lax.axis_size(axis)
-    return lax.ppermute(block, axis, [((i - distance) % count, i) for i in range(count)])
+    return moved(block, axis, lambda i: (i + distance) % count)
+
+
+def partner(block, axis, bit):
+    return moved(block, axis, lambda i: i ^ 1 << bit)
 
 
 def after(value, *before):
     return lax.optimization_barrier((value, *before))[0]
 
 
-def gathered(block, axis, levels, before, halves=None):
-    have = {0: block}
-    for level in reversed(range(levels)):
-        for offset in list(have):
-            moving = have[offset] if offset == 0 else after(have[offset], before)
-            if halves and offset:
-                have[offset | 1 << level] = tuple(partner(part, axis, level) for part in halves(moving))
+def spread(have, top):
+    for level in reversed(range(top)):
+        for offset, block in list(have.items()):
+            if isinstance(block, tuple):
+                have[offset | 1 << level] = tuple(partner(part, "mom", level) for part in block[1:])
             else:
-                have[offset | 1 << level] = partner(moving, axis, level)
-    return [have[offset] for offset in sorted(have)]
+                have[offset | 1 << level] = partner(block, "mom", level)
+    return [
+        block[0] if isinstance(block, tuple) and len(block) == 3 else block
+        for _, block in sorted(have.items())
+    ]
 
 
 def beside(first, second):
@@ -122,9 +126,37 @@
                 turned[stop][mode, :, :tile] = couplings[index, 0, rows, :].T
                 turned[stop][mode, :, tile:] = couplings[index, 1, rows, :].T
 
+    def quick(name, function, args, outs):
+        return pl.pallas_call(
+            function,
+            in_specs=[VMEM] * len(args),
+            out_specs=[VMEM] * len(outs),
+            out_shape=[jax.ShapeDtypeStruct(*out) for out in outs],
+            compiler_params=pltpu.CompilerParams(vmem_limit_bytes=4 << 20),
+            cost_estimate=pl.CostEstimate(flops=0, transcendentals=0, bytes_accessed=4096),
+            name=name,
+        )(*args)
+
+    def choose(even, odd, out):
+        member = lax.axis_index("mom") % 2
+
+        @pl.when(member == 0)
+        def _():
+            out[...] = even[...]
+
+        @pl.when(member == 1)
+        def _():
+            out[...] = odd[...]
+
+    top = levels - 1
     incoming = passed_along(green_function, "mom", group)
     turned = kernel("prepare", prepare, [phonon_modes, couplings], [((modes, slab, width), BF16)] * stops)
-    own_blocks = gathered(green_function, "mom", levels, turned[0])
+    far = partner(green_function, "mom", top)
+    ready = after(far, turned[0], incoming)
+    own_blocks = spread({0: green_function, 1 << top: ready}, top)
+    (leaves,) = quick("choose", choose, [incoming, ready], [(green_function.shape, BF16)])
+    count = lax.axis_size("mom")
+    next_far = moved(leaves, "mom", lambda i: (i + group) % count if i % 2 else i ^ 1 << top)
 
     def later(listing, chosen, *refs):
         *blocks, weights, turned, couplings, leaving, spectral = refs
@@ -148,23 +180,12 @@
         "own_stop", own, [phonon_modes, spectral, weights, turned[1], couplings], [(term_shape, F32)]
     )
 
-    def halves(block):
-        def split(block, real, imag):
-            real[...] = block[0]
-            imag[...] = block[1]
-
-        half = jax.ShapeDtypeStruct(block.shape[1:], block.dtype)
-        return pl.pallas_call(
-            split,
-            in_specs=[VMEM],
-            out_specs=[VMEM] * 2,
-            out_shape=[half] * 2,
-            compiler_params=pltpu.CompilerParams(vmem_limit_bytes=4 << 20),
-            cost_estimate=pl.CostEstimate(flops=0, transcendentals=0, bytes_accessed=4096),
-            name="split",
-        )(block)
-
-    next_blocks = gathered(incoming, "mom", levels, total, halves)
+    def split(block, real, imag):
+        real[...] = block[0]
+        imag[...] = block[1]
+
+    real, imag = quick("split", split, [after(next_far, leaving)], [((tile, slab), BF16)] * 2)
+    next_blocks = spread({0: incoming, 1 << top: (next_far, real, imag)}, top)
 
     def earlier(listing, chosen, *refs):
         *parts, weights, turned, couplings, before, out, spectral = refs
@@ -186,15 +207,8 @@
         out[0] = whole[:, :tile].T
         out[1] = -whole[:, tile:].T
 
-    return pl.pallas_call(
-        finish,
-        in_specs=[VMEM, VMEM],
-        out_specs=VMEM,
-        out_shape=jax.ShapeDtypeStruct((2, tile, slab), F32),
-        compiler_params=pltpu.CompilerParams(vmem_limit_bytes=4 << 20),
-        cost_estimate=pl.CostEstimate(flops=0, transcendentals=0, bytes_accessed=4096),
-        name="finish",
-    )(total, arrived)
+    (rows,) = quick("finish", finish, [total, arrived], [((2, tile, slab), F32)])
+    return rows
 
 
 def solution(mesh):

time: 26.6 us -> 26.2 us (0.985)
  waiting for transfers between devices: 3.23 us -> 1.54 us
  starting transfers between devices: 7.96 us -> 9.24 us
    ppermute x9, waiting for transfers between devices: 3.23 us -> 1.54 us  [moved(): lax.ppermute(block, axis, [(i, route(i)) for i in range(lax.axis_size(axi...]
    ppermute x9, starting transfers between devices: 7.96 us -> 9.24 us  [moved(): lax.ppermute(block, axis, [(i, route(i)) for i in range(lax.axis_size(axi...]
    pallas_call x2 -> x3, Pallas kernels: 1.02 us -> 1.05 us  [quick(): pl.pallas_call(function, in_specs=[VMEM] * len(args), out_specs=[VMEM] *...]
    unnamed x14 -> x12, local copies, waits for them, and re-layouts: 4.09 us -> 4.08 us
  transfers between devices with their start and end apart: 9 -> 9, of which waited for: 3 -> 1; matrix products, arithmetic and copies ran while one was open for 0% -> 0% of each run, Pallas kernels for 38% -> 39%
where the time goes in v4:
time: 26.2 us; the launch traced here: 26 us
  Pallas kernels  11.1 us (42%)
  starting transfers between devices  9.24 us (35%)
  local copies, waits for them, and re-layouts  4.08 us (16%)
  waiting for transfers between devices  1.54 us (6%)
    pallas_call x4, Pallas kernels, kernel(): pl.pallas_call(started, in_specs=[ANY] + [VMEM] * (len(args) - 1), out_sp...  10 us
    ppermute x9, starting transfers between devices, moved(): lax.ppermute(block, axis, [(i, route(i)) for i in range(lax.axis_size(axi...  9.24 us
    unnamed x12, local copies, waits for them, and re-layouts  4.08 us
    ppermute x9, waiting for transfers between devices, moved(): lax.ppermute(block, axis, [(i, route(i)) for i in range(lax.axis_size(axi...  1.54 us
    pallas_call x3, Pallas kernels, quick(): pl.pallas_call(function, in_specs=[VMEM] * len(args), out_specs=[VMEM] *...  1.05 us
  transfers between devices with their start and end apart: 9, of which 1 were waited for; matrix products, arithmetic and copies ran while one was open for 0% of the time, Pallas kernels for 39%

profile of v4, /device:TPU:0, one launch (start us, length us, event | category | flops | bytes accessed | tf_op | source)
XLA Modules:
  0.0 26.0 jit_solution(501107821977139811)
XLA Ops:
  0.0 3.0 %collective-permute-start = (bf16[2,128,512]{2,1,0:T(8,128)(2,1)}, bf16[2,128,512]{2,1,0:T(8,128)(2,1)S(1)}, u32[]{:S(2)}, u32[]{:S(2)}) collective-permute-start(bf16[2,128,512]{2,1,0:T(8,128)(2,1)} %refs_0_.3), channel_id=1, source_target_pairs={{0,4},{1,5},{2,6},{3,7},{4,8},{5,9},{6,10},{7,11},{8,12},{9,13},{1... | collective-permute-start | bytes 786440 | tf_op jit(solution)/shard_map/ppermute | solution.py:15
  3.0 1.5 %collective-permute-start.2 = (bf16[2,128,512]{2,1,0:T(8,128)(2,1)}, bf16[2,128,512]{2,1,0:T(8,128)(2,1)S(1)}, u32[]{:S(2)}, u32[]{:S(2)}) collective-permute-start(bf16[2,128,512]{2,1,0:T(8,128)(2,1)} %refs_0_.3), channel_id=1, source_target_pairs={{0,2},{1,3},{2,0},{3,1},{4,6},{5,7},{6,4},{7,5},{8,10},{9,11},{10,... | collective-permute-start | bytes 786440 | tf_op jit(solution)/shard_map/ppermute | solution.py:15
  4.5 0.0 collective-permute-start.4
  4.5 0.0 copy-start
  4.5 3.4 %copy-done = bf16[8,2,512,512]{3,2,1,0:T(8,128)(2,1)S(1)} copy-done((bf16[8,2,512,512]{3,2,1,0:T(8,128)(2,1)S(1)}, bf16[8,2,512,512]{3,2,1,0:T(8,128)(2,1)}, u32[]{:S(2)}) %copy-start) | copy-done | bytes 8388632
  7.9 0.0 copy-start.3
  7.9 0.7 %copy-done.3 = s32[3,4]{1,0:T(4,128)S(1)} copy-done((s32[3,4]{1,0:T(4,128)S(1)}, s32[3,4]{1,0:T(4,128)}, u32[]{:S(2)}) %copy-start.3) | copy-done | bytes 72
  8.6 0.0 copy-start.1
  8.6 0.0 copy-start.2
  8.6 0.0 copy-start.4
  8.6 0.0 copy-start.5
  8.6 1.4 %prepare.1 = (bf16[4,512,256]{2,1,0:T(8,128)(2,1)S(1)}, bf16[4,512,256]{2,1,0:T(8,128)(2,1)S(1)}, bf16[4,512,256]{2,1,0:T(8,128)(2,1)S(1)}) custom-call(s32[3,4]{1,0:T(4,128)S(1)} %copy-done.3, bf16[8,2,512,512]{3,2,1,0:T(8,128)(2,1)S(1)} %copy-done), custom_call_target="tpu_custom_call" | custom-call | bytes 4096 | tf_op jit(solution)/shard_map/prepare/pallas_call | solution.py:109
  10.0 1.5 %collective-permute-done.even.refs_0_ = bf16[2,128,512]{2,1,0:T(8,128)(2,1)S(1)} collective-permute-done((bf16[2,128,512]{2,1,0:T(8,128)(2,1)}, bf16[2,128,512]{2,1,0:T(8,128)(2,1)S(1)}, u32[]{:S(2)}, u32[]{:S(2)}) %collective-permute-start) | collective-permute-done | bytes 262176 | tf_op jit(solution)/shard_map/ppermute | solution.py:15
  11.6 0.0 collective-permute-done.2.odd.refs_2_
  11.6 0.0 collective-permute-start.5
  11.6 1.5 %collective-permute-start.3 = (bf16[2,128,512]{2,1,0:T(8,128)(2,1)S(1)}, bf16[2,128,512]{2,1,0:T(8,128)(2,1)S(1)}, u32[]{:S(2)}, u32[]{:S(2)}) collective-permute-start(bf16[2,128,512]{2,1,0:T(8,128)(2,1)S(1)} %choose.1), channel_id=1, source_target_pairs={{0,2},{1,5},{2,0},{3,7},{4,6},{5,9},{6,4},{7,11},{8,10},{9,13},{10... | collective-permute-start | bytes 786440 | tf_op jit(solution)/shard_map/ppermute | solution.py:15
  13.1 0.0 collective-permute-start.1
  13.1 0.0 collective-permute-done.4.refs_1_
  13.1 0.0 collective-permute-done.5.refs_3_
  13.2 0.0 copy-done.1
  13.2 0.0 copy-done.2
  13.2 0.0 copy-done.4
  13.2 0.0 copy-done.5
  13.2 3.0 %later_stop.1 = (bf16[512,256]{1,0:T(8,128)(2,1)S(1)}, bf16[512,1024]{1,0:T(8,128)(2,1)S(1)}) custom-call(s32[3,4]{1,0:T(4,128)S(1)} %copy-done.4, bf16[2,128,512]{2,1,0:T(8,128)(2,1)S(1)} %copy-done.2, bf16[2,128,512]{2,1,0:T(8,128)(2,1)S(1)} %collective-permute-done.4.refs_1_, bf16[2,128,512]{2,1,0:T(8,128)(2,1)S(1)} %collective-permute-done.2.odd.refs_2_, ...), custom_call_target="tpu_custom_call" | custom-call | bytes 4096 | tf_op jit(solution)/shard_map/later_stop/pallas_call | solution.py:109
  16.2 2.6 %collective-permute-start.8 = (bf16[512,256]{1,0:T(8,128)(2,1)S(1)}, bf16[512,256]{1,0:T(8,128)(2,1)S(1)}, u32[]{:S(2)}, u32[]{:S(2)}) collective-permute-start(bf16[512,256]{1,0:T(8,128)(2,1)S(1)} %get-tuple-element.16), channel_id=1, source_target_pairs={{0,12},{1,13},{2,14},{3,15},{4,0},{5,1},{6,2},{7,3},{8,4},{9,5},{1... | collective-permute-start | bytes 786440 | tf_op jit(solution)/shard_map/ppermute | solution.py:15
  18.8 0.0 collective-permute-done.3.block.refs_2_
  18.8 0.4 %collective-permute-start.6 = (bf16[128,512]{1,0:T(8,128)(2,1)S(1)}, bf16[128,512]{1,0:T(8,128)(2,1)S(1)}, u32[]{:S(2)}, u32[]{:S(2)}) collective-permute-start(bf16[128,512]{1,0:T(8,128)(2,1)S(1)} %get-tuple-element.18), channel_id=1, source_target_pairs={{0,1},{1,0},{2,3},{3,2},{4,5},{5,4},{6,7},{7,6},{8,9},{9,8},{10,11... | collective-permute-start | bytes 393224 | tf_op jit(solution)/shard_map/ppermute | solution.py:15
  19.3 0.1 collective-permute-start.7
  19.4 2.5 %own_stop.1.refs_8_ = f32[512,256]{1,0:T(8,128)S(1)} custom-call(s32[3,4]{1,0:T(4,128)S(1)} %copy-done.4, bf16[512,1024]{1,0:T(8,128)(2,1)S(1)} %get-tuple-element.21.refs_0_, f32[3,4]{1,0:T(4,128)S(1)} %copy-done.5, bf16[4,512,256]{2,1,0:T(8,128)(2,1)S(1)} %get-tuple-element.22.refs_2_, bf16[8,2,512,512]{3,2,1,0:T(8,128)(2,1)S(1)} %copy-done.1), custom_call_target="tpu_custom_call" | custom-call | bytes 4096 | tf_op jit(solution)/shard_map/own_stop/pallas_call | solution.py:109
  22.0 0.0 collective-permute-done.1.refs_1_
  22.0 0.0 collective-permute-done.6.refs_3_
  22.0 0.0 collective-permute-done.7.refs_4_
  22.0 3.0 %earlier_stop.1.total = f32[512,256]{1,0:T(8,128)S(1)} custom-call(s32[3,4]{1,0:T(4,128)S(1)} %copy-done.4, bf16[2,128,512]{2,1,0:T(8,128)(2,1)S(1)} %collective-permute-done.even.refs_0_, bf16[2,128,512]{2,1,0:T(8,128)(2,1)S(1)} %collective-permute-done.1.refs_1_, bf16[2,128,512]{2,1,0:T(8,128)(2,1)S(1)} %collective-permute-done.3.block.refs_2_, ...), custom_call_target="tpu_custom_call" | custom-call | bytes 4096 | tf_op jit(solution)/shard_map/earlier_stop/pallas_call | solution.py:109
  25.0 0.0 collective-permute-done.8.arrived
  25.0 1.0 %finish.1 = f32[2,128,512]{2,1,0:T(8,128)} custom-call(f32[512,256]{1,0:T(8,128)S(1)} %earlier_stop.1.total, bf16[512,256]{1,0:T(8,128)(2,1)S(1)} %collective-permute-done.8.arrived), custom_call_target="tpu_custom_call" | custom-call | bytes 4096 | tf_op jit(solution)/shard_map/finish/pallas_call | solution.py:130
  (2 shorter events, 0.0 us)
Async XLA Ops:
  0.0 11.6 %collective-permute-start = (bf16[2,128,512]{2,1,0:T(8,128)(2,1)}, bf16[2,128,512]{2,1,0:T(8,128)(2,1)S(1)}, u32[]{:S(2)}, u32[]{:S(2)}) collective-permute-start(bf16[2,128,512]{2,1,0:T(8,128)(2,1)} %refs_0_.3), channel_id=1, source_target_pairs={{0,4},{1,5},{2,6},{3,7},{4,8},{5,9},{6,10},{7,11},{8,12},{9,13},{1... | collective-permute-start | bytes 786440 | tf_op jit(solution)/shard_map/ppermute | solution.py:15
  3.0 8.5 %collective-permute-start.2 = (bf16[2,128,512]{2,1,0:T(8,128)(2,1)}, bf16[2,128,512]{2,1,0:T(8,128)(2,1)S(1)}, u32[]{:S(2)}, u32[]{:S(2)}) collective-permute-start(bf16[2,128,512]{2,1,0:T(8,128)(2,1)} %refs_0_.3), channel_id=1, source_target_pairs={{0,2},{1,3},{2,0},{3,1},{4,6},{5,7},{6,4},{7,5},{8,10},{9,11},{10,... | collective-permute-start | bytes 786440 | tf_op jit(solution)/shard_map/ppermute | solution.py:15
  4.5 8.6 %collective-permute-start.4 = (bf16[2,128,512]{2,1,0:T(8,128)(2,1)}, bf16[2,128,512]{2,1,0:T(8,128)(2,1)S(1)}, u32[]{:S(2)}, u32[]{:S(2)}) collective-permute-start(bf16[2,128,512]{2,1,0:T(8,128)(2,1)} %refs_0_.3), channel_id=1, source_target_pairs={{0,1},{1,0},{2,3},{3,2},{4,5},{5,4},{6,7},{7,6},{8,9},{9,8},{10,11... | collective-permute-start | bytes 786440 | tf_op jit(solution)/shard_map/ppermute | solution.py:15
  4.5 3.4 %copy-start = (bf16[8,2,512,512]{3,2,1,0:T(8,128)(2,1)S(1)}, bf16[8,2,512,512]{3,2,1,0:T(8,128)(2,1)}, u32[]{:S(2)}) copy-start(bf16[8,2,512,512]{3,2,1,0:T(8,128)(2,1)} %refs_7_.1) | copy-start | bytes 25165828
  7.9 0.7 %copy-start.3 = (s32[3,4]{1,0:T(4,128)S(1)}, s32[3,4]{1,0:T(4,128)}, u32[]{:S(2)}) copy-start(s32[3,4]{1,0:T(4,128)} %listed.7) | copy-start | bytes 148
  8.6 4.6 %copy-start.1 = (bf16[8,2,512,512]{3,2,1,0:T(8,128)(2,1)S(1)}, bf16[8,2,512,512]{3,2,1,0:T(8,128)(2,1)}, u32[]{:S(2)}) copy-start(bf16[8,2,512,512]{3,2,1,0:T(8,128)(2,1)} %refs_7_.1) | copy-start | bytes 25165828
  8.6 4.6 %copy-start.2 = (bf16[2,128,512]{2,1,0:T(8,128)(2,1)S(1)}, bf16[2,128,512]{2,1,0:T(8,128)(2,1)}, u32[]{:S(2)}) copy-start(bf16[2,128,512]{2,1,0:T(8,128)(2,1)} %refs_0_.3) | copy-start | bytes 786436
  8.6 4.6 %copy-start.4 = (s32[3,4]{1,0:T(4,128)S(1)}, s32[3,4]{1,0:T(4,128)}, u32[]{:S(2)}) copy-start(s32[3,4]{1,0:T(4,128)} %listed.7) | copy-start | bytes 148
  8.6 4.6 %copy-start.5 = (f32[3,4]{1,0:T(4,128)S(1)}, f32[3,4]{1,0:T(4,128)}, u32[]{:S(2)}) copy-start(f32[3,4]{1,0:T(4,128)} %refs_5_.1) | copy-start | bytes 148
  11.6 1.6 %collective-permute-start.5 = (bf16[2,128,512]{2,1,0:T(8,128)(2,1)S(1)}, bf16[2,128,512]{2,1,0:T(8,128)(2,1)S(1)}, u32[]{:S(2)}, u32[]{:S(2)}) collective-permute-start(bf16[2,128,512]{2,1,0:T(8,128)(2,1)S(1)} %collective-permute-done.2.odd.refs_2_), channel_id=1, source_target_pairs={{0,1},{1,0},{2,3},{3,2},{4,5},{5,4},{6,7},{7,6},{8,9},{9,8},{10,11... | collective-permute-start | bytes 786440 | tf_op jit(solution)/shard_map/ppermute | solution.py:15
  11.6 7.2 %collective-permute-start.3 = (bf16[2,128,512]{2,1,0:T(8,128)(2,1)S(1)}, bf16[2,128,512]{2,1,0:T(8,128)(2,1)S(1)}, u32[]{:S(2)}, u32[]{:S(2)}) collective-permute-start(bf16[2,128,512]{2,1,0:T(8,128)(2,1)S(1)} %choose.1), channel_id=1, source_target_pairs={{0,2},{1,5},{2,0},{3,7},{4,6},{5,9},{6,4},{7,11},{8,10},{9,13},{10... | collective-permute-start | bytes 786440 | tf_op jit(solution)/shard_map/ppermute | solution.py:15
  13.1 8.8 %collective-permute-start.1 = (bf16[2,128,512]{2,1,0:T(8,128)(2,1)S(1)}, bf16[2,128,512]{2,1,0:T(8,128)(2,1)S(1)}, u32[]{:S(2)}, u32[]{:S(2)}) collective-permute-start(bf16[2,128,512]{2,1,0:T(8,128)(2,1)S(1)} %collective-permute-done.even.refs_0_), channel_id=1, source_target_pairs={{0,1},{1,0},{2,3},{3,2},{4,5},{5,4},{6,7},{7,6},{8,9},{9,8},{10,11... | collective-permute-start | bytes 786440 | tf_op jit(solution)/shard_map/ppermute | solution.py:15
  16.2 8.8 %collective-permute-start.8 = (bf16[512,256]{1,0:T(8,128)(2,1)S(1)}, bf16[512,256]{1,0:T(8,128)(2,1)S(1)}, u32[]{:S(2)}, u32[]{:S(2)}) collective-permute-start(bf16[512,256]{1,0:T(8,128)(2,1)S(1)} %get-tuple-element.16), channel_id=1, source_target_pairs={{0,12},{1,13},{2,14},{3,15},{4,0},{5,1},{6,2},{7,3},{8,4},{9,5},{1... | collective-permute-start | bytes 786440 | tf_op jit(solution)/shard_map/ppermute | solution.py:15
  18.8 3.1 %collective-permute-start.6 = (bf16[128,512]{1,0:T(8,128)(2,1)S(1)}, bf16[128,512]{1,0:T(8,128)(2,1)S(1)}, u32[]{:S(2)}, u32[]{:S(2)}) collective-permute-start(bf16[128,512]{1,0:T(8,128)(2,1)S(1)} %get-tuple-element.18), channel_id=1, source_target_pairs={{0,1},{1,0},{2,3},{3,2},{4,5},{5,4},{6,7},{7,6},{8,9},{9,8},{10,11... | collective-permute-start | bytes 393224 | tf_op jit(solution)/shard_map/ppermute | solution.py:15
  19.3 2.7 %collective-permute-start.7 = (bf16[128,512]{1,0:T(8,128)(2,1)S(1)}, bf16[128,512]{1,0:T(8,128)(2,1)S(1)}, u32[]{:S(2)}, u32[]{:S(2)}) collective-permute-start(bf16[128,512]{1,0:T(8,128)(2,1)S(1)} %get-tuple-element.19), channel_id=1, source_target_pairs={{0,1},{1,0},{2,3},{3,2},{4,5},{5,4},{6,7},{7,6},{8,9},{9,8},{10,11... | collective-permute-start | bytes 393224 | tf_op jit(solution)/shard_map/ppermute | solution.py:15

commit v5 on v4

--- a/solution.py
+++ b/solution.py
@@ -63,6 +63,40 @@
             imag = reals[i][:, spots[j]].astype(F32) - reals[j][:, spots[i]].T.astype(F32)
             spectral[spots[i], spots[j]] = real.astype(BF16)
             spectral[spots[i], imag_spots[j]] = imag.astype(BF16)
+
+
+def triangle(tile):
+    row = lax.broadcasted_iota(jnp.int32, (tile, tile), 0)
+    column = lax.broadcasted_iota(jnp.int32, (tile, tile), 1)
+    return row <= column
+
+
+def packed(total, group, leaving, whole):
+    tile = total.shape[1] // 2
+    whole[...] = total
+    for offset in range(1, group):
+        spot = slice((offset - 1) * tile, offset * tile)
+        leaving[spot] = whole[pl.ds(own_row(offset, group, tile), tile), :].astype(BF16)
+    own = whole[pl.ds(own_row(0, group, tile), tile), :]
+    both = jnp.where(triangle(tile), own[:, :tile], own[:, tile:])
+    half = tile // 2
+    leaving[(group - 1) * tile :] = beside(both[:half], both[half:]).astype(BF16)
+
+
+def add_packed(whole, arrived, group):
+    tile = whole.shape[1] // 2
+    for offset in range(1, group):
+        spot = pl.ds(own_row(offset, group, tile), tile)
+        whole[spot, :] += arrived[(offset - 1) * tile : offset * tile].astype(F32)
+    both = arrived[(group - 1) * tile :].astype(F32)
+    both = jnp.concatenate([both[:, :tile], both[:, tile:]], axis=0)
+    turned = both.T
+    upper = triangle(tile)
+    row = lax.broadcasted_iota(jnp.int32, (tile, tile), 0)
+    column = lax.broadcasted_iota(jnp.int32, (tile, tile), 1)
+    real = jnp.where(upper, both, turned)
+    imag = jnp.where(row > column, both, jnp.where(row < column, -turned, 0.0))
+    whole[pl.ds(own_row(0, group, tile), tile), :] += beside(real, imag)
 
 
 def stop_term(stop, weights, spectral, turned, couplings, chosen, listing, start):
@@ -159,17 +193,17 @@
     next_far = moved(leaves, "mom", lambda i: (i + group) % count if i % 2 else i ^ 1 << top)
 
     def later(listing, chosen, *refs):
-        *blocks, weights, turned, couplings, leaving, spectral = refs
+        *blocks, weights, turned, couplings, leaving, spectral, whole = refs
         fill_spectral(blocks, spectral)
-        leaving[...] = stop_term(
-            0, weights, spectral, turned, couplings, chosen, listing, None
-        ).astype(BF16)
+        total = stop_term(0, weights, spectral, turned, couplings, chosen, listing, None)
+        packed(total, group, leaving, whole)
 
     leaving, spectral = kernel(
         "later_stop",
         later,
         [phonon_modes, *own_blocks, weights, turned[0], couplings],
-        [(term_shape, BF16), (spectral_shape, BF16)],
+        [((slab - tile // 2, width), BF16), (spectral_shape, BF16)],
+        [pltpu.VMEM(term_shape, F32)],
     )
     arrived = passed_along(leaving, "mom", -group)
 
@@ -202,13 +236,31 @@
         [pltpu.VMEM(spectral_shape, BF16)],
     )
 
-    def finish(total, arrived, out):
-        whole = total[...] + arrived[...].astype(F32)
-        out[0] = whole[:, :tile].T
-        out[1] = -whole[:, tile:].T
-
-    (rows,) = quick("finish", finish, [total, arrived], [((2, tile, slab), F32)])
-    return rows
+    def finish(total, arrived, out, whole, rows, sems):
+        whole[...] = total[...]
+        add_packed(whole, arrived, group)
+        copies = [pltpu.make_async_copy(rows.at[half], out.at[half], sems.at[half]) for half in range(2)]
+        rows[0] = whole[:, :tile].T
+        copies[0].start()
+        rows[1] = -whole[:, tile:].T
+        copies[1].start()
+        for copy in copies:
+            copy.wait()
+
+    return pl.pallas_call(
+        finish,
+        in_specs=[VMEM] * 2,
+        out_specs=ANY,
+        out_shape=jax.ShapeDtypeStruct((2, tile, slab), F32),
+        scratch_shapes=[
+            pltpu.VMEM(term_shape, F32),
+            pltpu.VMEM((2, tile, slab), F32),
+            pltpu.SemaphoreType.DMA((2,)),
+        ],
+        compiler_params=pltpu.CompilerParams(vmem_limit_bytes=6 << 20),
+        cost_estimate=pl.CostEstimate(flops=0, transcendentals=0, bytes_accessed=4096),
+        name="finish",
+    )(total, arrived)
 
 
 def solution(mesh):

time: 26.2 us -> 26.3 us (level)
    pallas_call x0 -> x1, Pallas kernels: none -> 1.05 us  [body(): pl.pallas_call(finish, in_specs=[VMEM] * 2, out_specs=ANY, out_shape=jax....]
    pallas_call x3 -> x2, Pallas kernels: 1.05 us -> 0.04 us  [quick(): pl.pallas_call(function, in_specs=[VMEM] * len(args), out_specs=[VMEM] *...]
where the time goes in v5:
time: 26.3 us; the launch traced here: 26.1 us
  Pallas kernels  11.1 us (42%)
  starting transfers between devices  9.24 us (35%)
  local copies, waits for them, and re-layouts  4.08 us (16%)
  waiting for transfers between devices  1.54 us (6%)
    pallas_call x4, Pallas kernels, kernel(): pl.pallas_call(started, in_specs=[ANY] + [VMEM] * (len(args) - 1), out_sp...  10 us
    ppermute x9, starting transfers between devices, moved(): lax.ppermute(block, axis, [(i, route(i)) for i in range(lax.axis_size(axi...  9.24 us
    unnamed x12, local copies, waits for them, and re-layouts  4.08 us
    ppermute x9, waiting for transfers between devices, moved(): lax.ppermute(block, axis, [(i, route(i)) for i in range(lax.axis_size(axi...  1.54 us
    pallas_call x1, Pallas kernels, body(): pl.pallas_call(finish, in_specs=[VMEM] * 2, out_specs=ANY, out_shape=jax....  1.05 us
  transfers between devices with their start and end apart: 9, of which 1 were waited for; matrix products, arithmetic and copies ran while one was open for 0% of the time, Pallas kernels for 39%

profile of v5, /device:TPU:0, one launch (start us, length us, event | category | flops | bytes accessed | tf_op | source)
XLA Modules:
  0.0 26.1 jit_solution(9859622216066238922)
XLA Ops:
  0.0 3.0 %collective-permute-start = (bf16[2,128,512]{2,1,0:T(8,128)(2,1)}, bf16[2,128,512]{2,1,0:T(8,128)(2,1)S(1)}, u32[]{:S(2)}, u32[]{:S(2)}) collective-permute-start(bf16[2,128,512]{2,1,0:T(8,128)(2,1)} %refs_0_.3), channel_id=1, source_target_pairs={{0,4},{1,5},{2,6},{3,7},{4,8},{5,9},{6,10},{7,11},{8,12},{9,13},{1... | collective-permute-start | bytes 786440 | tf_op jit(solution)/shard_map/ppermute | solution.py:15
  3.0 1.5 %collective-permute-start.2 = (bf16[2,128,512]{2,1,0:T(8,128)(2,1)}, bf16[2,128,512]{2,1,0:T(8,128)(2,1)S(1)}, u32[]{:S(2)}, u32[]{:S(2)}) collective-permute-start(bf16[2,128,512]{2,1,0:T(8,128)(2,1)} %refs_0_.3), channel_id=1, source_target_pairs={{0,2},{1,3},{2,0},{3,1},{4,6},{5,7},{6,4},{7,5},{8,10},{9,11},{10,... | collective-permute-start | bytes 786440 | tf_op jit(solution)/shard_map/ppermute | solution.py:15
  4.5 0.0 collective-permute-start.4
  4.5 0.0 copy-start
  4.5 3.4 %copy-done = bf16[8,2,512,512]{3,2,1,0:T(8,128)(2,1)S(1)} copy-done((bf16[8,2,512,512]{3,2,1,0:T(8,128)(2,1)S(1)}, bf16[8,2,512,512]{3,2,1,0:T(8,128)(2,1)}, u32[]{:S(2)}) %copy-start) | copy-done | bytes 8388632
  7.9 0.0 copy-start.3
  7.9 0.7 %copy-done.3 = s32[3,4]{1,0:T(4,128)S(1)} copy-done((s32[3,4]{1,0:T(4,128)S(1)}, s32[3,4]{1,0:T(4,128)}, u32[]{:S(2)}) %copy-start.3) | copy-done | bytes 72
  8.6 0.0 copy-start.1
  8.6 0.0 copy-start.2
  8.6 0.0 copy-start.4
  8.6 0.0 copy-start.5
  8.6 1.4 %prepare.1 = (bf16[4,512,256]{2,1,0:T(8,128)(2,1)S(1)}, bf16[4,512,256]{2,1,0:T(8,128)(2,1)S(1)}, bf16[4,512,256]{2,1,0:T(8,128)(2,1)S(1)}) custom-call(s32[3,4]{1,0:T(4,128)S(1)} %copy-done.3, bf16[8,2,512,512]{3,2,1,0:T(8,128)(2,1)S(1)} %copy-done), custom_call_target="tpu_custom_call" | custom-call | bytes 4096 | tf_op jit(solution)/shard_map/prepare/pallas_call | solution.py:143
  10.0 1.5 %collective-permute-done.even.refs_0_ = bf16[2,128,512]{2,1,0:T(8,128)(2,1)S(1)} collective-permute-done((bf16[2,128,512]{2,1,0:T(8,128)(2,1)}, bf16[2,128,512]{2,1,0:T(8,128)(2,1)S(1)}, u32[]{:S(2)}, u32[]{:S(2)}) %collective-permute-start) | collective-permute-done | bytes 262176 | tf_op jit(solution)/shard_map/ppermute | solution.py:15
  11.6 0.0 collective-permute-done.2.odd.refs_2_
  11.6 0.0 collective-permute-start.5
  11.6 1.5 %collective-permute-start.3 = (bf16[2,128,512]{2,1,0:T(8,128)(2,1)S(1)}, bf16[2,128,512]{2,1,0:T(8,128)(2,1)S(1)}, u32[]{:S(2)}, u32[]{:S(2)}) collective-permute-start(bf16[2,128,512]{2,1,0:T(8,128)(2,1)S(1)} %choose.1), channel_id=1, source_target_pairs={{0,2},{1,5},{2,0},{3,7},{4,6},{5,9},{6,4},{7,11},{8,10},{9,13},{10... | collective-permute-start | bytes 786440 | tf_op jit(solution)/shard_map/ppermute | solution.py:15
  13.1 0.0 collective-permute-start.1
  13.1 0.0 collective-permute-done.4.refs_1_
  13.1 0.0 collective-permute-done.5.refs_3_
  13.2 0.0 copy-done.1
  13.2 0.0 copy-done.2
  13.2 0.0 copy-done.4
  13.2 0.0 copy-done.5
  13.2 3.0 %later_stop.1 = (bf16[448,256]{1,0:T(8,128)(2,1)S(1)}, bf16[512,1024]{1,0:T(8,128)(2,1)S(1)}) custom-call(s32[3,4]{1,0:T(4,128)S(1)} %copy-done.4, bf16[2,128,512]{2,1,0:T(8,128)(2,1)S(1)} %copy-done.2, bf16[2,128,512]{2,1,0:T(8,128)(2,1)S(1)} %collective-permute-done.4.refs_1_, bf16[2,128,512]{2,1,0:T(8,128)(2,1)S(1)} %collective-permute-done.2.odd.refs_2_, ...), custom_call_target="tpu_custom_call" | custom-call | bytes 4096 | tf_op jit(solution)/shard_map/later_stop/pallas_call | solution.py:143
  16.2 2.6 %collective-permute-start.8 = (bf16[448,256]{1,0:T(8,128)(2,1)S(1)}, bf16[448,256]{1,0:T(8,128)(2,1)S(1)}, u32[]{:S(2)}, u32[]{:S(2)}) collective-permute-start(bf16[448,256]{1,0:T(8,128)(2,1)S(1)} %get-tuple-element.16), channel_id=1, source_target_pairs={{0,12},{1,13},{2,14},{3,15},{4,0},{5,1},{6,2},{7,3},{8,4},{9,5},{1... | collective-permute-start | bytes 688136 | tf_op jit(solution)/shard_map/ppermute | solution.py:15
  18.8 0.0 collective-permute-done.3.block.refs_2_
  18.9 0.4 %collective-permute-start.6 = (bf16[128,512]{1,0:T(8,128)(2,1)S(1)}, bf16[128,512]{1,0:T(8,128)(2,1)S(1)}, u32[]{:S(2)}, u32[]{:S(2)}) collective-permute-start(bf16[128,512]{1,0:T(8,128)(2,1)S(1)} %get-tuple-element.18), channel_id=1, source_target_pairs={{0,1},{1,0},{2,3},{3,2},{4,5},{5,4},{6,7},{7,6},{8,9},{9,8},{10,11... | collective-permute-start | bytes 393224 | tf_op jit(solution)/shard_map/ppermute | solution.py:15
  19.3 0.2 collective-permute-start.7
  19.4 2.5 %own_stop.1.refs_8_ = f32[512,256]{1,0:T(8,128)S(1)} custom-call(s32[3,4]{1,0:T(4,128)S(1)} %copy-done.4, bf16[512,1024]{1,0:T(8,128)(2,1)S(1)} %get-tuple-element.21.refs_0_, f32[3,4]{1,0:T(4,128)S(1)} %copy-done.5, bf16[4,512,256]{2,1,0:T(8,128)(2,1)S(1)} %get-tuple-element.22.refs_2_, bf16[8,2,512,512]{3,2,1,0:T(8,128)(2,1)S(1)} %copy-done.1), custom_call_target="tpu_custom_call" | custom-call | bytes 4096 | tf_op jit(solution)/shard_map/own_stop/pallas_call | solution.py:143
  22.0 0.0 collective-permute-done.1.refs_1_
  22.0 0.0 collective-permute-done.6.refs_3_
  22.0 0.0 collective-permute-done.7.refs_4_
  22.0 3.0 %earlier_stop.1.total = f32[512,256]{1,0:T(8,128)S(1)} custom-call(s32[3,4]{1,0:T(4,128)S(1)} %copy-done.4, bf16[2,128,512]{2,1,0:T(8,128)(2,1)S(1)} %collective-permute-done.even.refs_0_, bf16[2,128,512]{2,1,0:T(8,128)(2,1)S(1)} %collective-permute-done.1.refs_1_, bf16[2,128,512]{2,1,0:T(8,128)(2,1)S(1)} %collective-permute-done.3.block.refs_2_, ...), custom_call_target="tpu_custom_call" | custom-call | bytes 4096 | tf_op jit(solution)/shard_map/earlier_stop/pallas_call | solution.py:143
  25.0 0.0 collective-permute-done.8.arrived
  25.0 1.0 %finish.1 = f32[2,128,512]{2,1,0:T(8,128)} custom-call(f32[512,256]{1,0:T(8,128)S(1)} %earlier_stop.1.total, bf16[448,256]{1,0:T(8,128)(2,1)S(1)} %collective-permute-done.8.arrived), custom_call_target="tpu_custom_call" | custom-call | bytes 4096 | tf_op jit(solution)/shard_map/finish/pallas_call | solution.py:250
  (2 shorter events, 0.0 us)
Async XLA Ops:
  0.0 11.6 %collective-permute-start = (bf16[2,128,512]{2,1,0:T(8,128)(2,1)}, bf16[2,128,512]{2,1,0:T(8,128)(2,1)S(1)}, u32[]{:S(2)}, u32[]{:S(2)}) collective-permute-start(bf16[2,128,512]{2,1,0:T(8,128)(2,1)} %refs_0_.3), channel_id=1, source_target_pairs={{0,4},{1,5},{2,6},{3,7},{4,8},{5,9},{6,10},{7,11},{8,12},{9,13},{1... | collective-permute-start | bytes 786440 | tf_op jit(solution)/shard_map/ppermute | solution.py:15
  3.0 8.5 %collective-permute-start.2 = (bf16[2,128,512]{2,1,0:T(8,128)(2,1)}, bf16[2,128,512]{2,1,0:T(8,128)(2,1)S(1)}, u32[]{:S(2)}, u32[]{:S(2)}) collective-permute-start(bf16[2,128,512]{2,1,0:T(8,128)(2,1)} %refs_0_.3), channel_id=1, source_target_pairs={{0,2},{1,3},{2,0},{3,1},{4,6},{5,7},{6,4},{7,5},{8,10},{9,11},{10,... | collective-permute-start | bytes 786440 | tf_op jit(solution)/shard_map/ppermute | solution.py:15
  4.5 8.6 %collective-permute-start.4 = (bf16[2,128,512]{2,1,0:T(8,128)(2,1)}, bf16[2,128,512]{2,1,0:T(8,128)(2,1)S(1)}, u32[]{:S(2)}, u32[]{:S(2)}) collective-permute-start(bf16[2,128,512]{2,1,0:T(8,128)(2,1)} %refs_0_.3), channel_id=1, source_target_pairs={{0,1},{1,0},{2,3},{3,2},{4,5},{5,4},{6,7},{7,6},{8,9},{9,8},{10,11... | collective-permute-start | bytes 786440 | tf_op jit(solution)/shard_map/ppermute | solution.py:15
  4.5 3.4 %copy-start = (bf16[8,2,512,512]{3,2,1,0:T(8,128)(2,1)S(1)}, bf16[8,2,512,512]{3,2,1,0:T(8,128)(2,1)}, u32[]{:S(2)}) copy-start(bf16[8,2,512,512]{3,2,1,0:T(8,128)(2,1)} %refs_7_.1) | copy-start | bytes 25165828
  7.9 0.7 %copy-start.3 = (s32[3,4]{1,0:T(4,128)S(1)}, s32[3,4]{1,0:T(4,128)}, u32[]{:S(2)}) copy-start(s32[3,4]{1,0:T(4,128)} %listed.7) | copy-start | bytes 148
  8.6 4.6 %copy-start.1 = (bf16[8,2,512,512]{3,2,1,0:T(8,128)(2,1)S(1)}, bf16[8,2,512,512]{3,2,1,0:T(8,128)(2,1)}, u32[]{:S(2)}) copy-start(bf16[8,2,512,512]{3,2,1,0:T(8,128)(2,1)} %refs_7_.1) | copy-start | bytes 25165828
  8.6 4.6 %copy-start.2 = (bf16[2,128,512]{2,1,0:T(8,128)(2,1)S(1)}, bf16[2,128,512]{2,1,0:T(8,128)(2,1)}, u32[]{:S(2)}) copy-start(bf16[2,128,512]{2,1,0:T(8,128)(2,1)} %refs_0_.3) | copy-start | bytes 786436
  8.6 4.6 %copy-start.4 = (s32[3,4]{1,0:T(4,128)S(1)}, s32[3,4]{1,0:T(4,128)}, u32[]{:S(2)}) copy-start(s32[3,4]{1,0:T(4,128)} %listed.7) | copy-start | bytes 148
  8.6 4.6 %copy-start.5 = (f32[3,4]{1,0:T(4,128)S(1)}, f32[3,4]{1,0:T(4,128)}, u32[]{:S(2)}) copy-start(f32[3,4]{1,0:T(4,128)} %refs_5_.1) | copy-start | bytes 148
  11.6 1.6 %collective-permute-start.5 = (bf16[2,128,512]{2,1,0:T(8,128)(2,1)S(1)}, bf16[2,128,512]{2,1,0:T(8,128)(2,1)S(1)}, u32[]{:S(2)}, u32[]{:S(2)}) collective-permute-start(bf16[2,128,512]{2,1,0:T(8,128)(2,1)S(1)} %collective-permute-done.2.odd.refs_2_), channel_id=1, source_target_pairs={{0,1},{1,0},{2,3},{3,2},{4,5},{5,4},{6,7},{7,6},{8,9},{9,8},{10,11... | collective-permute-start | bytes 786440 | tf_op jit(solution)/shard_map/ppermute | solution.py:15
  11.6 7.2 %collective-permute-start.3 = (bf16[2,128,512]{2,1,0:T(8,128)(2,1)S(1)}, bf16[2,128,512]{2,1,0:T(8,128)(2,1)S(1)}, u32[]{:S(2)}, u32[]{:S(2)}) collective-permute-start(bf16[2,128,512]{2,1,0:T(8,128)(2,1)S(1)} %choose.1), channel_id=1, source_target_pairs={{0,2},{1,5},{2,0},{3,7},{4,6},{5,9},{6,4},{7,11},{8,10},{9,13},{10... | collective-permute-start | bytes 786440 | tf_op jit(solution)/shard_map/ppermute | solution.py:15
  13.1 8.8 %collective-permute-start.1 = (bf16[2,128,512]{2,1,0:T(8,128)(2,1)S(1)}, bf16[2,128,512]{2,1,0:T(8,128)(2,1)S(1)}, u32[]{:S(2)}, u32[]{:S(2)}) collective-permute-start(bf16[2,128,512]{2,1,0:T(8,128)(2,1)S(1)} %collective-permute-done.even.refs_0_), channel_id=1, source_target_pairs={{0,1},{1,0},{2,3},{3,2},{4,5},{5,4},{6,7},{7,6},{8,9},{9,8},{10,11... | collective-permute-start | bytes 786440 | tf_op jit(solution)/shard_map/ppermute | solution.py:15
  16.2 8.8 %collective-permute-start.8 = (bf16[448,256]{1,0:T(8,128)(2,1)S(1)}, bf16[448,256]{1,0:T(8,128)(2,1)S(1)}, u32[]{:S(2)}, u32[]{:S(2)}) collective-permute-start(bf16[448,256]{1,0:T(8,128)(2,1)S(1)} %get-tuple-element.16), channel_id=1, source_target_pairs={{0,12},{1,13},{2,14},{3,15},{4,0},{5,1},{6,2},{7,3},{8,4},{9,5},{1... | collective-permute-start | bytes 688136 | tf_op jit(solution)/shard_map/ppermute | solution.py:15
  18.9 3.1 %collective-permute-start.6 = (bf16[128,512]{1,0:T(8,128)(2,1)S(1)}, bf16[128,512]{1,0:T(8,128)(2,1)S(1)}, u32[]{:S(2)}, u32[]{:S(2)}) collective-permute-start(bf16[128,512]{1,0:T(8,128)(2,1)S(1)} %get-tuple-element.18), channel_id=1, source_target_pairs={{0,1},{1,0},{2,3},{3,2},{4,5},{5,4},{6,7},{7,6},{8,9},{9,8},{10,11... | collective-permute-start | bytes 393224 | tf_op jit(solution)/shard_map/ppermute | solution.py:15
  19.3 2.8 %collective-permute-start.7 = (bf16[128,512]{1,0:T(8,128)(2,1)S(1)}, bf16[128,512]{1,0:T(8,128)(2,1)S(1)}, u32[]{:S(2)}, u32[]{:S(2)}) collective-permute-start(bf16[128,512]{1,0:T(8,128)(2,1)S(1)} %get-tuple-element.19), channel_id=1, source_target_pairs={{0,1},{1,0},{2,3},{3,2},{4,5},{5,4},{6,7},{7,6},{8,9},{9,8},{10,11... | collective-permute-start | bytes 393224 | tf_op jit(solution)/shard_map/ppermute | solution.py:15

commit v6 on v5

--- a/solution.py
+++ b/solution.py
@@ -99,24 +99,23 @@
     whole[pl.ds(own_row(0, group, tile), tile), :] += beside(real, imag)
 
 
-def stop_term(stop, weights, spectral, turned, couplings, chosen, listing, start):
+def stop_term(stop, weights, spectral, turned, picked, start, modes=None):
     count, slab, width = turned.shape
     tile = width // 2
     rights = []
-    for mode in range(count):
+    modes = range(count) if modes is None else modes
+    for mode in modes:
         real, imag = turned[mode, :, :tile], turned[mode, :, tile:]
         rights.append(jnp.concatenate([beside(real, -imag), beside(imag, real)], axis=0))
     products = jnp.dot(
         spectral[...], jnp.concatenate(rights, axis=1), preferred_element_type=F32
     ).astype(BF16)
-    listing.wait()
     total = start
-    for mode in range(count):
-        product = products[:, mode * width : (mode + 1) * width]
+    for place, mode in enumerate(modes):
+        product = products[:, place * width : (place + 1) * width]
         real, imag = product[:, :tile], product[:, tile:]
         right = jnp.concatenate([product, beside(-imag, real)], axis=0)
-        index = chosen[stop, mode]
-        left = beside(couplings[index, 0], couplings[index, 1])
+        left = beside(picked[mode, 0], picked[mode, 1])
         term = weights[stop : stop + 1, mode : mode + 1] * jnp.dot(
             left, right, preferred_element_type=F32
         )
@@ -133,32 +132,39 @@
     term_shape = (slab, width)
     spectral_shape = (slab, 2 * slab)
 
-    def kernel(name, function, args, outs, scratch=()):
-        def started(listed, *refs):
-            *refs, chosen, sem = refs
-            listing = pltpu.make_async_copy(listed, chosen, sem)
-            listing.start()
-            function(listing, chosen, *refs)
-
+    def kernel(name, function, args, outs, scratch=(), leading=VMEM):
         return pl.pallas_call(
-            started,
-            in_specs=[ANY] + [VMEM] * (len(args) - 1),
+            function,
+            in_specs=[leading] + [VMEM] * (len(args) - 1),
             out_specs=[VMEM] * len(outs),
             out_shape=[jax.ShapeDtypeStruct(*out) for out in outs],
-            scratch_shapes=[*scratch, pltpu.SMEM((stops, modes), jnp.int32), pltpu.SemaphoreType.DMA],
+            scratch_shapes=list(scratch),
             compiler_params=pltpu.CompilerParams(vmem_limit_bytes=12 << 20),
             cost_estimate=pl.CostEstimate(flops=0, transcendentals=0, bytes_accessed=4096),
             name=name,
         )(*args)
 
-    def prepare(listing, chosen, couplings, *turned):
+    def prepare(listed, couplings, *refs):
+        picked, turned = refs[:stops], refs[stops : 2 * stops]
+        chosen, listed_sem, sems = refs[2 * stops :]
+        listing = pltpu.make_async_copy(listed, chosen, listed_sem)
+        listing.start()
         listing.wait()
+        copies = [
+            pltpu.make_async_copy(couplings.at[chosen[stop, mode]], picked[stop].at[mode], sems.at[stop, mode])
+            for stop in range(stops)
+            for mode in range(modes)
+        ]
+        for copy in copies:
+            copy.start()
         rows = pl.ds(own_row(0, group, tile), tile)
         for stop in range(stops):
             for mode in range(modes):
                 index = chosen[stop, mode]
                 turned[stop][mode, :, :tile] = couplings[index, 0, rows, :].T
                 turned[stop][mode, :, tile:] = couplings[index, 1, rows, :].T
+        for copy in copies:
+            copy.wait()
 
     def quick(name, function, args, outs):
         return pl.pallas_call(
@@ -184,54 +190,71 @@
 
     top = levels - 1
     incoming = passed_along(green_function, "mom", group)
-    turned = kernel("prepare", prepare, [phonon_modes, couplings], [((modes, slab, width), BF16)] * stops)
+    prepared = kernel(
+        "prepare",
+        prepare,
+        [phonon_modes, couplings],
+        [((modes, 2, slab, slab), BF16)] * stops + [((modes, slab, width), BF16)] * stops,
+        [
+            pltpu.SMEM((stops, modes), jnp.int32),
+            pltpu.SemaphoreType.DMA,
+            pltpu.SemaphoreType.DMA((stops, modes)),
+        ],
+        ANY,
+    )
+    picked, turned = prepared[:stops], prepared[stops:]
     far = partner(green_function, "mom", top)
-    ready = after(far, turned[0], incoming)
+    ready = after(far, turned[0])
     own_blocks = spread({0: green_function, 1 << top: ready}, top)
     (leaves,) = quick("choose", choose, [incoming, ready], [(green_function.shape, BF16)])
     count = lax.axis_size("mom")
     next_far = moved(leaves, "mom", lambda i: (i + group) % count if i % 2 else i ^ 1 << top)
 
-    def later(listing, chosen, *refs):
-        *blocks, weights, turned, couplings, leaving, spectral, whole = refs
+    def later(*refs):
+        *blocks, weights, turned, picked, leaving, spectral, whole = refs
         fill_spectral(blocks, spectral)
-        total = stop_term(0, weights, spectral, turned, couplings, chosen, listing, None)
+        total = stop_term(0, weights, spectral, turned, picked, None)
         packed(total, group, leaving, whole)
 
     leaving, spectral = kernel(
         "later_stop",
         later,
-        [phonon_modes, *own_blocks, weights, turned[0], couplings],
+        [*own_blocks, weights, turned[0], picked[0]],
         [((slab - tile // 2, width), BF16), (spectral_shape, BF16)],
         [pltpu.VMEM(term_shape, F32)],
     )
     arrived = passed_along(leaving, "mom", -group)
 
-    def own(listing, chosen, spectral, weights, turned, couplings, out):
-        out[...] = stop_term(1, weights, spectral, turned, couplings, chosen, listing, None)
-
-    (total,) = kernel(
-        "own_stop", own, [phonon_modes, spectral, weights, turned[1], couplings], [(term_shape, F32)]
-    )
+    def own(spectral, weights, turned, picked, out):
+        out[...] = stop_term(1, weights, spectral, turned, picked, None, range(modes // 2))
+
+    def own_rest(spectral, weights, turned, picked, before, out):
+        rest = range(modes // 2, modes)
+        out[...] = stop_term(1, weights, spectral, turned, picked, before[...], rest)
+
+    own_args = [spectral, weights, turned[1], picked[1]]
+    (begun,) = kernel("own_stop", own, own_args, [(term_shape, F32)])
 
     def split(block, real, imag):
         real[...] = block[0]
         imag[...] = block[1]
 
-    real, imag = quick("split", split, [after(next_far, leaving)], [((tile, slab), BF16)] * 2)
+    real, imag = quick("split", split, [after(next_far, begun)], [((tile, slab), BF16)] * 2)
+    own_args[0] = after(spectral, real)
+    (total,) = kernel("own_rest", own_rest, [*own_args, begun], [(term_shape, F32)])
     next_blocks = spread({0: incoming, 1 << top: (next_far, real, imag)}, top)
 
-    def earlier(listing, chosen, *refs):
-        *parts, weights, turned, couplings, before, out, spectral = refs
+    def earlier(*refs):
+        *parts, weights, turned, picked, before, out, spectral = refs
         parts = iter(parts)
         blocks = [(next(parts), next(parts)) if isinstance(b, tuple) else next(parts) for b in next_blocks]
         fill_spectral(blocks, spectral)
-        out[...] = stop_term(2, weights, spectral, turned, couplings, chosen, listing, before[...])
+        out[...] = stop_term(2, weights, spectral, turned, picked, before[...])
 
     (total,) = kernel(
         "earlier_stop",
         earlier,
-        [phonon_modes, *jax.tree.leaves(next_blocks), weights, turned[2], couplings, total],
+        [*jax.tree.leaves(next_blocks), weights, turned[2], picked[2], total],
         [(term_shape, F32)],
         [pltpu.VMEM(spectral_shape, BF16)],
     )

time: 26.3 us -> 25.6 us (0.973)
  starting transfers between devices: 9.24 us -> 8.15 us
  Pallas kernels: 11.1 us -> 11.9 us
  waiting for transfers between devices: 1.54 us -> 1.23 us
    ppermute x9, starting transfers between devices: 9.24 us -> 8.15 us  [moved(): lax.ppermute(block, axis, [(i, route(i)) for i in range(lax.axis_size(axi...]
    pallas_call x4 -> x5, Pallas kernels: 10 us -> 10.8 us  [kernel(): pl.pallas_call(function, in_specs=[leading] + [VMEM] * (len(args) - 1), o...]
    ppermute x9, waiting for transfers between devices: 1.54 us -> 1.23 us  [moved(): lax.ppermute(block, axis, [(i, route(i)) for i in range(lax.axis_size(axi...]
    unnamed x12 -> x8, local copies, waits for them, and re-layouts: 4.08 us -> 4.07 us
  transfers between devices with their start and end apart: 9 -> 9, of which waited for: 1 -> 1; matrix products, arithmetic and copies ran while one was open for 0% -> 0% of each run, Pallas kernels for 39% -> 43%
where the time goes in v6:
time: 25.6 us; the launch traced here: 25.5 us
  Pallas kernels  11.9 us (46%)
  starting transfers between devices  8.15 us (32%)
  local copies, waits for them, and re-layouts  4.07 us (16%)
  waiting for transfers between devices  1.23 us (5%)
    pallas_call x5, Pallas kernels, kernel(): pl.pallas_call(function, in_specs=[leading] + [VMEM] * (len(args) - 1), o...  10.8 us
    ppermute x9, starting transfers between devices, moved(): lax.ppermute(block, axis, [(i, route(i)) for i in range(lax.axis_size(axi...  8.15 us
    unnamed x8, local copies, waits for them, and re-layouts  4.07 us
    ppermute x9, waiting for transfers between devices, moved(): lax.ppermute(block, axis, [(i, route(i)) for i in range(lax.axis_size(axi...  1.23 us
    pallas_call x1, Pallas kernels, body(): pl.pallas_call(finish, in_specs=[VMEM] * 2, out_specs=ANY, out_shape=jax....  1.05 us
  transfers between devices with their start and end apart: 9, of which 1 were waited for; matrix products, arithmetic and copies ran while one was open for 0% of the time, Pallas kernels for 43%

profile of v6, /device:TPU:0, one launch (start us, length us, event | category | flops | bytes accessed | tf_op | source)
XLA Modules:
  0.0 25.5 jit_solution(7961011665220668055)
XLA Ops:
  0.0 2.9 %collective-permute-start.2 = (bf16[2,128,512]{2,1,0:T(8,128)(2,1)}, bf16[2,128,512]{2,1,0:T(8,128)(2,1)S(1)}, u32[]{:S(2)}, u32[]{:S(2)}) collective-permute-start(bf16[2,128,512]{2,1,0:T(8,128)(2,1)} %refs_0_.1), channel_id=1, source_target_pairs={{0,2},{1,3},{2,0},{3,1},{4,6},{5,7},{6,4},{7,5},{8,10},{9,11},{10,... | collective-permute-start | bytes 786440 | tf_op jit(solution)/shard_map/ppermute | solution.py:15
  2.9 1.6 %collective-permute-start = (bf16[2,128,512]{2,1,0:T(8,128)(2,1)}, bf16[2,128,512]{2,1,0:T(8,128)(2,1)S(1)}, u32[]{:S(2)}, u32[]{:S(2)}) collective-permute-start(bf16[2,128,512]{2,1,0:T(8,128)(2,1)} %refs_0_.1), channel_id=1, source_target_pairs={{0,4},{1,5},{2,6},{3,7},{4,8},{5,9},{6,10},{7,11},{8,12},{9,13},{1... | collective-permute-start | bytes 786440 | tf_op jit(solution)/shard_map/ppermute | solution.py:15
  4.5 0.0 collective-permute-start.4
  4.5 0.0 copy-start
  4.5 3.4 %copy-done = bf16[8,2,512,512]{3,2,1,0:T(8,128)(2,1)S(1)} copy-done((bf16[8,2,512,512]{3,2,1,0:T(8,128)(2,1)S(1)}, bf16[8,2,512,512]{3,2,1,0:T(8,128)(2,1)}, u32[]{:S(2)}) %copy-start) | copy-done | bytes 8388632
  7.9 0.0 copy-start.3
  7.9 0.7 %copy-done.3 = s32[3,4]{1,0:T(4,128)S(1)} copy-done((s32[3,4]{1,0:T(4,128)S(1)}, s32[3,4]{1,0:T(4,128)}, u32[]{:S(2)}) %copy-start.3) | copy-done | bytes 72
  8.6 0.0 copy-start.1
  8.6 0.0 copy-start.2
  8.6 2.4 %prepare.1 = (bf16[4,2,512,512]{3,2,1,0:T(8,128)(2,1)S(1)}, bf16[4,2,512,512]{3,2,1,0:T(8,128)(2,1)S(1)}, bf16[4,2,512,512]{3,2,1,0:T(8,128)(2,1)S(1)}, bf16[4,5...) custom-call(s32[3,4]{1,0:T(4,128)S(1)} %copy-done.3, ...), custom_call_target="tpu_custom_call" | custom-call | bytes 4096 | tf_op jit(solution)/shard_map/prepare/pallas_call | solution.py:136
  11.0 0.0 collective-permute-done.2.odd.refs_2_
  11.0 0.6 %collective-permute-start.5 = (bf16[2,128,512]{2,1,0:T(8,128)(2,1)S(1)}, bf16[2,128,512]{2,1,0:T(8,128)(2,1)S(1)}, u32[]{:S(2)}, u32[]{:S(2)}) collective-permute-start(bf16[2,128,512]{2,1,0:T(8,128)(2,1)S(1)} %collective-permute-done.2.odd.refs_2_), channel_id=1, source_target_pairs={{0,1},{1,0},{2,3},{3,2},{4,5},{5,4},{6,7},{7,6},{8,9},{9,8},{10,11... | collective-permute-start | bytes 786440 | tf_op jit(solution)/shard_map/ppermute | solution.py:15
  11.6 1.2 %collective-permute-done.even.refs_0_ = bf16[2,128,512]{2,1,0:T(8,128)(2,1)S(1)} collective-permute-done((bf16[2,128,512]{2,1,0:T(8,128)(2,1)}, bf16[2,128,512]{2,1,0:T(8,128)(2,1)S(1)}, u32[]{:S(2)}, u32[]{:S(2)}) %collective-permute-start) | collective-permute-done | bytes 262176 | tf_op jit(solution)/shard_map/ppermute | solution.py:15
  12.8 0.6 %collective-permute-start.3 = (bf16[2,128,512]{2,1,0:T(8,128)(2,1)S(1)}, bf16[2,128,512]{2,1,0:T(8,128)(2,1)S(1)}, u32[]{:S(2)}, u32[]{:S(2)}) collective-permute-start(bf16[2,128,512]{2,1,0:T(8,128)(2,1)S(1)} %choose.1), channel_id=1, source_target_pairs={{0,2},{1,5},{2,0},{3,7},{4,6},{5,9},{6,4},{7,11},{8,10},{9,13},{10... | collective-permute-start | bytes 786440 | tf_op jit(solution)/shard_map/ppermute | solution.py:15
  13.4 0.0 collective-permute-start.1
  13.4 0.0 collective-permute-done.4.refs_1_
  13.4 0.0 collective-permute-done.5.refs_3_
  13.4 0.0 copy-done.1
  13.4 0.0 copy-done.2
  13.5 2.9 %later_stop.1 = (bf16[448,256]{1,0:T(8,128)(2,1)S(1)}, bf16[512,1024]{1,0:T(8,128)(2,1)S(1)}) custom-call(bf16[2,128,512]{2,1,0:T(8,128)(2,1)S(1)} %copy-done.1, bf16[2,128,512]{2,1,0:T(8,128)(2,1)S(1)} %collective-permute-done.4.refs_1_, bf16[2,128,512]{2,1,0:T(8,128)(2,1)S(1)} %collective-permute-done.2.odd.refs_2_, ...), custom_call_target="tpu_custom_call" | custom-call | bytes 4096 | tf_op jit(solution)/shard_map/later_stop/pallas_call | solution.py:136
  16.3 1.9 %collective-permute-start.8 = (bf16[448,256]{1,0:T(8,128)(2,1)S(1)}, bf16[448,256]{1,0:T(8,128)(2,1)S(1)}, u32[]{:S(2)}, u32[]{:S(2)}) collective-permute-start(bf16[448,256]{1,0:T(8,128)(2,1)S(1)} %get-tuple-element.30), channel_id=1, source_target_pairs={{0,12},{1,13},{2,14},{3,15},{4,0},{5,1},{6,2},{7,3},{8,4},{9,5},{1... | collective-permute-start | bytes 688136 | tf_op jit(solution)/shard_map/ppermute | solution.py:15
  18.2 1.3 %own_stop.1.before = f32[512,256]{1,0:T(8,128)S(1)} custom-call(bf16[512,1024]{1,0:T(8,128)(2,1)S(1)} %get-tuple-element.29.spectral, f32[3,4]{1,0:T(4,128)S(1)} %copy-done.2, bf16[4,512,256]{2,1,0:T(8,128)(2,1)S(1)} %get-tuple-element.22.turned, bf16[4,2,512,512]{3,2,1,0:T(8,128)(2,1)S(1)} %get-tuple-element.23.picked), custom_call_target="tpu_custom_call" | custom-call | bytes 4096 | tf_op jit(solution)/shard_map/own_stop/pallas_call | solution.py:136
  19.6 0.0 collective-permute-done.3.block.refs_2_
  19.6 0.1 collective-permute-start.6
  19.8 0.4 %collective-permute-start.7 = (bf16[128,512]{1,0:T(8,128)(2,1)S(1)}, bf16[128,512]{1,0:T(8,128)(2,1)S(1)}, u32[]{:S(2)}, u32[]{:S(2)}) collective-permute-start(bf16[128,512]{1,0:T(8,128)(2,1)S(1)} %get-tuple-element.26), channel_id=1, source_target_pairs={{0,1},{1,0},{2,3},{3,2},{4,5},{5,4},{6,7},{7,6},{8,9},{9,8},{10,11... | collective-permute-start | bytes 393224 | tf_op jit(solution)/shard_map/ppermute | solution.py:15
  20.2 1.3 %own_rest.1.refs_8_ = f32[512,256]{1,0:T(8,128)S(1)} custom-call(bf16[512,1024]{1,0:T(8,128)(2,1)S(1)} %get-tuple-element.29.spectral, f32[3,4]{1,0:T(4,128)S(1)} %copy-done.2, bf16[4,512,256]{2,1,0:T(8,128)(2,1)S(1)} %get-tuple-element.22.turned, bf16[4,2,512,512]{3,2,1,0:T(8,128)(2,1)S(1)} %get-tuple-element.23.picked, f32[512,256]{1,0:T(8,128)S(1)} %own_stop.1.before), custom_call_target="tpu_custom_call" | custom-call | bytes 4096 | tf_op jit(solution)/shard_map/own_rest/pallas_call | solution.py:136
  21.5 0.0 collective-permute-done.1.refs_1_
  21.6 0.0 collective-permute-done.6.refs_3_
  21.6 0.0 collective-permute-done.7.refs_4_
  21.6 2.8 %earlier_stop.1.total = f32[512,256]{1,0:T(8,128)S(1)} custom-call(bf16[2,128,512]{2,1,0:T(8,128)(2,1)S(1)} %collective-permute-done.even.refs_0_, bf16[2,128,512]{2,1,0:T(8,128)(2,1)S(1)} %collective-permute-done.1.refs_1_, bf16[2,128,512]{2,1,0:T(8,128)(2,1)S(1)} %collective-permute-done.3.block.refs_2_, ...), custom_call_target="tpu_custom_call" | custom-call | bytes 4096 | tf_op jit(solution)/shard_map/earlier_stop/pallas_call | solution.py:136
  24.4 0.0 collective-permute-done.8.arrived
  24.4 1.0 %finish.1 = f32[2,128,512]{2,1,0:T(8,128)} custom-call(f32[512,256]{1,0:T(8,128)S(1)} %earlier_stop.1.total, bf16[448,256]{1,0:T(8,128)(2,1)S(1)} %collective-permute-done.8.arrived), custom_call_target="tpu_custom_call" | custom-call | bytes 4096 | tf_op jit(solution)/shard_map/finish/pallas_call | solution.py:273
  (2 shorter events, 0.0 us)
Async XLA Ops:
  0.0 11.0 %collective-permute-start.2 = (bf16[2,128,512]{2,1,0:T(8,128)(2,1)}, bf16[2,128,512]{2,1,0:T(8,128)(2,1)S(1)}, u32[]{:S(2)}, u32[]{:S(2)}) collective-permute-start(bf16[2,128,512]{2,1,0:T(8,128)(2,1)} %refs_0_.1), channel_id=1, source_target_pairs={{0,2},{1,3},{2,0},{3,1},{4,6},{5,7},{6,4},{7,5},{8,10},{9,11},{10,... | collective-permute-start | bytes 786440 | tf_op jit(solution)/shard_map/ppermute | solution.py:15
  2.9 9.9 %collective-permute-start = (bf16[2,128,512]{2,1,0:T(8,128)(2,1)}, bf16[2,128,512]{2,1,0:T(8,128)(2,1)S(1)}, u32[]{:S(2)}, u32[]{:S(2)}) collective-permute-start(bf16[2,128,512]{2,1,0:T(8,128)(2,1)} %refs_0_.1), channel_id=1, source_target_pairs={{0,4},{1,5},{2,6},{3,7},{4,8},{5,9},{6,10},{7,11},{8,12},{9,13},{1... | collective-permute-start | bytes 786440 | tf_op jit(solution)/shard_map/ppermute | solution.py:15
  4.5 8.9 %collective-permute-start.4 = (bf16[2,128,512]{2,1,0:T(8,128)(2,1)}, bf16[2,128,512]{2,1,0:T(8,128)(2,1)S(1)}, u32[]{:S(2)}, u32[]{:S(2)}) collective-permute-start(bf16[2,128,512]{2,1,0:T(8,128)(2,1)} %refs_0_.1), channel_id=1, source_target_pairs={{0,1},{1,0},{2,3},{3,2},{4,5},{5,4},{6,7},{7,6},{8,9},{9,8},{10,11... | collective-permute-start | bytes 786440 | tf_op jit(solution)/shard_map/ppermute | solution.py:15
  4.5 3.4 %copy-start = (bf16[8,2,512,512]{3,2,1,0:T(8,128)(2,1)S(1)}, bf16[8,2,512,512]{3,2,1,0:T(8,128)(2,1)}, u32[]{:S(2)}) copy-start(bf16[8,2,512,512]{3,2,1,0:T(8,128)(2,1)} %couplings.1) | copy-start | bytes 25165828
  7.9 0.7 %copy-start.3 = (s32[3,4]{1,0:T(4,128)S(1)}, s32[3,4]{1,0:T(4,128)}, u32[]{:S(2)}) copy-start(s32[3,4]{1,0:T(4,128)} %listed.1) | copy-start | bytes 148
  8.6 4.8 %copy-start.1 = (bf16[2,128,512]{2,1,0:T(8,128)(2,1)S(1)}, bf16[2,128,512]{2,1,0:T(8,128)(2,1)}, u32[]{:S(2)}) copy-start(bf16[2,128,512]{2,1,0:T(8,128)(2,1)} %refs_0_.1) | copy-start | bytes 786436
  8.6 4.9 %copy-start.2 = (f32[3,4]{1,0:T(4,128)S(1)}, f32[3,4]{1,0:T(4,128)}, u32[]{:S(2)}) copy-start(f32[3,4]{1,0:T(4,128)} %refs_5_.1) | copy-start | bytes 148
  11.0 2.4 %collective-permute-start.5 = (bf16[2,128,512]{2,1,0:T(8,128)(2,1)S(1)}, bf16[2,128,512]{2,1,0:T(8,128)(2,1)S(1)}, u32[]{:S(2)}, u32[]{:S(2)}) collective-permute-start(bf16[2,128,512]{2,1,0:T(8,128)(2,1)S(1)} %collective-permute-done.2.odd.refs_2_), channel_id=1, source_target_pairs={{0,1},{1,0},{2,3},{3,2},{4,5},{5,4},{6,7},{7,6},{8,9},{9,8},{10,11... | collective-permute-start | bytes 786440 | tf_op jit(solution)/shard_map/ppermute | solution.py:15
  12.8 6.8 %collective-permute-start.3 = (bf16[2,128,512]{2,1,0:T(8,128)(2,1)S(1)}, bf16[2,128,512]{2,1,0:T(8,128)(2,1)S(1)}, u32[]{:S(2)}, u32[]{:S(2)}) collective-permute-start(bf16[2,128,512]{2,1,0:T(8,128)(2,1)S(1)} %choose.1), channel_id=1, source_target_pairs={{0,2},{1,5},{2,0},{3,7},{4,6},{5,9},{6,4},{7,11},{8,10},{9,13},{10... | collective-permute-start | bytes 786440 | tf_op jit(solution)/shard_map/ppermute | solution.py:15
  13.4 8.1 %collective-permute-start.1 = (bf16[2,128,512]{2,1,0:T(8,128)(2,1)S(1)}, bf16[2,128,512]{2,1,0:T(8,128)(2,1)S(1)}, u32[]{:S(2)}, u32[]{:S(2)}) collective-permute-start(bf16[2,128,512]{2,1,0:T(8,128)(2,1)S(1)} %collective-permute-done.even.refs_0_), channel_id=1, source_target_pairs={{0,1},{1,0},{2,3},{3,2},{4,5},{5,4},{6,7},{7,6},{8,9},{9,8},{10,11... | collective-permute-start | bytes 786440 | tf_op jit(solution)/shard_map/ppermute | solution.py:15
  16.3 8.1 %collective-permute-start.8 = (bf16[448,256]{1,0:T(8,128)(2,1)S(1)}, bf16[448,256]{1,0:T(8,128)(2,1)S(1)}, u32[]{:S(2)}, u32[]{:S(2)}) collective-permute-start(bf16[448,256]{1,0:T(8,128)(2,1)S(1)} %get-tuple-element.30), channel_id=1, source_target_pairs={{0,12},{1,13},{2,14},{3,15},{4,0},{5,1},{6,2},{7,3},{8,4},{9,5},{1... | collective-permute-start | bytes 688136 | tf_op jit(solution)/shard_map/ppermute | solution.py:15
  19.6 1.9 %collective-permute-start.6 = (bf16[128,512]{1,0:T(8,128)(2,1)S(1)}, bf16[128,512]{1,0:T(8,128)(2,1)S(1)}, u32[]{:S(2)}, u32[]{:S(2)}) collective-permute-start(bf16[128,512]{1,0:T(8,128)(2,1)S(1)} %get-tuple-element.25), channel_id=1, source_target_pairs={{0,1},{1,0},{2,3},{3,2},{4,5},{5,4},{6,7},{7,6},{8,9},{9,8},{10,11... | collective-permute-start | bytes 393224 | tf_op jit(solution)/shard_map/ppermute | solution.py:15
  19.8 1.8 %collective-permute-start.7 = (bf16[128,512]{1,0:T(8,128)(2,1)S(1)}, bf16[128,512]{1,0:T(8,128)(2,1)S(1)}, u32[]{:S(2)}, u32[]{:S(2)}) collective-permute-start(bf16[128,512]{1,0:T(8,128)(2,1)S(1)} %get-tuple-element.26), channel_id=1, source_target_pairs={{0,1},{1,0},{2,3},{3,2},{4,5},{5,4},{6,7},{7,6},{8,9},{9,8},{10,11... | collective-permute-start | bytes 393224 | tf_op jit(solution)/shard_map/ppermute | solution.py:15

commit v7 on v6

--- a/solution.py
+++ b/solution.py
@@ -73,30 +73,31 @@
 
 def packed(total, group, leaving, whole):
     tile = total.shape[1] // 2
-    whole[...] = total
+    whole[...] = total.astype(BF16)
     for offset in range(1, group):
         spot = slice((offset - 1) * tile, offset * tile)
-        leaving[spot] = whole[pl.ds(own_row(offset, group, tile), tile), :].astype(BF16)
+        leaving[spot] = whole[pl.ds(own_row(offset, group, tile), tile), :]
     own = whole[pl.ds(own_row(0, group, tile), tile), :]
     both = jnp.where(triangle(tile), own[:, :tile], own[:, tile:])
     half = tile // 2
-    leaving[(group - 1) * tile :] = beside(both[:half], both[half:]).astype(BF16)
-
-
-def add_packed(whole, arrived, group):
-    tile = whole.shape[1] // 2
+    leaving[(group - 1) * tile :] = beside(both[:half], both[half:])
+
+
+def packed_part(arrived, group, part):
+    tile = arrived.shape[1] // 2
+    columns = slice(part * tile, (part + 1) * tile)
     for offset in range(1, group):
-        spot = pl.ds(own_row(offset, group, tile), tile)
-        whole[spot, :] += arrived[(offset - 1) * tile : offset * tile].astype(F32)
+        turned = arrived[(offset - 1) * tile : offset * tile, columns].T.astype(F32)
+        yield offset, -turned if part else turned
     both = arrived[(group - 1) * tile :].astype(F32)
     both = jnp.concatenate([both[:, :tile], both[:, tile:]], axis=0)
     turned = both.T
-    upper = triangle(tile)
     row = lax.broadcasted_iota(jnp.int32, (tile, tile), 0)
     column = lax.broadcasted_iota(jnp.int32, (tile, tile), 1)
-    real = jnp.where(upper, both, turned)
-    imag = jnp.where(row > column, both, jnp.where(row < column, -turned, 0.0))
-    whole[pl.ds(own_row(0, group, tile), tile), :] += beside(real, imag)
+    if part:
+        yield 0, jnp.where(row > column, both, jnp.where(row < column, -turned, 0.0))
+    else:
+        yield 0, jnp.where(row <= column, both, turned)
 
 
 def stop_term(stop, weights, spectral, turned, picked, start, modes=None):
@@ -221,7 +222,7 @@
         later,
         [*own_blocks, weights, turned[0], picked[0]],
         [((slab - tile // 2, width), BF16), (spectral_shape, BF16)],
-        [pltpu.VMEM(term_shape, F32)],
+        [pltpu.VMEM(term_shape, BF16)],
     )
     arrived = passed_along(leaving, "mom", -group)
 
@@ -249,24 +250,26 @@
         parts = iter(parts)
         blocks = [(next(parts), next(parts)) if isinstance(b, tuple) else next(parts) for b in next_blocks]
         fill_spectral(blocks, spectral)
-        out[...] = stop_term(2, weights, spectral, turned, picked, before[...])
+        total = stop_term(2, weights, spectral, turned, picked, before[...])
+        out[0] = total[:, :tile].T
+        out[1] = -total[:, tile:].T
 
     (total,) = kernel(
         "earlier_stop",
         earlier,
         [*jax.tree.leaves(next_blocks), weights, turned[2], picked[2], total],
-        [(term_shape, F32)],
+        [((2, tile, slab), F32)],
         [pltpu.VMEM(spectral_shape, BF16)],
     )
 
-    def finish(total, arrived, out, whole, rows, sems):
-        whole[...] = total[...]
-        add_packed(whole, arrived, group)
-        copies = [pltpu.make_async_copy(rows.at[half], out.at[half], sems.at[half]) for half in range(2)]
-        rows[0] = whole[:, :tile].T
-        copies[0].start()
-        rows[1] = -whole[:, tile:].T
-        copies[1].start()
+    def finish(total, arrived, out, rows, sems):
+        copies = []
+        for part in range(2):
+            for offset, block in packed_part(arrived, group, part):
+                spot = pl.ds(own_row(offset, group, tile), tile)
+                rows[part, :, spot] = total[part, :, spot] + block
+            copies.append(pltpu.make_async_copy(rows.at[part], out.at[part], sems.at[part]))
+            copies[part].start()
         for copy in copies:
             copy.wait()
 
@@ -276,7 +279,6 @@
         out_specs=ANY,
         out_shape=jax.ShapeDtypeStruct((2, tile, slab), F32),
         scratch_shapes=[
-            pltpu.VMEM(term_shape, F32),
             pltpu.VMEM((2, tile, slab), F32),
             pltpu.SemaphoreType.DMA((2,)),
         ],

time: 25.6 us -> 25.6 us (level)
  no operation moved by 1% of the time
where the time goes in v7:
time: 25.6 us; the launch traced here: 25.5 us
  Pallas kernels  11.9 us (46%)
  starting transfers between devices  8.15 us (32%)
  local copies, waits for them, and re-layouts  4.07 us (16%)
  waiting for transfers between devices  1.23 us (5%)
    pallas_call x5, Pallas kernels, kernel(): pl.pallas_call(function, in_specs=[leading] + [VMEM] * (len(args) - 1), o...  10.9 us
    ppermute x9, starting transfers between devices, moved(): lax.ppermute(block, axis, [(i, route(i)) for i in range(lax.axis_size(axi...  8.15 us
    unnamed x8, local copies, waits for them, and re-layouts  4.07 us
    ppermute x9, waiting for transfers between devices, moved(): lax.ppermute(block, axis, [(i, route(i)) for i in range(lax.axis_size(axi...  1.23 us
    pallas_call x1, Pallas kernels, body(): pl.pallas_call(finish, in_specs=[VMEM] * 2, out_specs=ANY, out_shape=jax....  0.93 us
  transfers between devices with their start and end apart: 9, of which 1 were waited for; matrix products, arithmetic and copies ran while one was open for 0% of the time, Pallas kernels for 43%

profile of v7, /device:TPU:0, one launch (start us, length us, event | category | flops | bytes accessed | tf_op | source)
XLA Modules:
  0.0 25.5 jit_solution(1959404275556124484)
XLA Ops:
  0.0 2.9 %collective-permute-start.2 = (bf16[2,128,512]{2,1,0:T(8,128)(2,1)}, bf16[2,128,512]{2,1,0:T(8,128)(2,1)S(1)}, u32[]{:S(2)}, u32[]{:S(2)}) collective-permute-start(bf16[2,128,512]{2,1,0:T(8,128)(2,1)} %refs_0_.1), channel_id=1, source_target_pairs={{0,2},{1,3},{2,0},{3,1},{4,6},{5,7},{6,4},{7,5},{8,10},{9,11},{10,... | collective-permute-start | bytes 786440 | tf_op jit(solution)/shard_map/ppermute | solution.py:15
  2.9 1.6 %collective-permute-start = (bf16[2,128,512]{2,1,0:T(8,128)(2,1)}, bf16[2,128,512]{2,1,0:T(8,128)(2,1)S(1)}, u32[]{:S(2)}, u32[]{:S(2)}) collective-permute-start(bf16[2,128,512]{2,1,0:T(8,128)(2,1)} %refs_0_.1), channel_id=1, source_target_pairs={{0,4},{1,5},{2,6},{3,7},{4,8},{5,9},{6,10},{7,11},{8,12},{9,13},{1... | collective-permute-start | bytes 786440 | tf_op jit(solution)/shard_map/ppermute | solution.py:15
  4.5 0.0 collective-permute-start.4
  4.5 0.0 copy-start
  4.5 3.4 %copy-done = bf16[8,2,512,512]{3,2,1,0:T(8,128)(2,1)S(1)} copy-done((bf16[8,2,512,512]{3,2,1,0:T(8,128)(2,1)S(1)}, bf16[8,2,512,512]{3,2,1,0:T(8,128)(2,1)}, u32[]{:S(2)}) %copy-start) | copy-done | bytes 8388632
  7.9 0.0 copy-start.3
  7.9 0.7 %copy-done.3 = s32[3,4]{1,0:T(4,128)S(1)} copy-done((s32[3,4]{1,0:T(4,128)S(1)}, s32[3,4]{1,0:T(4,128)}, u32[]{:S(2)}) %copy-start.3) | copy-done | bytes 72
  8.6 0.0 copy-start.1
  8.6 0.0 copy-start.2
  8.6 2.4 %prepare.1 = (bf16[4,2,512,512]{3,2,1,0:T(8,128)(2,1)S(1)}, bf16[4,2,512,512]{3,2,1,0:T(8,128)(2,1)S(1)}, bf16[4,2,512,512]{3,2,1,0:T(8,128)(2,1)S(1)}, bf16[4,5...) custom-call(s32[3,4]{1,0:T(4,128)S(1)} %copy-done.3, ...), custom_call_target="tpu_custom_call" | custom-call | bytes 4096 | tf_op jit(solution)/shard_map/prepare/pallas_call | solution.py:137
  11.0 0.0 collective-permute-done.2.odd.refs_2_
  11.0 0.6 %collective-permute-start.5 = (bf16[2,128,512]{2,1,0:T(8,128)(2,1)S(1)}, bf16[2,128,512]{2,1,0:T(8,128)(2,1)S(1)}, u32[]{:S(2)}, u32[]{:S(2)}) collective-permute-start(bf16[2,128,512]{2,1,0:T(8,128)(2,1)S(1)} %collective-permute-done.2.odd.refs_2_), channel_id=1, source_target_pairs={{0,1},{1,0},{2,3},{3,2},{4,5},{5,4},{6,7},{7,6},{8,9},{9,8},{10,11... | collective-permute-start | bytes 786440 | tf_op jit(solution)/shard_map/ppermute | solution.py:15
  11.6 1.2 %collective-permute-done.even.refs_0_ = bf16[2,128,512]{2,1,0:T(8,128)(2,1)S(1)} collective-permute-done((bf16[2,128,512]{2,1,0:T(8,128)(2,1)}, bf16[2,128,512]{2,1,0:T(8,128)(2,1)S(1)}, u32[]{:S(2)}, u32[]{:S(2)}) %collective-permute-start) | collective-permute-done | bytes 262176 | tf_op jit(solution)/shard_map/ppermute | solution.py:15
  12.8 0.6 %collective-permute-start.3 = (bf16[2,128,512]{2,1,0:T(8,128)(2,1)S(1)}, bf16[2,128,512]{2,1,0:T(8,128)(2,1)S(1)}, u32[]{:S(2)}, u32[]{:S(2)}) collective-permute-start(bf16[2,128,512]{2,1,0:T(8,128)(2,1)S(1)} %choose.1), channel_id=1, source_target_pairs={{0,2},{1,5},{2,0},{3,7},{4,6},{5,9},{6,4},{7,11},{8,10},{9,13},{10... | collective-permute-start | bytes 786440 | tf_op jit(solution)/shard_map/ppermute | solution.py:15
  13.4 0.0 collective-permute-start.1
  13.4 0.0 collective-permute-done.4.refs_1_
  13.4 0.0 collective-permute-done.5.refs_3_
  13.4 0.0 copy-done.1
  13.4 0.0 copy-done.2
  13.5 2.9 %later_stop.1 = (bf16[448,256]{1,0:T(8,128)(2,1)S(1)}, bf16[512,1024]{1,0:T(8,128)(2,1)S(1)}) custom-call(bf16[2,128,512]{2,1,0:T(8,128)(2,1)S(1)} %copy-done.1, bf16[2,128,512]{2,1,0:T(8,128)(2,1)S(1)} %collective-permute-done.4.refs_1_, bf16[2,128,512]{2,1,0:T(8,128)(2,1)S(1)} %collective-permute-done.2.odd.refs_2_, ...), custom_call_target="tpu_custom_call" | custom-call | bytes 4096 | tf_op jit(solution)/shard_map/later_stop/pallas_call | solution.py:137
  16.3 1.9 %collective-permute-start.8 = (bf16[448,256]{1,0:T(8,128)(2,1)S(1)}, bf16[448,256]{1,0:T(8,128)(2,1)S(1)}, u32[]{:S(2)}, u32[]{:S(2)}) collective-permute-start(bf16[448,256]{1,0:T(8,128)(2,1)S(1)} %get-tuple-element.30), channel_id=1, source_target_pairs={{0,12},{1,13},{2,14},{3,15},{4,0},{5,1},{6,2},{7,3},{8,4},{9,5},{1... | collective-permute-start | bytes 688136 | tf_op jit(solution)/shard_map/ppermute | solution.py:15
  18.2 1.3 %own_stop.1.before = f32[512,256]{1,0:T(8,128)S(1)} custom-call(bf16[512,1024]{1,0:T(8,128)(2,1)S(1)} %get-tuple-element.29.spectral, f32[3,4]{1,0:T(4,128)S(1)} %copy-done.2, bf16[4,512,256]{2,1,0:T(8,128)(2,1)S(1)} %get-tuple-element.22.turned, bf16[4,2,512,512]{3,2,1,0:T(8,128)(2,1)S(1)} %get-tuple-element.23.picked), custom_call_target="tpu_custom_call" | custom-call | bytes 4096 | tf_op jit(solution)/shard_map/own_stop/pallas_call | solution.py:137
  19.6 0.0 collective-permute-done.3.block.refs_2_
  19.6 0.1 collective-permute-start.6
  19.8 0.4 %collective-permute-start.7 = (bf16[128,512]{1,0:T(8,128)(2,1)S(1)}, bf16[128,512]{1,0:T(8,128)(2,1)S(1)}, u32[]{:S(2)}, u32[]{:S(2)}) collective-permute-start(bf16[128,512]{1,0:T(8,128)(2,1)S(1)} %get-tuple-element.26), channel_id=1, source_target_pairs={{0,1},{1,0},{2,3},{3,2},{4,5},{5,4},{6,7},{7,6},{8,9},{9,8},{10,11... | collective-permute-start | bytes 393224 | tf_op jit(solution)/shard_map/ppermute | solution.py:15
  20.2 1.3 %own_rest.1.refs_8_ = f32[512,256]{1,0:T(8,128)S(1)} custom-call(bf16[512,1024]{1,0:T(8,128)(2,1)S(1)} %get-tuple-element.29.spectral, f32[3,4]{1,0:T(4,128)S(1)} %copy-done.2, bf16[4,512,256]{2,1,0:T(8,128)(2,1)S(1)} %get-tuple-element.22.turned, bf16[4,2,512,512]{3,2,1,0:T(8,128)(2,1)S(1)} %get-tuple-element.23.picked, f32[512,256]{1,0:T(8,128)S(1)} %own_stop.1.before), custom_call_target="tpu_custom_call" | custom-call | bytes 4096 | tf_op jit(solution)/shard_map/own_rest/pallas_call | solution.py:137
  21.5 0.0 collective-permute-done.1.refs_1_
  21.6 0.0 collective-permute-done.6.refs_3_
  21.6 0.0 collective-permute-done.7.refs_4_
  21.6 2.9 %earlier_stop.1.total = f32[2,128,512]{2,1,0:T(8,128)S(1)} custom-call(bf16[2,128,512]{2,1,0:T(8,128)(2,1)S(1)} %collective-permute-done.even.refs_0_, bf16[2,128,512]{2,1,0:T(8,128)(2,1)S(1)} %collective-permute-done.1.refs_1_, bf16[2,128,512]{2,1,0:T(8,128)(2,1)S(1)} %collective-permute-done.3.block.refs_2_, ...), custom_call_target="tpu_custom_call" | custom-call | bytes 4096 | tf_op jit(solution)/shard_map/earlier_stop/pallas_call | solution.py:137
  24.5 0.0 collective-permute-done.8.arrived
  24.5 0.9 %finish.1 = f32[2,128,512]{2,1,0:T(8,128)} custom-call(f32[2,128,512]{2,1,0:T(8,128)S(1)} %earlier_stop.1.total, bf16[448,256]{1,0:T(8,128)(2,1)S(1)} %collective-permute-done.8.arrived), custom_call_target="tpu_custom_call" | custom-call | bytes 4096 | tf_op jit(solution)/shard_map/finish/pallas_call | solution.py:276
  (2 shorter events, 0.0 us)
Async XLA Ops:
  0.0 11.0 %collective-permute-start.2 = (bf16[2,128,512]{2,1,0:T(8,128)(2,1)}, bf16[2,128,512]{2,1,0:T(8,128)(2,1)S(1)}, u32[]{:S(2)}, u32[]{:S(2)}) collective-permute-start(bf16[2,128,512]{2,1,0:T(8,128)(2,1)} %refs_0_.1), channel_id=1, source_target_pairs={{0,2},{1,3},{2,0},{3,1},{4,6},{5,7},{6,4},{7,5},{8,10},{9,11},{10,... | collective-permute-start | bytes 786440 | tf_op jit(solution)/shard_map/ppermute | solution.py:15
  2.9 9.9 %collective-permute-start = (bf16[2,128,512]{2,1,0:T(8,128)(2,1)}, bf16[2,128,512]{2,1,0:T(8,128)(2,1)S(1)}, u32[]{:S(2)}, u32[]{:S(2)}) collective-permute-start(bf16[2,128,512]{2,1,0:T(8,128)(2,1)} %refs_0_.1), channel_id=1, source_target_pairs={{0,4},{1,5},{2,6},{3,7},{4,8},{5,9},{6,10},{7,11},{8,12},{9,13},{1... | collective-permute-start | bytes 786440 | tf_op jit(solution)/shard_map/ppermute | solution.py:15
  4.5 8.9 %collective-permute-start.4 = (bf16[2,128,512]{2,1,0:T(8,128)(2,1)}, bf16[2,128,512]{2,1,0:T(8,128)(2,1)S(1)}, u32[]{:S(2)}, u32[]{:S(2)}) collective-permute-start(bf16[2,128,512]{2,1,0:T(8,128)(2,1)} %refs_0_.1), channel_id=1, source_target_pairs={{0,1},{1,0},{2,3},{3,2},{4,5},{5,4},{6,7},{7,6},{8,9},{9,8},{10,11... | collective-permute-start | bytes 786440 | tf_op jit(solution)/shard_map/ppermute | solution.py:15
  4.5 3.4 %copy-start = (bf16[8,2,512,512]{3,2,1,0:T(8,128)(2,1)S(1)}, bf16[8,2,512,512]{3,2,1,0:T(8,128)(2,1)}, u32[]{:S(2)}) copy-start(bf16[8,2,512,512]{3,2,1,0:T(8,128)(2,1)} %couplings.1) | copy-start | bytes 25165828
  7.9 0.7 %copy-start.3 = (s32[3,4]{1,0:T(4,128)S(1)}, s32[3,4]{1,0:T(4,128)}, u32[]{:S(2)}) copy-start(s32[3,4]{1,0:T(4,128)} %listed.1) | copy-start | bytes 148
  8.6 4.8 %copy-start.1 = (bf16[2,128,512]{2,1,0:T(8,128)(2,1)S(1)}, bf16[2,128,512]{2,1,0:T(8,128)(2,1)}, u32[]{:S(2)}) copy-start(bf16[2,128,512]{2,1,0:T(8,128)(2,1)} %refs_0_.1) | copy-start | bytes 786436
  8.6 4.9 %copy-start.2 = (f32[3,4]{1,0:T(4,128)S(1)}, f32[3,4]{1,0:T(4,128)}, u32[]{:S(2)}) copy-start(f32[3,4]{1,0:T(4,128)} %refs_5_.1) | copy-start | bytes 148
  11.0 2.4 %collective-permute-start.5 = (bf16[2,128,512]{2,1,0:T(8,128)(2,1)S(1)}, bf16[2,128,512]{2,1,0:T(8,128)(2,1)S(1)}, u32[]{:S(2)}, u32[]{:S(2)}) collective-permute-start(bf16[2,128,512]{2,1,0:T(8,128)(2,1)S(1)} %collective-permute-done.2.odd.refs_2_), channel_id=1, source_target_pairs={{0,1},{1,0},{2,3},{3,2},{4,5},{5,4},{6,7},{7,6},{8,9},{9,8},{10,11... | collective-permute-start | bytes 786440 | tf_op jit(solution)/shard_map/ppermute | solution.py:15
  12.8 6.7 %collective-permute-start.3 = (bf16[2,128,512]{2,1,0:T(8,128)(2,1)S(1)}, bf16[2,128,512]{2,1,0:T(8,128)(2,1)S(1)}, u32[]{:S(2)}, u32[]{:S(2)}) collective-permute-start(bf16[2,128,512]{2,1,0:T(8,128)(2,1)S(1)} %choose.1), channel_id=1, source_target_pairs={{0,2},{1,5},{2,0},{3,7},{4,6},{5,9},{6,4},{7,11},{8,10},{9,13},{10... | collective-permute-start | bytes 786440 | tf_op jit(solution)/shard_map/ppermute | solution.py:15
  13.4 8.1 %collective-permute-start.1 = (bf16[2,128,512]{2,1,0:T(8,128)(2,1)S(1)}, bf16[2,128,512]{2,1,0:T(8,128)(2,1)S(1)}, u32[]{:S(2)}, u32[]{:S(2)}) collective-permute-start(bf16[2,128,512]{2,1,0:T(8,128)(2,1)S(1)} %collective-permute-done.even.refs_0_), channel_id=1, source_target_pairs={{0,1},{1,0},{2,3},{3,2},{4,5},{5,4},{6,7},{7,6},{8,9},{9,8},{10,11... | collective-permute-start | bytes 786440 | tf_op jit(solution)/shard_map/ppermute | solution.py:15
  16.3 8.2 %collective-permute-start.8 = (bf16[448,256]{1,0:T(8,128)(2,1)S(1)}, bf16[448,256]{1,0:T(8,128)(2,1)S(1)}, u32[]{:S(2)}, u32[]{:S(2)}) collective-permute-start(bf16[448,256]{1,0:T(8,128)(2,1)S(1)} %get-tuple-element.30), channel_id=1, source_target_pairs={{0,12},{1,13},{2,14},{3,15},{4,0},{5,1},{6,2},{7,3},{8,4},{9,5},{1... | collective-permute-start | bytes 688136 | tf_op jit(solution)/shard_map/ppermute | solution.py:15
  19.6 1.9 %collective-permute-start.6 = (bf16[128,512]{1,0:T(8,128)(2,1)S(1)}, bf16[128,512]{1,0:T(8,128)(2,1)S(1)}, u32[]{:S(2)}, u32[]{:S(2)}) collective-permute-start(bf16[128,512]{1,0:T(8,128)(2,1)S(1)} %get-tuple-element.25), channel_id=1, source_target_pairs={{0,1},{1,0},{2,3},{3,2},{4,5},{5,4},{6,7},{7,6},{8,9},{9,8},{10,11... | collective-permute-start | bytes 393224 | tf_op jit(solution)/shard_map/ppermute | solution.py:15
  19.8 1.8 %collective-permute-start.7 = (bf16[128,512]{1,0:T(8,128)(2,1)S(1)}, bf16[128,512]{1,0:T(8,128)(2,1)S(1)}, u32[]{:S(2)}, u32[]{:S(2)}) collective-permute-start(bf16[128,512]{1,0:T(8,128)(2,1)S(1)} %get-tuple-element.26), channel_id=1, source_target_pairs={{0,1},{1,0},{2,3},{3,2},{4,5},{5,4},{6,7},{7,6},{8,9},{9,8},{10,11... | collective-permute-start | bytes 393224 | tf_op jit(solution)/shard_map/ppermute | solution.py:15
